TPU v7x, 32 devices: a whole 2x2x4 slice. The times are simulated.
32 devices in a mesh: job: 2 (over y), pole: 4 (over z), col: 4 (over x, core).
Axes of the slice: x: 2, y: 2, z: 4, core: 2. Of those that a mesh axis runs over, the one named last changes fastest.
Arguments:
- inverse: bfloat16 [8, 2, 6144, 6144], P(('job', 'pole'), None, 'col'), parts along dimension 0, may hold values from -6 to 6
- panels: bfloat16 [8, 3, 2, 6144, 128], P(('job', 'pole'), None, None, 'col'), parts along dimension 0, may hold values from -0.078125 to 0.078125
- diag_inverse: float32 [8, 3, 2, 128, 128], P(('job', 'pole')), parts along dimension 0, may hold values from -6 to 6
- pole_weights: float32 [8, 2], P(('job', 'pole')), parts along dimension 0, may hold values from -1 to 1
- supports: int32 [32, 8], replicated, may hold values from 0 to 143, as said below
- counts: int32 [32], replicated, may hold values from 1 to 8, as said below
- panel_order: int32 [3], replicated, may hold values from 0 to 2, each once
- row_orbitals: bfloat16 [64, 8, 128, 512], P(('job', 'col'), None, None, 'pole'), parts along dimension 0, may hold values from -0.5 to 0.5
- panel_orbitals: bfloat16 [64, 3, 128, 512], P(('job', 'col'), None, None, 'pole'), parts along dimension 0, may hold values from -0.078125 to 0.078125
- core_density: float32 [64, 512], P(('job', 'col'), 'pole'), parts along dimension 0, may hold values from 0.5 to 4
Outputs:
- valence_density: float32 [64, 512], P(('job', 'col'), 'pole'), parts along dimension 0
- exchange_potential: float32 [64, 512], P(('job', 'col'), 'pole'), parts along dimension 0
- diag_density: float32 [6, 128, 128], P('job'), parts along dimension 0
There are 2 independent parts, one for each index of `job`. A program takes and returns all parts, laid end to end along the dimension named above; an argument that names none is the same for every part. Nothing has to cross between parts.
Inputs may be any that keep to these rules, and one draw needn't show every extreme that they name: `supports`: the ids within one tile's list are distinct. Block g belongs to index g // 36 of col. Over the first counts[t] entries of all tiles of one index of col, at most 3 distinct blocks belong to any one index of col, and exactly 3 for some pair in every draw. `counts`: some tile of every index of col has a full list.
All inputs are finite; a program needn't handle non-finite values.
Results may differ from a plain program's by a relative error of at most 0.0029.
Values may be sent and summed in bfloat16 or wider, within the bound.
No kernel may reach another device: no remote copies, remote signals or barrier semaphores. Data moves between devices by JAX's collectives and lax.ppermute only.
A program may use at most 128 MiB of HBM per device.

v0:
```python
import jax
import jax.numpy as jnp
from jax import lax
from jax.sharding import PartitionSpec as P

W = 128
PANELS = 3
S_MAX = 8
CAP = 3


exchange_coeff = (3.0 / 3.141592653589793) ** (1.0 / 3.0)
density_floor = 0.5


def body(
    inverse,
    panels,
    diag_inverse,
    pole_weights,
    supports,
    counts,
    panel_order,
    row_orbitals,
    panel_orbitals,
    core_density,
):
    rows_local = inverse.shape[2]
    order_size = inverse.shape[3]
    stacked = inverse[0].reshape(2 * rows_local, order_size)
    ordered = jnp.take(panels[0], panel_order, axis=0)
    send_rows = ordered.transpose(2, 0, 1, 3).reshape(rows_local, PANELS * 2 * W)
    product = jnp.dot(
        stacked,
        lax.all_gather(send_rows, "col", axis=0, tiled=True),
        preferred_element_type=jnp.float32,
    )
    product = product.reshape(2, rows_local, PANELS, 2, W)
    real_part = -(product[0, :, :, 0] - product[1, :, :, 1])
    imag_part = -(product[0, :, :, 1] + product[1, :, :, 0])
    weight_real = pole_weights[0, 0]
    weight_imag = pole_weights[0, 1]
    partial_density = weight_real * imag_part + weight_imag * real_part
    lower_rows = ordered.astype(jnp.float32)
    highest = lax.Precision.HIGHEST
    cross_real = jnp.einsum(
        "jiw,ijv->jwv", lower_rows[:, 0], real_part, precision=highest
    ) - jnp.einsum("jiw,ijv->jwv", lower_rows[:, 1], imag_part, precision=highest)
    cross_imag = jnp.einsum(
        "jiw,ijv->jwv", lower_rows[:, 0], imag_part, precision=highest
    ) + jnp.einsum("jiw,ijv->jwv", lower_rows[:, 1], real_part, precision=highest)
    col_index = lax.axis_index("col")
    leading = (col_index == 0).astype(jnp.float32)
    diag_ordered = jnp.take(diag_inverse[0], panel_order, axis=0)
    diag_term = leading * (weight_real * diag_ordered[:, 1] + weight_imag * diag_ordered[:, 0]) - (
        weight_real * cross_imag + weight_imag * cross_real
    )
    density_sum = lax.psum(partial_density, "pole")
    diag_density = lax.psum(diag_term, ("pole", "col"))
    density_blocks = density_sum.astype(jnp.bfloat16)
    blocks = (
        density_blocks.reshape(rows_local // W, W, PANELS, W)
        .transpose(0, 2, 1, 3)
        .reshape(-1, W, W)
    )
    per_device = blocks.shape[0]
    col_count = lax.axis_size("col")
    tile_count = row_orbitals.shape[0]
    my_supports = lax.dynamic_slice_in_dim(supports, col_index * tile_count, tile_count, 0)
    my_counts = lax.dynamic_slice_in_dim(counts, col_index * tile_count, tile_count, 0)
    live_slots = jnp.arange(S_MAX, dtype=jnp.int32)[None, :] < my_counts[:, None]
    every_live = jnp.arange(S_MAX, dtype=jnp.int32)[None, :] < counts[:, None]
    owners = supports // per_device
    local_index = supports % per_device
    mine_live = every_live & (owners == col_index)
    hit_table = (
        mine_live[:, :, None]
        & (local_index[:, :, None] == jnp.arange(per_device, dtype=jnp.int32)[None, None, :])
    ).astype(jnp.int32)
    needed = jnp.max(hit_table.reshape(col_count, tile_count * S_MAX, per_device), axis=1)
    position = jnp.cumsum(needed, axis=1) - 1
    chosen = (
        (needed[:, None, :] == 1)
        & (position[:, None, :] == jnp.arange(CAP, dtype=jnp.int32)[None, :, None])
    ).astype(jnp.bfloat16)
    outgoing = jnp.einsum(
        "dcb,bwv->dcwv", chosen, blocks, preferred_element_type=jnp.float32
    ).astype(jnp.bfloat16)
    incoming = lax.all_to_all(outgoing, "col", split_axis=0, concat_axis=0, tiled=True)
    wanted_table = (
        live_slots[:, :, None]
        & (
            my_supports[:, :, None]
            == jnp.arange(col_count * per_device, dtype=jnp.int32)[None, None, :]
        )
    ).astype(jnp.int32)
    wanted = jnp.max(wanted_table.reshape(-1, col_count * per_device), axis=0).reshape(
        col_count, per_device
    )
    slot_table = (
        jnp.cumsum(wanted, axis=1) - 1 + jnp.arange(col_count, dtype=jnp.int32)[:, None] * CAP
    ).reshape(-1)
    slot_index = jnp.where(live_slots, slot_table[my_supports], 0)
    picked = incoming.reshape(col_count * CAP, W, W)[slot_index]
    panel_pick = (
        (my_supports % PANELS)[:, :, None] == jnp.arange(PANELS, dtype=jnp.int32)[None, None, :]
    ).astype(jnp.bfloat16)
    panel_values = jnp.einsum(
        "tkj,tjmr->tkmr", panel_pick, panel_orbitals, preferred_element_type=jnp.float32
    ).astype(jnp.bfloat16)
    mixed = jnp.einsum("tkim,tkmr->tkir", picked, panel_values, preferred_element_type=jnp.float32)
    contribution = jnp.sum(row_orbitals.astype(jnp.float32) * mixed, axis=2)
    valence = jnp.sum(contribution * live_slots[:, :, None].astype(jnp.float32), axis=1)
    clamped = jnp.maximum(core_density + valence, density_floor)
    potential = -exchange_coeff * clamped ** (1.0 / 3.0)
    return (valence, potential, diag_density)


def solution(mesh):
    placed = (
        P(("job", "pole"), None, "col", None),
        P(("job", "pole"), None, None, "col", None),
        P(("job", "pole"), None, None, None, None),
        P(("job", "pole"), None),
        P(),
        P(),
        P(),
        P(("job", "col"), None, None, "pole"),
        P(("job", "col"), None, None, "pole"),
        P(("job", "col"), "pole"),
    )
    return jax.shard_map(
        body,
        mesh=mesh,
        in_specs=placed,
        out_specs=(P(("job", "col"), "pole"), P(("job", "col"), "pole"), P("job", None, None)),
        check_vma=False,
    )
```

profile of v0, /device:TPU:0, one launch (start us, length us, event | category | flops | bytes accessed | tf_op | source)
XLA Modules:
  0.0 387.0 jit_solution(12929315986518939983)
XLA Ops:
  8.9 2.3 gather_fusion
  11.2 2.8 copy.92
  22.6 1.8 gather_fusion.3
  29.2 2.1 convolution_convert_fusion
  31.3 2.3 broadcast_select_fusion
  33.6 50.6 %all-gather.2.cloned.1.call-done = bf16[6144,768]{0,1:T(8,128)(2,1)} async-done(((bf16[1536,768]{0,1:T(8,128)(2,1)}), bf16[6144,768]{0,1:T(8,128)(2,1)}) %all-gather.2.cloned.1.call-update) | async-done | bytes 9437200 | tf_op jit(solution)/shard_map/all_gather | solution.py:35
  84.2 37.8 %convolution_bitcast_fusion = f32[3072,768]{0,1:T(8,128)} fusion(bf16[6144,768]{0,1:T(8,128)(2,1)} %all-gather.2.cloned.1.call-done, bf16[3072,6144]{1,0:T(8,128)(2,1)} %bitcast.85), kind=kOutput, calls=%fused_computation.4 | convolution fusion | flops 28991029248 | bytes 56623104 | tf_op jit(solution)/shard_map/dot_general | solution.py:33
  122.0 13.2 %reshape.159 = f32[2,1536,3,2,128]{1,0,4,3,2:T(2,128)} reshape(f32[3072,768]{0,1:T(8,128)} %convolution_bitcast_fusion) | data formatting | bytes 18874368 | tf_op jit(solution)/shard_map/reshape | solution.py:38
  135.3 14.4 %fusion.52 = (f32[1,1536,3,1,128]{1,0,4,3,2:T(1,128)}, f32[1,1536,3,1,128]{1,0,4,3,2:T(1,128)}, f32[1,1536,3,1,128]{1,0,4,3,2:T(1,128)}, f32[1,1536,3,1,128]{1,0,4,3,2:T(1,128)}) fusion(f32[2,1536,3,2,128]{1,0,4,3,2:T(2,128)} %reshape.159), kind=kLoop, calls=%fused_computation.81 | loop fusion | bytes 18874368 | tf_op jit(solution)/shard_map/slice | solution.py:39
  149.7 5.4 %copy.111 = f32[1,1536,3,1,128]{4,1,2,3,0:T(8,128)S(1)} copy(f32[1,1536,3,1,128]{1,0,4,3,2:T(1,128)} %get-tuple-element.6) | data formatting | bytes 4718592
  155.1 6.8 %copy.112 = f32[1,1536,3,1,128]{4,1,2,3,0:T(8,128)} copy(f32[1,1536,3,1,128]{1,0,4,3,2:T(1,128)} %get-tuple-element.5) | data formatting | bytes 4718592
  162.0 4.3 %fusion = f32[3,128,128]{2,1,0:T(8,128)} fusion(bf16[3,2,1536,128]{2,3,0,1:T(8,128)(2,1)} %broadcast_select_fusion, f32[1,1536,3,1,128]{4,1,2,3,0:T(8,128)S(1)} %copy.111, f32[1,1536,3,1,128]{4,1,2,3,0:T(8,128)} %copy.112), kind=kOutput, calls=%fused_computation.6 | convolution fusion | flops 907149312 | bytes 6094848 | tf_op jit(solution)/shard_map/jiw,ijv->jwv/dot_general | solution.py:46
  166.3 2.2 fusion.2
  168.6 5.4 %copy.109 = f32[1,1536,3,1,128]{4,1,2,3,0:T(8,128)S(1)} copy(f32[1,1536,3,1,128]{1,0,4,3,2:T(1,128)} %get-tuple-element.8) | data formatting | bytes 4718592
  174.0 6.6 %copy.110 = f32[1,1536,3,1,128]{4,1,2,3,0:T(8,128)} copy(f32[1,1536,3,1,128]{1,0,4,3,2:T(1,128)} %get-tuple-element.7) | data formatting | bytes 4718592
  180.7 6.3 %fusion.4 = f32[1536,3,128]{2,0,1:T(8,128)} fusion(f32[]{:T(128)} %bitcast.9, f32[]{:T(128)} %bitcast.2, f32[1,1536,3,1,128]{4,1,2,3,0:T(8,128)S(1)} %copy.109, f32[1,1536,3,1,128]{4,1,2,3,0:T(8,128)} %copy.110, f32[1,1536,3,1,128]{4,1,2,3,0:T(8,128)} %copy-done.3, f32[1,1536,3,1,128]{4,1,2,3,0:T(8,128)} %copy.112), kind=kLoop, calls=%fused_computation.11 | loop fusion | flops 4128768 | bytes 11796488 | tf_op jit(solution)/shard_map/add | solution.py:43
  187.0 87.9 %all-reduce.4 = bf16[1536,3,128]{2,0,1:T(8,128)(2,1)S(1)} all-reduce(f32[1536,3,128]{2,0,1:T(8,128)} %fusion.4), channel_id=1, replica_groups=mesh['job'=2,'pole'=4,'col'=4] {'pole'}, use_global_device_ids=true, to_apply=%region_2.3 | all-reduce | flops 589824 | bytes 3538944 | tf_op jit(solution)/shard_map/psum | solution.py:58
  276.8 3.5 all-to-all-start
  280.6 4.7 %fusion.31 = f32[3,128,128]{2,1,0:T(8,128)S(1)} fusion(f32[3,128,128]{2,1,0:T(8,128)S(1)} %copy-done.12, bf16[3,2,1536,128]{2,3,0,1:T(8,128)(2,1)} %broadcast_select_fusion, f32[]{:T(128)} %bitcast.9, f32[1,1536,3,1,128]{4,1,2,3,0:T(8,128)S(1)} %copy.109, f32[1,1536,3,1,128]{4,1,2,3,0:T(8,128)} %copy.110), kind=kOutput, calls=%fused_computation.33 | convolution fusion | flops 907247616 | bytes 6291968 | tf_op jit(solution)/shard_map/jiw,ijv->jwv/dot_general | solution.py:48
  285.3 3.6 fusion.25
  288.9 2.2 gather_fusion.2
  291.1 3.8 multiply_reduce_fusion
  295.7 82.9 %all-reduce.3.cloned.1.call-done = f32[3,128,128]{2,1,0:T(8,128)} async-done(((f32[3,128,128]{2,1,0:T(8,128)}), f32[3,128,128]{2,1,0:T(8,128)}) %all-reduce.3.cloned.1.call-update) | async-done | bytes 196624 | tf_op jit(solution)/shard_map/psum | solution.py:59
  378.5 1.6 copy.127
  (90 shorter events, 17.8 us)
Async XLA Ops:
  7.2 1.7 copy-start
  7.2 77.0 %all-gather.2.cloned.1.call-start = ((), (), s32[]{:S(2)}) async-start(), calls=%async_computation.1 | async-start | bytes 11796480 | tf_op jit(solution)/shard_map/all_gather | solution.py:35
  8.7 5.3 %copy-start.16 = (pred[3]{0:T(512)(128)(4,1)}, pred[3]{0:T(512)(128)(4,1)S(1)}, u32[]{:S(2)}) copy-start(pred[3]{0:T(512)(128)(4,1)S(1)} %compare_and_fusion) | copy-start | bytes 13
  8.9 2.3 copy-start.15
  14.1 1.5 copy-start.5
  17.1 0.7 copy-start.13
  17.1 0.9 copy-start.19
  20.9 8.3 %copy-start.9 = (bf16[8,3,128,128]{3,2,1,0:T(8,128)(2,1)S(1)}, bf16[8,3,128,128]{3,2,1,0:T(8,128)(2,1)}, u32[]{:S(2)}) copy-start(bf16[8,3,128,128]{3,2,1,0:T(8,128)(2,1)} %param.18) | copy-start | bytes 2359300
  22.6 8.7 %copy-start.6 = (bf16[3,2,1536,128]{2,3,0,1:T(8,128)(2,1)S(1)}, bf16[3,2,1536,128]{2,3,0,1:T(8,128)(2,1)}, u32[]{:S(2)}) copy-start(bf16[3,2,1536,128]{2,3,0,1:T(8,128)(2,1)} %copy-done.5) | copy-start | bytes 7077892
  155.1 11.2 %copy-start.3 = (f32[1,1536,3,1,128]{4,1,2,3,0:T(8,128)}, f32[1,1536,3,1,128]{4,1,2,3,0:T(8,128)S(1)}, u32[]{:S(2)}) copy-start(f32[1,1536,3,1,128]{4,1,2,3,0:T(8,128)S(1)} %copy.111) | copy-start | bytes 7077892
  162.0 4.4 %copy-start.4 = (f32[1,1536,3,1,128]{4,1,2,3,0:T(8,128)S(1)}, f32[1,1536,3,1,128]{4,1,2,3,0:T(8,128)}, u32[]{:S(2)}) copy-start(f32[1,1536,3,1,128]{4,1,2,3,0:T(8,128)} %copy.112) | copy-start | bytes 7077892
  162.0 4.4 %copy-start.7 = (bf16[3,2,1536,128]{2,3,0,1:T(8,128)(2,1)S(1)}, bf16[3,2,1536,128]{2,3,0,1:T(8,128)(2,1)}, u32[]{:S(2)}) copy-start(bf16[3,2,1536,128]{2,3,0,1:T(8,128)(2,1)} %broadcast_select_fusion) | copy-start | bytes 7077892
  187.0 88.0 %copy-start.18 = (pred[4,36]{1,0:T(4,128)(4,1)S(1)}, pred[4,36]{1,0:T(4,128)(4,1)}, u32[]{:S(2)}) copy-start(pred[4,36]{1,0:T(4,128)(4,1)} %broadcast_compare_fusion) | copy-start | bytes 436
  275.0 5.5 %copy-start.12 = (f32[3,128,128]{2,1,0:T(8,128)S(1)}, f32[3,128,128]{2,1,0:T(8,128)}, u32[]{:S(2)}) copy-start(f32[3,128,128]{2,1,0:T(8,128)} %fusion) | copy-start | bytes 589828
  276.8 12.1 %all-to-all-start = ((bf16[4,3,128,128]{3,2,1,0:T(8,128)(2,1)}), bf16[4,3,128,128]{3,2,1,0:T(8,128)(2,1)S(1)}, u32[]{:S(2)}, u32[]{:S(2)}) async-start(bf16[4,3,128,128]{3,2,1,0:T(8,128)(2,1)} %copy.100), calls=%async_computation | async-start | bytes 786432 | tf_op jit(solution)/shard_map/all_to_all | solution.py:89
  280.2 5.0 %copy-start.10 = (f32[3,2,128,128]{3,2,0,1:T(8,128)S(1)}, f32[3,2,128,128]{3,2,0,1:T(8,128)}, u32[]{:S(2)}) copy-start(f32[3,2,128,128]{3,2,0,1:T(8,128)} %copy_select_fusion) | copy-start | bytes 1179652
  280.3 5.0 %copy-start.11 = (f32[3,128,128]{2,1,0:T(8,128)S(1)}, f32[3,128,128]{2,1,0:T(8,128)}, u32[]{:S(2)}) copy-start(f32[3,128,128]{2,1,0:T(8,128)} %fusion.2) | copy-start | bytes 589828
  280.3 98.3 %all-reduce.3.cloned.1.call-start = ((), (), s32[]{:S(2)}) async-start(), calls=%async_computation.2 | async-start | bytes 393216 | tf_op jit(solution)/shard_map/psum | solution.py:59
  280.5 4.8 %copy-start.2 = (f32[1,1536,3,1,128]{4,1,2,3,0:T(8,128)S(1)}, f32[1,1536,3,1,128]{4,1,2,3,0:T(8,128)}, u32[]{:S(2)}) copy-start(f32[1,1536,3,1,128]{4,1,2,3,0:T(8,128)} %copy.110) | copy-start | bytes 7077892
  280.6 4.8 %copy-start.8 = (bf16[3,2,1536,128]{2,3,0,1:T(8,128)(2,1)S(1)}, bf16[3,2,1536,128]{2,3,0,1:T(8,128)(2,1)}, u32[]{:S(2)}) copy-start(bf16[3,2,1536,128]{2,3,0,1:T(8,128)(2,1)} %broadcast_select_fusion) | copy-start | bytes 7077892
  291.1 89.1 %copy-start.1 = (bf16[1,3,2,1536,128]{4,3,2,1,0:T(8,128)(2,1)S(1)}, bf16[1,3,2,1536,128]{4,3,2,1,0:T(8,128)(2,1)}, u32[]{:S(2)}) copy-start(bf16[1,3,2,1536,128]{4,3,2,1,0:T(8,128)(2,1)} %param.11) | copy-start | bytes 7077892
  291.1 3.9 %copy-start.17 = (f32[8,128]{1,0:T(8,128)S(1)}, f32[8,128]{1,0:T(8,128)}, u32[]{:S(2)}) copy-start(f32[8,128]{1,0:T(8,128)} %param.19) | copy-start | bytes 12292
  295.0 85.1 %copy-start.14 = (f32[8,128]{1,0:T(8,128)}, f32[8,128]{1,0:T(8,128)S(1)}, u32[]{:S(2)}) copy-start(f32[8,128]{1,0:T(8,128)S(1)} %multiply_reduce_fusion.1) | copy-start | bytes 12292
Sparse Core Ops, SparseCore 0:
  17.2 66.9 all-gather.1
  289.0 89.4 all-reduce.2
where the time goes:
time: 388 us; the launch traced here: 387 us
  waiting for transfers between devices  133 us (34%)
  blocking collectives  87.9 us (23%)
  local copies, waits for them, and re-layouts  71.2 us (18%)
  matrix products  59.5 us (15%)
  other arithmetic  16.8 us (4%)
  between operations  14.3 us (4%)
    psum x1, blocking collectives, body(): density_sum = lax.psum(partial_density, 'pole')  87.9 us
    psum x1, waiting for transfers between devices, body(): diag_density = lax.psum(diag_term, ('pole', 'col'))  82.9 us
    all_gather x1, waiting for transfers between devices, body(): lax.all_gather(send_rows, 'col', axis=0, tiled=True)  50.6 us
    dot_general x1, matrix products, body(): jnp.dot(stacked, lax.all_gather(send_rows, 'col', axis=0, tiled=True), pr...  37.8 us
    unnamed x45, local copies, waits for them, and re-layouts  28 us
    slice x1, local copies, waits for them, and re-layouts, body(): real_part = -(product[0, :, :, 0] - product[1, :, :, 1])  14.4 us
    reshape x1, local copies, waits for them, and re-layouts, body(): product = product.reshape(2, rows_local, PANELS, 2, W)  13.2 us
  transfers between devices with their start and end apart: 3, of which 2 were waited for; matrix products, arithmetic and copies ran while one was open for 8% of the time, Pallas kernels for 0%

commit v1 on v0

v1 whole, which is shorter than its diff:
```python
import functools

import jax
import jax.numpy as jnp
from jax import lax
from jax.experimental import pallas as pl
from jax.experimental.pallas import tpu as pltpu
from jax.sharding import PartitionSpec as P


CAP = 3

exchange_coeff = (3.0 / 3.141592653589793) ** (1.0 / 3.0)
density_floor = 0.5

F32 = jnp.float32
BF16 = jnp.bfloat16
SMEM = pl.BlockSpec(memory_space=pltpu.SMEM)
VMEM = pl.BlockSpec(memory_space=pltpu.VMEM)
LIMIT = 10 * 1024 * 1024
NEAR_LIMIT = 32 * 1024 * 1024


def swap(value, axis, mask):
    size = lax.axis_size(axis)
    return lax.ppermute(value, axis, [(i, i ^ mask) for i in range(size)])


def tree_sum(values):
    while len(values) > 1:
        values = [values[i] + values[i + 1] for i in range(0, len(values) - 1, 2)] + values[len(values) // 2 * 2 :]
    return values[0]


def row_block(rows):
    for size in (512, 384, 256, 128):
        if rows % size == 0:
            return size
    return rows


def complex_product(g_ref, rows, start, lower):
    real, imag = lower
    columns = pl.ds(start, real.shape[0])
    first = jnp.dot(
        g_ref[0, rows, columns], jnp.concatenate([real, imag], axis=1), preferred_element_type=F32
    )
    second = jnp.dot(
        g_ref[1, rows, columns], jnp.concatenate([-imag, real], axis=1), preferred_element_type=F32
    )
    return first + second


def near_kernel(place_ref, g_hbm, own_ref, partner_ref, acc_ref, far_ref, near_ref, near_sem, far_sem):
    panels, tile, _ = acc_ref.shape
    length, order = g_hbm.shape[1:]
    cols = order // length
    tiles = length // tile
    m = pl.program_id(0)
    me = place_ref[0]
    starts = [pl.multiple_of((me ^ mask) * length, length) for mask in range(cols)]

    def near_copy(step, mask):
        rows = pl.ds(step * tile, tile)
        return pltpu.make_async_copy(
            g_hbm.at[:, rows, pl.ds(starts[mask], length)],
            near_ref.at[:, rows, pl.ds(mask * length, length)],
            near_sem.at[step, mask],
        )

    def far_copy(mask):
        return pltpu.make_async_copy(
            g_hbm.at[:, :, pl.ds(starts[mask], length)],
            far_ref.at[:, :, pl.ds((mask - 2) * length, length)],
            far_sem.at[mask - 2],
        )

    @pl.when(m == 0)
    def _():
        for step in range(tiles):
            for mask in range(2):
                near_copy(step, mask).start()
        for mask in range(2, cols):
            far_copy(mask).start()

    rows = pl.ds(pl.multiple_of(m * tile, tile), tile)
    near_copy(m, 0).wait()
    for q in range(panels):
        acc_ref[q] = complex_product(near_ref, rows, 0, (own_ref[q, 0], own_ref[q, 1]))
    near_copy(m, 1).wait()
    for q in range(panels):
        acc_ref[q] += complex_product(near_ref, rows, length, (partner_ref[q, 0], partner_ref[q, 1]))

    @pl.when(m == tiles - 1)
    def _():
        for mask in range(2, cols):
            far_copy(mask).wait()


def near_product(place, matrix, own, partner):
    panels, _, rows, width = own.shape
    order = matrix.shape[2]
    tile = row_block(rows)
    whole = pl.BlockSpec(own.shape, lambda m: (0, 0, 0, 0), pipeline_mode=pl.Buffered(1))
    return pl.pallas_call(
        near_kernel,
        grid=(rows // tile,),
        in_specs=[SMEM, pl.BlockSpec(memory_space=pl.ANY), whole, whole],
        out_specs=[pl.BlockSpec((panels, tile, 2 * width), lambda m: (0, m, 0)), VMEM],
        out_shape=[
            jax.ShapeDtypeStruct((panels, rows, 2 * width), F32),
            pltpu.VMEM((2, rows, order - 2 * rows), BF16),
        ],
        scratch_shapes=[
            pltpu.VMEM((2, rows, 2 * rows), BF16),
            pltpu.SemaphoreType.DMA((rows // tile, 2)),
            pltpu.SemaphoreType.DMA((order // rows - 2,)),
        ],
        compiler_params=pltpu.CompilerParams(vmem_limit_bytes=NEAR_LIMIT),
        cost_estimate=pl.CostEstimate(
            flops=2 * 8 * rows * rows * panels * width, bytes_accessed=4 * rows * order, transcendentals=0
        ),
        name="near_product",
    )(place, matrix, own, partner)


def far_terms(g_ref, rows, step, offset, left_ref, right_ref):
    length = g_ref.shape[1]
    total = None
    for mask, ref in ((2 * step, left_ref), (2 * step + 1, right_ref)):
        term = complex_product(g_ref, rows, (mask - 2) * length + offset, (ref[0], ref[1]))
        total = term if total is None else total + term
    return total


def far_kernel(step, offset, g_ref, left_ref, right_ref, acc_ref, out_ref):
    tile = out_ref.shape[0]
    rows = pl.ds(pl.multiple_of(pl.program_id(0) * tile, tile), tile)
    out_ref[...] = acc_ref[...] + far_terms(g_ref, rows, step, offset, left_ref, right_ref)


def far_product(g, left, right, acc, panel, step, offset):
    _, depth, width = left.shape
    rows = g.shape[1]
    tile = row_block(rows)
    whole = pl.BlockSpec(left.shape, lambda m: (0, 0, 0), pipeline_mode=pl.Buffered(1))
    return pl.pallas_call(
        functools.partial(far_kernel, step, offset),
        grid=(rows // tile,),
        in_specs=[
            VMEM,
            whole,
            whole,
            pl.BlockSpec((None, tile, 2 * width), lambda m: (panel, m, 0)),
        ],
        out_specs=pl.BlockSpec((None, tile, 2 * width), lambda m: (panel, m, 0)),
        out_shape=jax.ShapeDtypeStruct(acc.shape, F32),
        input_output_aliases={3: 0},
        compiler_params=pltpu.CompilerParams(vmem_limit_bytes=LIMIT),
        cost_estimate=pl.CostEstimate(
            flops=2 * 8 * rows * depth * width, bytes_accessed=8 * rows * width, transcendentals=0
        ),
        name="far_product",
    )(g, left, right, acc)


def last_kernel(
    poles, step, offset, place_ref, g_ref, left_ref, right_ref, acc_ref, own_ref, diag_ref, weight_ref, *rest
):
    out_refs, (y_ref, d_ref) = rest[:poles], rest[poles:]
    m = pl.program_id(0)
    tile, width = own_ref.shape[1:]
    count = tile // width
    blocks = y_ref.shape[0]
    rows = pl.ds(pl.multiple_of(m * tile, tile), tile)

    weight_real = weight_ref[0, 0]
    weight_imag = weight_ref[0, 1]
    total = acc_ref[...] + far_terms(g_ref, rows, step, offset, left_ref, right_ref)
    real = -total[:, :width]
    imag = -total[:, width:]
    density = weight_real * imag + weight_imag * real
    other = weight_real * real - weight_imag * imag
    y_ref[pl.ds(m * count, count)] = density.reshape(count, poles, width // poles, width)

    def cross(lower, value):
        high = value.astype(BF16)
        low = (value - high.astype(F32)).astype(BF16)
        both = lax.dot_general(
            lower,
            jnp.concatenate([high, low], axis=1),
            (((0,), (0,)), ((), ())),
            preferred_element_type=F32,
        )
        return both[:, :width] + both[:, width:]

    part = (cross(own_ref[0], density) + cross(own_ref[1], other)).reshape(d_ref.shape)

    @pl.when(m == 0)
    def _():
        lead = (place_ref[0] == 0).astype(F32)
        term = lead * (weight_real * diag_ref[1] + weight_imag * diag_ref[0])
        d_ref[...] = term.reshape(d_ref.shape) - part

    @pl.when(m > 0)
    def _():
        d_ref[...] -= part

    @pl.when(m == pl.num_programs(0) - 1)
    def _():
        for mask, out_ref in enumerate(out_refs):
            other_pole = place_ref[1] ^ mask
            kind = out_ref.dtype
            out_ref[:blocks] = y_ref[:, other_pole].astype(kind)
            diag = d_ref[other_pole]
            high = diag.astype(kind)
            out_ref[blocks] = high
            if kind != F32:
                out_ref[blocks + 1] = (diag - high.astype(F32)).astype(kind)


def last_product(place, g, left, right, acc, own, diag, weights, panel, step, offset, poles, kind):
    _, depth, width = left.shape
    rows = g.shape[1]
    tile = row_block(rows)
    blocks = rows // width
    whole = pl.BlockSpec(left.shape, lambda m: (0, 0, 0), pipeline_mode=pl.Buffered(1))
    shape = (blocks + (1 if kind == F32 else 2), width // poles, width)
    return pl.pallas_call(
        functools.partial(last_kernel, poles, step, offset),
        grid=(rows // tile,),
        in_specs=[
            SMEM,
            VMEM,
            whole,
            whole,
            pl.BlockSpec((None, tile, 2 * width), lambda m: (panel, m, 0)),
            pl.BlockSpec((None, 2, tile, width), lambda m: (panel, 0, m, 0)),
            pl.BlockSpec((None, 2, width, width), lambda m: (panel, 0, 0, 0)),
            SMEM,
        ],
        out_specs=[pl.BlockSpec(shape, lambda m: (0, 0, 0))] * poles,
        scratch_shapes=[
            pltpu.VMEM((blocks, poles, width // poles, width), F32),
            pltpu.VMEM((poles, width // poles, width), F32),
        ],
        out_shape=[jax.ShapeDtypeStruct(shape, kind)] * poles,
        compiler_params=pltpu.CompilerParams(vmem_limit_bytes=LIMIT),
        cost_estimate=pl.CostEstimate(
            flops=2 * 8 * rows * depth * width, bytes_accessed=8 * rows * width, transcendentals=0
        ),
        name="last_product",
    )(place, g, left, right, acc, own, diag, weights)


def table_kernel(per_device, panels, place_ref, order_ref, supports_ref, counts_ref, send_ref, slot_ref):
    tiles, most = supports_ref.shape
    cols = send_ref.shape[0]
    total = cols * per_device
    me = place_ref[0]
    supports = supports_ref[...]
    counts = counts_ref[...]
    ids = lax.broadcasted_iota(jnp.int32, (tiles, total), 1)
    named = []
    for k in range(most):
        named.append((supports[:, k : k + 1] == ids) & (counts > k))
    any_named = named[0]
    for hit in named[1:]:
        any_named = any_named | hit
    tile_hits = jnp.where(any_named, 1.0, 0.0)
    group_row = lax.broadcasted_iota(jnp.int32, (cols, tiles), 0)
    group_tile = lax.broadcasted_iota(jnp.int32, (cols, tiles), 1)
    group = jnp.where(
        (group_tile >= group_row * (tiles // cols)) & (group_tile < (group_row + 1) * (tiles // cols)), 1.0, 0.0
    )
    needed = jnp.minimum(
        jnp.dot(group.astype(BF16), tile_hits.astype(BF16), preferred_element_type=F32), 1.0
    )
    first = lax.broadcasted_iota(jnp.int32, (total, total), 0)
    second = lax.broadcasted_iota(jnp.int32, (total, total), 1)
    earlier = (first <= second) & (first // per_device == second // per_device)
    rank = jnp.dot(
        needed.astype(BF16), jnp.where(earlier, 1.0, 0.0).astype(BF16), preferred_element_type=F32
    )
    block = lax.broadcasted_iota(jnp.int32, (cols, total), 1)
    dest = lax.broadcasted_iota(jnp.int32, (cols, total), 0)
    owner = block // per_device
    local = block - owner * per_device
    row = local // panels
    spot = local - row * panels
    panel = jnp.zeros_like(spot)
    for j in range(panels):
        panel = jnp.where(spot == j, order_ref[j], panel)
    code = (panel * (per_device // panels) + row).astype(F32)
    mine = (needed > 0.5) & (owner == me)
    lane = lax.broadcasted_iota(jnp.int32, send_ref.shape, 1)
    send = jnp.zeros(send_ref.shape, F32)
    for c in range(CAP):
        value = jnp.sum(jnp.where(mine & (rank == c + 1.0), code, 0.0), axis=1, keepdims=True)
        send = jnp.where(lane == c, value, send)
    send_ref[...] = send.astype(jnp.int32)
    mask = (owner ^ me).astype(F32)
    spots = jnp.where((needed > 0.5) & (dest == me), mask * CAP + jnp.minimum(rank, CAP) - 1.0, 0.0)
    spots = jnp.sum(spots, axis=0, keepdims=True)
    place = lax.broadcasted_iota(jnp.int32, slot_ref.shape, 1)
    slot = jnp.zeros(slot_ref.shape, F32)
    for k, hit in enumerate(named):
        slot = jnp.where(place == k, jnp.sum(jnp.where(hit, spots, 0.0), axis=1, keepdims=True), slot)
    slot_ref[...] = slot.astype(jnp.int32)


def tables(place, supports, counts, order, cols, per_device, panels):
    tiles, most = supports.shape
    return pl.pallas_call(
        functools.partial(table_kernel, per_device, panels),
        in_specs=[SMEM, SMEM, VMEM, VMEM],
        out_specs=[VMEM] * 2,
        out_shape=[
            jax.ShapeDtypeStruct((cols, most), jnp.int32),
            jax.ShapeDtypeStruct((tiles, most), jnp.int32),
        ],
        compiler_params=pltpu.CompilerParams(vmem_limit_bytes=LIMIT),
        cost_estimate=pl.CostEstimate(flops=1 << 20, bytes_accessed=1 << 20, transcendentals=0),
        name="tables",
    )(place, order, supports, counts.reshape(tiles, 1))


def total_of(parts, blocks):
    density = tree_sum([part[:blocks].astype(F32) for part in parts])
    diag = [part[blocks].astype(F32) for part in parts]
    if parts[0].dtype != F32:
        diag = [high + part[blocks + 1].astype(F32) for high, part in zip(diag, parts)]
    return density.astype(BF16), tree_sum(diag)


def settle_kernel(poles, blocks, *refs):
    density_ref, diag_ref = refs[-2:]
    for q in range(diag_ref.shape[0]):
        density, diag = total_of(refs[q * poles : (q + 1) * poles], blocks)
        density_ref[q * blocks : (q + 1) * blocks] = density
        diag_ref[q] = diag


def settle(groups, blocks):
    poles = len(groups[0])
    depth, width = groups[0][0].shape[1:]
    return pl.pallas_call(
        functools.partial(settle_kernel, poles, blocks),
        in_specs=[VMEM] * (poles * len(groups)),
        out_specs=[VMEM] * 2,
        out_shape=[
            jax.ShapeDtypeStruct((len(groups) * blocks, depth, width), BF16),
            jax.ShapeDtypeStruct((len(groups), depth, width), F32),
        ],
        compiler_params=pltpu.CompilerParams(vmem_limit_bytes=LIMIT),
        cost_estimate=pl.CostEstimate(flops=1 << 20, bytes_accessed=2 << 20, transcendentals=0),
        name="settle",
    )(*[part for group in groups for part in group])


def pick_kernel(poles, blocks, place_ref, send_ref, early_ref, early_diag_ref, *rest):
    parts, out_refs, all_ref = rest[:poles], rest[poles:-1], rest[-1]
    early = early_ref.shape[0]
    all_ref[:early] = early_ref[...]
    density, last_diag = total_of(parts, blocks)
    all_ref[early:] = density
    diags = [early_diag_ref[q] for q in range(early_diag_ref.shape[0])] + [last_diag]
    for mask, out_ref in enumerate(out_refs):
        for c in range(CAP):
            out_ref[c] = all_ref[send_ref[place_ref[0] ^ mask, c]]
        for q, diag in enumerate(diags):
            high = diag.astype(BF16)
            out_ref[CAP + 2 * q] = high
            out_ref[CAP + 2 * q + 1] = (diag - high.astype(F32)).astype(BF16)


def pick(place, send, early, early_diag, parts, blocks, cols):
    poles = len(parts)
    depth, width = early.shape[1:]
    shape = (CAP + 2 * (early_diag.shape[0] + 1), depth, width)
    return pl.pallas_call(
        functools.partial(pick_kernel, poles, blocks),
        in_specs=[SMEM, SMEM] + [VMEM] * (2 + poles),
        out_specs=[VMEM] * cols,
        out_shape=[jax.ShapeDtypeStruct(shape, BF16)] * cols,
        scratch_shapes=[pltpu.VMEM((early.shape[0] + blocks, depth, width), BF16)],
        compiler_params=pltpu.CompilerParams(vmem_limit_bytes=LIMIT),
        name="pick",
    )(place, send, early, early_diag, *parts)


def join_kernel(*refs):
    parts, out_ref = refs[:-1], refs[-1]
    for mask, part in enumerate(parts):
        for c in range(CAP):
            out_ref[mask * CAP + c] = part[c]
    for q in range(out_ref.shape[0] - len(parts) * CAP):
        place = CAP + 2 * q
        total = tree_sum([part[place].astype(F32) + part[place + 1].astype(F32) for part in parts])
        out_ref[len(parts) * CAP + q] = total.astype(BF16)


def join(parts):
    depth, width = parts[0].shape[1:]
    extra = (parts[0].shape[0] - CAP) // 2
    return pl.pallas_call(
        join_kernel,
        in_specs=[VMEM] * len(parts),
        out_specs=VMEM,
        out_shape=jax.ShapeDtypeStruct((len(parts) * CAP + extra, depth, width), BF16),
        compiler_params=pltpu.CompilerParams(vmem_limit_bytes=LIMIT),
        name="join",
    )(*parts)


def tile_kernel(
    place_ref, order_ref, slot_ref, supports_ref, counts_ref, row_ref, orbital_ref, core_ref, *rest
):
    parts = rest[:-4]
    valence_ref, potential_ref, diag_ref, blocks_ref = rest[-4:]
    tiles, most = row_ref.shape[:2]
    slots, poles, depth, width = blocks_ref.shape
    panels = diag_ref.shape[0]
    first = place_ref[0] * tiles

    for mask, part in enumerate(parts):
        owner = place_ref[1] ^ mask
        blocks_ref[:, owner] = part[:slots]
        for j in range(panels):
            diag_ref[j, owner] = part[slots + order_ref[j]].astype(F32)

    def one(t, _):
        valence = jnp.zeros((1, row_ref.shape[-1]), F32)
        for k in range(most):
            mixed = jnp.dot(
                blocks_ref[slot_ref[first + t, k]].reshape(poles * depth, width),
                orbital_ref[t, lax.rem(supports_ref[first + t, k], panels)],
                preferred_element_type=F32,
            )
            term = jnp.sum(row_ref[t, k].astype(F32) * mixed, axis=0, keepdims=True)
            valence = valence + jnp.where(k < counts_ref[first + t], term, 0.0)
        valence_ref[t] = valence
        return 0

    lax.fori_loop(0, tiles, one, 0, unroll=True)
    clamped = jnp.maximum(core_ref[...] + valence_ref[...], density_floor)
    potential_ref[...] = -exchange_coeff * clamped ** (1.0 / 3.0)


def tile_stage(place, order, slot, supports, counts, rows, orbitals, core, parts, cols):
    tiles, _, width, points = rows.shape
    panels = orbitals.shape[1]
    slots = cols * CAP
    poles = len(parts)
    depth = width // poles
    valence, potential, diag = pl.pallas_call(
        tile_kernel,
        in_specs=[SMEM] * 5 + [VMEM] * (3 + poles),
        out_specs=[VMEM] * 3,
        out_shape=[
            jax.ShapeDtypeStruct((tiles, 1, points), F32),
            jax.ShapeDtypeStruct((tiles, 1, points), F32),
            jax.ShapeDtypeStruct((panels, poles, depth, width), F32),
        ],
        scratch_shapes=[pltpu.VMEM((slots, poles, depth, width), BF16)],
        compiler_params=pltpu.CompilerParams(vmem_limit_bytes=LIMIT),
        name="tile_stage",
    )(place, order, slot, supports, counts, rows, orbitals, core.reshape(tiles, 1, points), *parts)
    return valence.reshape(tiles, points), potential.reshape(tiles, points), diag.reshape(panels, width, width)


def body(
    inverse,
    panels,
    diag_inverse,
    pole_weights,
    supports,
    counts,
    panel_order,
    row_orbitals,
    panel_orbitals,
    core_density,
):
    cols = lax.axis_size("col")
    poles = lax.axis_size("pole")
    me = lax.axis_index("col").astype(jnp.int32)
    my_pole = lax.axis_index("pole").astype(jnp.int32)
    matrix = inverse[0]
    own = panels[0]
    diag = diag_inverse[0]
    panel_count, _, rows, width = own.shape
    blocks = rows // width
    per_device = blocks * panel_count
    place = jnp.stack([me, my_pole])
    steps = range(1, cols // 2)

    pieces = []
    for q in range(panel_count):
        parts = 2 if q == panel_count - 1 else 1
        pieces += [(q, part * (rows // parts), rows // parts) for part in range(parts)]

    remote = {}
    source = own
    for piece, (q, offset, depth) in enumerate(pieces):
        part = source[q, :, offset : offset + depth]
        if piece == 0:
            part, source = lax.optimization_barrier((part, own))
        for step in steps:
            remote[step, piece] = swap(part, "col", 2 * step)
    partner = swap(own, "col", 1)
    forward = {}
    for (step, piece), value in remote.items():
        forward[step, piece] = swap(value, "col", 1)

    send, slot = tables(place, supports, counts, panel_order, cols, per_device, panel_count)
    acc, staged = near_product(place, matrix, own, partner)
    sums = []
    for piece, (q, offset, depth) in enumerate(pieces):
        for step in steps:
            left, right = remote[step, piece], forward[step, piece]
            if step < cols // 2 - 1 or offset + depth < rows:
                acc = far_product(staged, left, right, acc, q, step, offset)
                continue
            kind = F32 if q == 0 else BF16
            parts = last_product(place, staged, left, right, acc, own, diag, pole_weights, q, step, offset, poles, kind)
            group = [parts[0]]
            for mask in range(1, poles):
                group.append(swap(parts[mask], "pole", mask))
            sums.append(group)

    early, early_diag = settle(sums[:-1], blocks)
    messages = pick(place, send, early, early_diag, sums[-1], blocks, cols)
    arrived = [messages[0]] + [swap(messages[mask], "col", mask) for mask in range(1, cols)]
    joined = join(arrived)
    gathered = [joined] + [swap(joined, "pole", mask) for mask in range(1, poles)]
    return tile_stage(
        place,
        panel_order,
        slot,
        supports,
        counts,
        row_orbitals,
        panel_orbitals,
        core_density,
        gathered,
        cols,
    )


def solution(mesh):
    placed = (
        P(("job", "pole"), None, "col", None),
        P(("job", "pole"), None, None, "col", None),
        P(("job", "pole"), None, None, None, None),
        P(("job", "pole"), None),
        P(),
        P(),
        P(),
        P(("job", "col"), None, None, "pole"),
        P(("job", "col"), None, None, "pole"),
        P(("job", "col"), "pole"),
    )
    return jax.shard_map(
        body,
        mesh=mesh,
        in_specs=placed,
        out_specs=(P(("job", "col"), "pole"), P(("job", "col"), "pole"), P("job", None, None)),
        check_vma=False,
    )
```

time: 388 us -> 170 us (0.44)
  blocking collectives: 87.9 us -> 0 us
  waiting for transfers between devices: 133 us -> 69.9 us
  matrix products: 59.5 us -> 0 us
  Pallas kernels: 0 us -> 55.7 us
  local copies, waits for them, and re-layouts: 71.2 us -> 15.6 us
  starting transfers between devices: 3.76 us -> 27 us
  other arithmetic: 16.8 us -> 0.07 us
  between operations: 14.3 us -> 0.87 us
    psum x1 -> x0, blocking collectives: 87.9 us -> none  [body(): density_sum = lax.psum(partial_density, 'pole')]
    psum x1 -> x0, waiting for transfers between devices: 82.9 us -> none  [body(): diag_density = lax.psum(diag_term, ('pole', 'col'))]
    ppermute x0 -> x24, waiting for transfers between devices: none -> 69.9 us  [swap(): return lax.ppermute(value, axis, [(i, i ^ mask) for i in range(size)])]
    dot_general x8 -> x0, matrix products: 59.5 us -> none  [the longest x1 37.8 us: body(): jnp.dot(stacked, lax.all_gather(send_rows, 'col', axis=0, tiled=True), pr...]
    pallas_call x0 -> x10, Pallas kernels: none -> 55.7 us  [the longest x1 25.1 us: near_product(): pl.pallas_call(near_kernel, grid=(rows // tile,), in_specs=[SMEM, pl.Bloc...]
    all_gather x1 -> x0, waiting for transfers between devices: 50.6 us -> none  [body(): lax.all_gather(send_rows, 'col', axis=0, tiled=True)]
    ppermute x0 -> x24, starting transfers between devices: none -> 27 us  [swap(): return lax.ppermute(value, axis, [(i, i ^ mask) for i in range(size)])]
    unnamed x45 -> x49, local copies, waits for them, and re-layouts: 28 us -> 10.2 us
  transfers between devices with their start and end apart: 3 -> 24, of which waited for: 2 -> 8; matrix products, arithmetic and copies ran while one was open for 8% -> 3% of each run, Pallas kernels for 0% -> 31%
where the time goes in v1:
time: 170 us; the launch traced here: 169 us
  waiting for transfers between devices  69.9 us (41%)
  Pallas kernels  55.7 us (33%)
  starting transfers between devices  27 us (16%)
  local copies, waits for them, and re-layouts  15.6 us (9%)
    ppermute x24, waiting for transfers between devices, swap(): return lax.ppermute(value, axis, [(i, i ^ mask) for i in range(size)])  69.9 us
    ppermute x24, starting transfers between devices, swap(): return lax.ppermute(value, axis, [(i, i ^ mask) for i in range(size)])  27 us
    pallas_call x1, Pallas kernels, near_product(): pl.pallas_call(near_kernel, grid=(rows // tile,), in_specs=[SMEM, pl.Bloc...  25.1 us
    pallas_call x3, Pallas kernels, last_product(): pl.pallas_call(functools.partial(last_kernel, poles, step, offset), grid=...  21.7 us
    unnamed x49, local copies, waits for them, and re-layouts  10.2 us
    squeeze x3, local copies, waits for them, and re-layouts, body(): part = source[q, :, offset:offset + depth]  5.23 us
  transfers between devices with their start and end apart: 24, of which 8 were waited for; matrix products, arithmetic and copies ran while one was open for 3% of the time, Pallas kernels for 31%

profile of v1, /device:TPU:0, one launch (start us, length us, event | category | flops | bytes accessed | tf_op | source)
XLA Modules:
  0.0 169.1 jit_solution(6135210284940305127)
XLA Ops:
  1.2 2.2 %slice_bitcast_fusion.1 = bf16[2,1536,128]{2,1,0:T(8,128)(2,1)} fusion(bf16[1,3,2,1536,128]{4,3,2,1,0:T(8,128)(2,1)} %param.11), kind=kLoop, calls=%fused_computation.1 | loop fusion | bytes 1572864 | tf_op jit(solution)/shard_map/squeeze | solution.py:505
  3.4 2.1 %slice_bitcast_fusion = bf16[2,1536,128]{2,1,0:T(8,128)(2,1)} fusion(bf16[3,2,1536,128]{3,2,1,0:T(8,128)(2,1)} %bitcast.19), kind=kLoop, calls=%fused_computation | loop fusion | bytes 1572864 | tf_op jit(solution)/shard_map/squeeze | solution.py:505
  5.5 2.5 %collective-permute-start.6 = (bf16[2,1536,128]{2,1,0:T(8,128)(2,1)}, bf16[2,1536,128]{2,1,0:T(8,128)(2,1)}, u32[]{:S(2)}, u32[]{:S(2)}) collective-permute-start(bf16[2,1536,128]{2,1,0:T(8,128)(2,1)} %slice_bitcast_fusion), channel_id=1, source_target_pairs={{0,2},{1,3},{2,0},{3,1},{4,6},{5,7},{6,4},{7,5},{8,10},{9,11},{10,... | collective-permute-start | bytes 2359304 | tf_op jit(solution)/shard_map/ppermute | solution.py:26
  9.0 2.0 %collective-permute-start.13 = (bf16[2,768,128]{2,1,0:T(8,128)(2,1)}, bf16[2,768,128]{2,1,0:T(8,128)(2,1)S(1)}, u32[]{:S(2)}, u32[]{:S(2)}) collective-permute-start(bf16[2,768,128]{2,1,0:T(8,128)(2,1)} %get-tuple-element.57), channel_id=1, source_target_pairs={{0,2},{1,3},{2,0},{3,1},{4,6},{5,7},{6,4},{7,5},{8,10},{9,11},{10,... | collective-permute-start | bytes 1179656 | tf_op jit(solution)/shard_map/ppermute | solution.py:26
  11.1 40.8 %collective-permute-done.13.left_ref = bf16[2,768,128]{2,1,0:T(8,128)(2,1)S(1)} collective-permute-done((bf16[2,768,128]{2,1,0:T(8,128)(2,1)}, bf16[2,768,128]{2,1,0:T(8,128)(2,1)S(1)}, u32[]{:S(2)}, u32[]{:S(2)}) %collective-permute-start.13) | collective-permute-done | bytes 393248 | tf_op jit(solution)/shard_map/ppermute | solution.py:26
  51.9 8.2 %collective-permute-done.11.left_ref = bf16[2,768,128]{2,1,0:T(8,128)(2,1)} collective-permute-done((bf16[2,768,128]{2,1,0:T(8,128)(2,1)}, bf16[2,768,128]{2,1,0:T(8,128)(2,1)}, u32[]{:S(2)}, u32[]{:S(2)}) %collective-permute-start.11) | collective-permute-done | bytes 393248 | tf_op jit(solution)/shard_map/ppermute | solution.py:26
  60.7 25.1 %near_product.1 = (f32[3,1536,256]{2,1,0:T(8,128)}, bf16[2,1536,3072]{2,1,0:T(8,128)(2,1)S(1)}) custom-call(s32[2]{0:T(128)S(1)} %pad_add_fusion.place_ref, bf16[2,1536,6144]{2,1,0:T(8,128)(2,1)} %bitcast.30, bf16[3,2,1536,128]{3,2,1,0:T(8,128)(2,1)S(1)} %bitcast.21, bf16[3,2,1536,128]{3,2,1,0:T(8,128)(2,1)} %collective-permute-done.partner_ref), custom_call_target="tpu_custom_call" | custom-call | flops 14495514624 | bytes 37748736 | tf_op jit(solution)/shard_map/near_product/pallas_call | solution.py:105
  85.8 2.3 %copy-done = f32[3,1536,256]{2,1,0:T(8,128)S(1)} copy-done((f32[3,1536,256]{2,1,0:T(8,128)S(1)}, f32[3,1536,256]{2,1,0:T(8,128)}, u32[]{:S(2)}) %copy-start) | copy-done | bytes 4718616
  88.1 7.7 %last_product.4 = (bf16[14,32,128]{2,1,0:T(8,128)(2,1)S(1)}, bf16[14,32,128]{2,1,0:T(8,128)(2,1)S(1)}, bf16[14,32,128]{2,1,0:T(8,128)(2,1)S(1)}, bf16[14,32,128]{2,1,0:T(8,128)(2,1)S(1)}) custom-call(s32[2]{0:T(128)S(1)} %pad_add_fusion.place_ref, bf16[2,1536,3072]{2,1,0:T(8,128)(2,1)S(1)} %get-tuple-element.32.g_ref, ...), custom_call_target="tpu_custom_call" | custom-call | flops 4831838208 | bytes 1572864 | tf_op jit(solution)/shard_map/last_product/pallas_call | solution.py:229
  96.5 3.9 %collective-permute-start.10 = (bf16[14,32,128]{2,1,0:T(8,128)(2,1)S(1)}, bf16[14,32,128]{2,1,0:T(8,128)(2,1)S(1)}, u32[]{:S(2)}, u32[]{:S(2)}) collective-permute-start(bf16[14,32,128]{2,1,0:T(8,128)(2,1)S(1)} %get-tuple-element.43), channel_id=1, source_target_pairs={{0,12},{4,8},{8,4},{12,0},{1,13},{5,9},{9,5},{13,1},{2,14},{6,10},... | collective-permute-start | bytes 344072 | tf_op jit(solution)/shard_map/ppermute | solution.py:26
  100.9 7.9 %last_product.3 = (f32[13,32,128]{2,1,0:T(8,128)S(1)}, f32[13,32,128]{2,1,0:T(8,128)S(1)}, f32[13,32,128]{2,1,0:T(8,128)}, f32[13,32,128]{2,1,0:T(8,128)}) custom-call(s32[2]{0:T(128)S(1)} %pad_add_fusion.place_ref, bf16[2,1536,3072]{2,1,0:T(8,128)(2,1)S(1)} %get-tuple-element.32.g_ref, bf16[2,1536,128]{2,1,0:T(8,128)(2,1)S(1)} %collective-permute-done.1.left_ref, ...), custom_call_target="tpu_custom_call" | custom-call | flops 4831838208 | bytes 1572864 | tf_op jit(solution)/shard_map/last_product/pallas_call | solution.py:229
  110.4 3.1 %far_product.1.acc_ref = f32[3,1536,256]{2,1,0:T(8,128)S(1)} custom-call(bf16[2,1536,3072]{2,1,0:T(8,128)(2,1)S(1)} %get-tuple-element.32.g_ref, bf16[2,768,128]{2,1,0:T(8,128)(2,1)S(1)} %collective-permute-done.13.left_ref, bf16[2,768,128]{2,1,0:T(8,128)(2,1)S(1)} %collective-permute-done.14.right_ref, ...), custom_call_target="tpu_custom_call", output_to_operand_aliasing={{}: (3, {})} | custom-call | flops 2415919104 | bytes 1572864 | tf_op jit(solution)/shard_map/far_product/pallas_call | solution.py:147
  113.5 3.0 %collective-permute-start.4 = (f32[13,32,128]{2,1,0:T(8,128)}, f32[13,32,128]{2,1,0:T(8,128)}, u32[]{:S(2)}, u32[]{:S(2)}) collective-permute-start(f32[13,32,128]{2,1,0:T(8,128)} %get-tuple-element.37), channel_id=1, source_target_pairs={{0,8},{4,12},{8,0},{12,4},{1,9},{5,13},{9,1},{13,5},{2,10},{6,14},... | collective-permute-start | bytes 638984 | tf_op jit(solution)/shard_map/ppermute | solution.py:26
  116.6 6.0 %last_product.5 = (bf16[14,32,128]{2,1,0:T(8,128)(2,1)S(1)}, bf16[14,32,128]{2,1,0:T(8,128)(2,1)}, bf16[14,32,128]{2,1,0:T(8,128)(2,1)}, bf16[14,32,128]{2,1,0:T(8,128)(2,1)}) custom-call(s32[2]{0:T(128)S(1)} %pad_add_fusion.place_ref, bf16[2,1536,3072]{2,1,0:T(8,128)(2,1)S(1)} %get-tuple-element.32.g_ref, ...), custom_call_target="tpu_custom_call" | custom-call | flops 2415919104 | bytes 1572864 | tf_op jit(solution)/shard_map/last_product/pallas_call | solution.py:229
  125.0 3.8 %collective-permute-start.16 = (bf16[14,32,128]{2,1,0:T(8,128)(2,1)}, bf16[14,32,128]{2,1,0:T(8,128)(2,1)S(1)}, u32[]{:S(2)}, u32[]{:S(2)}) collective-permute-start(bf16[14,32,128]{2,1,0:T(8,128)(2,1)} %get-tuple-element.48), channel_id=1, source_target_pairs={{0,8},{4,12},{8,0},{12,4},{1,9},{5,13},{9,1},{13,5},{2,10},{6,14},... | collective-permute-start | bytes 344072 | tf_op jit(solution)/shard_map/ppermute | solution.py:26
  130.9 4.2 %collective-permute-done.4.refs_2_ = f32[13,32,128]{2,1,0:T(8,128)} collective-permute-done((f32[13,32,128]{2,1,0:T(8,128)}, f32[13,32,128]{2,1,0:T(8,128)}, u32[]{:S(2)}, u32[]{:S(2)}) %collective-permute-start.4) | collective-permute-done | bytes 213024 | tf_op jit(solution)/shard_map/ppermute | solution.py:26
  139.8 3.4 %collective-permute-done.16.rest_2_ = bf16[14,32,128]{2,1,0:T(8,128)(2,1)S(1)} collective-permute-done((bf16[14,32,128]{2,1,0:T(8,128)(2,1)}, bf16[14,32,128]{2,1,0:T(8,128)(2,1)S(1)}, u32[]{:S(2)}, u32[]{:S(2)}) %collective-permute-start.16) | collective-permute-done | bytes 114720 | tf_op jit(solution)/shard_map/ppermute | solution.py:26
  145.2 1.6 collective-permute-start.19
  147.0 2.9 %collective-permute-done.19.refs_2_ = bf16[9,32,128]{2,1,0:T(8,128)(2,1)S(1)} collective-permute-done((bf16[9,32,128]{2,1,0:T(8,128)(2,1)S(1)}, bf16[9,32,128]{2,1,0:T(8,128)(2,1)S(1)}, u32[]{:S(2)}, u32[]{:S(2)}) %collective-permute-start.19) | collective-permute-done | bytes 73760 | tf_op jit(solution)/shard_map/ppermute | solution.py:26
  151.3 3.1 %collective-permute-start.21 = (bf16[15,32,128]{2,1,0:T(8,128)(2,1)S(1)}, bf16[15,32,128]{2,1,0:T(8,128)(2,1)S(1)}, u32[]{:S(2)}, u32[]{:S(2)}) collective-permute-start(bf16[15,32,128]{2,1,0:T(8,128)(2,1)S(1)} %join.1.rest_0_), channel_id=1, source_target_pairs={{0,4},{4,0},{8,12},{12,8},{1,5},{5,1},{9,13},{13,9},{2,6},{6,2},{1... | collective-permute-start | bytes 368648 | tf_op jit(solution)/shard_map/ppermute | solution.py:26
  154.3 1.6 collective-permute-start.22
  157.3 2.5 %collective-permute-done.21.rest_1_ = bf16[15,32,128]{2,1,0:T(8,128)(2,1)S(1)} collective-permute-done((bf16[15,32,128]{2,1,0:T(8,128)(2,1)S(1)}, bf16[15,32,128]{2,1,0:T(8,128)(2,1)S(1)}, u32[]{:S(2)}, u32[]{:S(2)}) %collective-permute-start.21) | collective-permute-done | bytes 122912 | tf_op jit(solution)/shard_map/ppermute | solution.py:26
  159.9 6.6 %collective-permute-done.22.rest_2_ = bf16[15,32,128]{2,1,0:T(8,128)(2,1)S(1)} collective-permute-done((bf16[15,32,128]{2,1,0:T(8,128)(2,1)S(1)}, bf16[15,32,128]{2,1,0:T(8,128)(2,1)S(1)}, u32[]{:S(2)}, u32[]{:S(2)}) %collective-permute-start.22) | collective-permute-done | bytes 122912 | tf_op jit(solution)/shard_map/ppermute | solution.py:26
  166.5 2.6 %tile_stage.1 = (f32[8,1,128]{2,1,0:T(1,128)}, f32[8,1,128]{2,1,0:T(1,128)}, f32[3,4,32,128]{3,2,1,0:T(8,128)}) custom-call(s32[2]{0:T(128)S(1)} %pad_add_fusion.place_ref, s32[3]{0:T(128)S(1)} %copy-done.21, s32[32,8]{1,0:T(8,128)S(1)} %get-tuple-element.30.slot_ref, s32[32,8]{1,0:T(8,128)S(1)} %copy.14.supports_ref, s32[32]{0:T(128)S(1)} %copy-done.22, ...), custom_call_target="tpu_custom_call" | custom-call | tf_op jit(solution)/shard_map/tile_stage/pallas_call | solution.py:456
  (88 shorter events, 19.3 us)
Async XLA Ops:
  0.6 60.0 %collective-permute-start = (bf16[3,2,1536,128]{3,2,1,0:T(8,128)(2,1)}, bf16[3,2,1536,128]{3,2,1,0:T(8,128)(2,1)}, u32[]{:S(2)}, u32[]{:S(2)}) collective-permute-start(bf16[3,2,1536,128]{3,2,1,0:T(8,128)(2,1)} %bitcast.18), channel_id=1, source_target_pairs={{0,1},{1,0},{2,3},{3,2},{4,5},{5,4},{6,7},{7,6},{8,9},{9,8},{10,11... | collective-permute-start | bytes 7077896 | tf_op jit(solution)/shard_map/ppermute | solution.py:26
  5.5 54.6 %collective-permute-start.6 = (bf16[2,1536,128]{2,1,0:T(8,128)(2,1)}, bf16[2,1536,128]{2,1,0:T(8,128)(2,1)}, u32[]{:S(2)}, u32[]{:S(2)}) collective-permute-start(bf16[2,1536,128]{2,1,0:T(8,128)(2,1)} %slice_bitcast_fusion), channel_id=1, source_target_pairs={{0,2},{1,3},{2,0},{3,1},{4,6},{5,7},{6,4},{7,5},{8,10},{9,11},{10,... | collective-permute-start | bytes 2359304 | tf_op jit(solution)/shard_map/ppermute | solution.py:26
  8.0 52.6 %collective-permute-start.1 = (bf16[2,1536,128]{2,1,0:T(8,128)(2,1)}, bf16[2,1536,128]{2,1,0:T(8,128)(2,1)S(1)}, u32[]{:S(2)}, u32[]{:S(2)}) collective-permute-start(bf16[2,1536,128]{2,1,0:T(8,128)(2,1)} %slice_bitcast_fusion.1), channel_id=1, source_target_pairs={{0,2},{1,3},{2,0},{3,1},{4,6},{5,7},{6,4},{7,5},{8,10},{9,11},{10,... | collective-permute-start | bytes 2359304 | tf_op jit(solution)/shard_map/ppermute | solution.py:26
  9.0 42.9 %collective-permute-start.13 = (bf16[2,768,128]{2,1,0:T(8,128)(2,1)}, bf16[2,768,128]{2,1,0:T(8,128)(2,1)S(1)}, u32[]{:S(2)}, u32[]{:S(2)}) collective-permute-start(bf16[2,768,128]{2,1,0:T(8,128)(2,1)} %get-tuple-element.57), channel_id=1, source_target_pairs={{0,2},{1,3},{2,0},{3,1},{4,6},{5,7},{6,4},{7,5},{8,10},{9,11},{10,... | collective-permute-start | bytes 1179656 | tf_op jit(solution)/shard_map/ppermute | solution.py:26
  11.0 49.1 %collective-permute-start.11 = (bf16[2,768,128]{2,1,0:T(8,128)(2,1)}, bf16[2,768,128]{2,1,0:T(8,128)(2,1)}, u32[]{:S(2)}, u32[]{:S(2)}) collective-permute-start(bf16[2,768,128]{2,1,0:T(8,128)(2,1)} %get-tuple-element.58), channel_id=1, source_target_pairs={{0,2},{1,3},{2,0},{3,1},{4,6},{5,7},{6,4},{7,5},{8,10},{9,11},{10,... | collective-permute-start | bytes 1179656 | tf_op jit(solution)/shard_map/ppermute | solution.py:26
  51.9 57.0 %collective-permute-start.14 = (bf16[2,768,128]{2,1,0:T(8,128)(2,1)S(1)}, bf16[2,768,128]{2,1,0:T(8,128)(2,1)S(1)}, u32[]{:S(2)}, u32[]{:S(2)}) collective-permute-start(bf16[2,768,128]{2,1,0:T(8,128)(2,1)S(1)} %collective-permute-done.13.left_ref), channel_id=1, source_target_pairs={{0,1},{1,0},{2,3},{3,2},{4,5},{5,4},{6,7},{7,6},{8,9},{9,8},{10,11... | collective-permute-start | bytes 1179656 | tf_op jit(solution)/shard_map/ppermute | solution.py:26
  60.1 53.4 %collective-permute-start.12 = (bf16[2,768,128]{2,1,0:T(8,128)(2,1)}, bf16[2,768,128]{2,1,0:T(8,128)(2,1)S(1)}, u32[]{:S(2)}, u32[]{:S(2)}) collective-permute-start(bf16[2,768,128]{2,1,0:T(8,128)(2,1)} %collective-permute-done.11.left_ref), channel_id=1, source_target_pairs={{0,1},{1,0},{2,3},{3,2},{4,5},{5,4},{6,7},{7,6},{8,9},{9,8},{10,11... | collective-permute-start | bytes 1179656 | tf_op jit(solution)/shard_map/ppermute | solution.py:26
  60.1 25.7 %collective-permute-start.7 = (bf16[2,1536,128]{2,1,0:T(8,128)(2,1)}, bf16[2,1536,128]{2,1,0:T(8,128)(2,1)S(1)}, u32[]{:S(2)}, u32[]{:S(2)}) collective-permute-start(bf16[2,1536,128]{2,1,0:T(8,128)(2,1)} %collective-permute-done.6.left_ref), channel_id=1, source_target_pairs={{0,1},{1,0},{2,3},{3,2},{4,5},{5,4},{6,7},{7,6},{8,9},{9,8},{10,11... | collective-permute-start | bytes 2359304 | tf_op jit(solution)/shard_map/ppermute | solution.py:26
  60.6 39.8 %collective-permute-start.2 = (bf16[2,1536,128]{2,1,0:T(8,128)(2,1)S(1)}, bf16[2,1536,128]{2,1,0:T(8,128)(2,1)S(1)}, u32[]{:S(2)}, u32[]{:S(2)}) collective-permute-start(bf16[2,1536,128]{2,1,0:T(8,128)(2,1)S(1)} %collective-permute-done.1.left_ref), channel_id=1, source_target_pairs={{0,1},{1,0},{2,3},{3,2},{4,5},{5,4},{6,7},{7,6},{8,9},{9,8},{10,11... | collective-permute-start | bytes 2359304 | tf_op jit(solution)/shard_map/ppermute | solution.py:26
  96.5 19.9 %collective-permute-start.10 = (bf16[14,32,128]{2,1,0:T(8,128)(2,1)S(1)}, bf16[14,32,128]{2,1,0:T(8,128)(2,1)S(1)}, u32[]{:S(2)}, u32[]{:S(2)}) collective-permute-start(bf16[14,32,128]{2,1,0:T(8,128)(2,1)S(1)} %get-tuple-element.43), channel_id=1, source_target_pairs={{0,12},{4,8},{8,4},{12,0},{1,13},{5,9},{9,5},{13,1},{2,14},{6,10},... | collective-permute-start | bytes 344072 | tf_op jit(solution)/shard_map/ppermute | solution.py:26
  100.4 22.9 %collective-permute-start.8 = (bf16[14,32,128]{2,1,0:T(8,128)(2,1)S(1)}, bf16[14,32,128]{2,1,0:T(8,128)(2,1)S(1)}, u32[]{:S(2)}, u32[]{:S(2)}) collective-permute-start(bf16[14,32,128]{2,1,0:T(8,128)(2,1)S(1)} %get-tuple-element.41), channel_id=1, source_target_pairs={{0,4},{4,0},{8,12},{12,8},{1,5},{5,1},{9,13},{13,9},{2,6},{6,2},{1... | collective-permute-start | bytes 344072 | tf_op jit(solution)/shard_map/ppermute | solution.py:26
  100.4 24.0 %collective-permute-start.9 = (bf16[14,32,128]{2,1,0:T(8,128)(2,1)S(1)}, bf16[14,32,128]{2,1,0:T(8,128)(2,1)S(1)}, u32[]{:S(2)}, u32[]{:S(2)}) collective-permute-start(bf16[14,32,128]{2,1,0:T(8,128)(2,1)S(1)} %get-tuple-element.42), channel_id=1, source_target_pairs={{0,8},{4,12},{8,0},{12,4},{1,9},{5,13},{9,1},{13,5},{2,10},{6,14},... | collective-permute-start | bytes 344072 | tf_op jit(solution)/shard_map/ppermute | solution.py:26
  108.9 19.9 %collective-permute-start.3 = (f32[13,32,128]{2,1,0:T(8,128)S(1)}, f32[13,32,128]{2,1,0:T(8,128)S(1)}, u32[]{:S(2)}, u32[]{:S(2)}) collective-permute-start(f32[13,32,128]{2,1,0:T(8,128)S(1)} %get-tuple-element.36), channel_id=1, source_target_pairs={{0,4},{4,0},{8,12},{12,8},{1,5},{5,1},{9,13},{13,9},{2,6},{6,2},{1... | collective-permute-start | bytes 638984 | tf_op jit(solution)/shard_map/ppermute | solution.py:26
  113.5 21.6 %collective-permute-start.4 = (f32[13,32,128]{2,1,0:T(8,128)}, f32[13,32,128]{2,1,0:T(8,128)}, u32[]{:S(2)}, u32[]{:S(2)}) collective-permute-start(f32[13,32,128]{2,1,0:T(8,128)} %get-tuple-element.37), channel_id=1, source_target_pairs={{0,8},{4,12},{8,0},{12,4},{1,9},{5,13},{9,1},{13,5},{2,10},{6,14},... | collective-permute-start | bytes 638984 | tf_op jit(solution)/shard_map/ppermute | solution.py:26
  116.5 18.6 %collective-permute-start.5 = (f32[13,32,128]{2,1,0:T(8,128)}, f32[13,32,128]{2,1,0:T(8,128)}, u32[]{:S(2)}, u32[]{:S(2)}) collective-permute-start(f32[13,32,128]{2,1,0:T(8,128)} %get-tuple-element.38), channel_id=1, source_target_pairs={{0,12},{4,8},{8,4},{12,0},{1,13},{5,9},{9,5},{13,1},{2,14},{6,10},... | collective-permute-start | bytes 638984 | tf_op jit(solution)/shard_map/ppermute | solution.py:26
  123.9 15.9 %collective-permute-start.15 = (bf16[14,32,128]{2,1,0:T(8,128)(2,1)}, bf16[14,32,128]{2,1,0:T(8,128)(2,1)S(1)}, u32[]{:S(2)}, u32[]{:S(2)}) collective-permute-start(bf16[14,32,128]{2,1,0:T(8,128)(2,1)} %get-tuple-element.47), channel_id=1, source_target_pairs={{0,4},{4,0},{8,12},{12,8},{1,5},{5,1},{9,13},{13,9},{2,6},{6,2},{1... | collective-permute-start | bytes 344072 | tf_op jit(solution)/shard_map/ppermute | solution.py:26
  125.0 18.2 %collective-permute-start.16 = (bf16[14,32,128]{2,1,0:T(8,128)(2,1)}, bf16[14,32,128]{2,1,0:T(8,128)(2,1)S(1)}, u32[]{:S(2)}, u32[]{:S(2)}) collective-permute-start(bf16[14,32,128]{2,1,0:T(8,128)(2,1)} %get-tuple-element.48), channel_id=1, source_target_pairs={{0,8},{4,12},{8,0},{12,4},{1,9},{5,13},{9,1},{13,5},{2,10},{6,14},... | collective-permute-start | bytes 344072 | tf_op jit(solution)/shard_map/ppermute | solution.py:26
  129.5 13.7 %collective-permute-start.17 = (bf16[14,32,128]{2,1,0:T(8,128)(2,1)}, bf16[14,32,128]{2,1,0:T(8,128)(2,1)}, u32[]{:S(2)}, u32[]{:S(2)}) collective-permute-start(bf16[14,32,128]{2,1,0:T(8,128)(2,1)} %get-tuple-element.49), channel_id=1, source_target_pairs={{0,12},{4,8},{8,4},{12,0},{1,13},{5,9},{9,5},{13,1},{2,14},{6,10},... | collective-permute-start | bytes 344072 | tf_op jit(solution)/shard_map/ppermute | solution.py:26
  145.1 1.9 %collective-permute-start.18 = (bf16[9,32,128]{2,1,0:T(8,128)(2,1)S(1)}, bf16[9,32,128]{2,1,0:T(8,128)(2,1)S(1)}, u32[]{:S(2)}, u32[]{:S(2)}) collective-permute-start(bf16[9,32,128]{2,1,0:T(8,128)(2,1)S(1)} %get-tuple-element.51), channel_id=1, source_target_pairs={{0,1},{1,0},{2,3},{3,2},{4,5},{5,4},{6,7},{7,6},{8,9},{9,8},{10,11... | collective-permute-start | bytes 221192 | tf_op jit(solution)/shard_map/ppermute | solution.py:26
  145.2 4.8 %collective-permute-start.19 = (bf16[9,32,128]{2,1,0:T(8,128)(2,1)S(1)}, bf16[9,32,128]{2,1,0:T(8,128)(2,1)S(1)}, u32[]{:S(2)}, u32[]{:S(2)}) collective-permute-start(bf16[9,32,128]{2,1,0:T(8,128)(2,1)S(1)} %get-tuple-element.52), channel_id=1, source_target_pairs={{0,2},{1,3},{2,0},{3,1},{4,6},{5,7},{6,4},{7,5},{8,10},{9,11},{10,... | collective-permute-start | bytes 221192 | tf_op jit(solution)/shard_map/ppermute | solution.py:26
  146.7 4.5 %collective-permute-start.20 = (bf16[9,32,128]{2,1,0:T(8,128)(2,1)S(1)}, bf16[9,32,128]{2,1,0:T(8,128)(2,1)S(1)}, u32[]{:S(2)}, u32[]{:S(2)}) collective-permute-start(bf16[9,32,128]{2,1,0:T(8,128)(2,1)S(1)} %get-tuple-element.53), channel_id=1, source_target_pairs={{0,3},{1,2},{2,1},{3,0},{4,7},{5,6},{6,5},{7,4},{8,11},{9,10},{10,... | collective-permute-start | bytes 221192 | tf_op jit(solution)/shard_map/ppermute | solution.py:26
  151.3 8.6 %collective-permute-start.21 = (bf16[15,32,128]{2,1,0:T(8,128)(2,1)S(1)}, bf16[15,32,128]{2,1,0:T(8,128)(2,1)S(1)}, u32[]{:S(2)}, u32[]{:S(2)}) collective-permute-start(bf16[15,32,128]{2,1,0:T(8,128)(2,1)S(1)} %join.1.rest_0_), channel_id=1, source_target_pairs={{0,4},{4,0},{8,12},{12,8},{1,5},{5,1},{9,13},{13,9},{2,6},{6,2},{1... | collective-permute-start | bytes 368648 | tf_op jit(solution)/shard_map/ppermute | solution.py:26
  154.3 12.2 %collective-permute-start.22 = (bf16[15,32,128]{2,1,0:T(8,128)(2,1)S(1)}, bf16[15,32,128]{2,1,0:T(8,128)(2,1)S(1)}, u32[]{:S(2)}, u32[]{:S(2)}) collective-permute-start(bf16[15,32,128]{2,1,0:T(8,128)(2,1)S(1)} %join.1.rest_0_), channel_id=1, source_target_pairs={{0,8},{4,12},{8,0},{12,4},{1,9},{5,13},{9,1},{13,5},{2,10},{6,14},... | collective-permute-start | bytes 368648 | tf_op jit(solution)/shard_map/ppermute | solution.py:26
  155.9 10.6 %collective-permute-start.23 = (bf16[15,32,128]{2,1,0:T(8,128)(2,1)S(1)}, bf16[15,32,128]{2,1,0:T(8,128)(2,1)S(1)}, u32[]{:S(2)}, u32[]{:S(2)}) collective-permute-start(bf16[15,32,128]{2,1,0:T(8,128)(2,1)S(1)} %join.1.rest_0_), channel_id=1, source_target_pairs={{0,12},{4,8},{8,4},{12,0},{1,13},{5,9},{9,5},{13,1},{2,14},{6,10},... | collective-permute-start | bytes 368648 | tf_op jit(solution)/shard_map/ppermute | solution.py:26
  (24 other events, 298.6 us)

commit v2 on v1

v2 whole, which is shorter than its diff:
```python
import functools

import jax
import jax.numpy as jnp
from jax import lax
from jax.experimental import pallas as pl
from jax.experimental.pallas import tpu as pltpu
from jax.sharding import PartitionSpec as P


CAP = 3

exchange_coeff = (3.0 / 3.141592653589793) ** (1.0 / 3.0)
density_floor = 0.5

F32 = jnp.float32
BF16 = jnp.bfloat16
SMEM = pl.BlockSpec(memory_space=pltpu.SMEM)
VMEM = pl.BlockSpec(memory_space=pltpu.VMEM)
LIMIT = 10 * 1024 * 1024
NEAR_LIMIT = 26 * 1024 * 1024


def swap(value, axis, mask):
    size = lax.axis_size(axis)
    return lax.ppermute(value, axis, [(i, i ^ mask) for i in range(size)])


def tree_sum(values):
    while len(values) > 1:
        values = [values[i] + values[i + 1] for i in range(0, len(values) - 1, 2)] + values[len(values) // 2 * 2 :]
    return values[0]


def row_block(rows):
    for size in (512, 384, 256, 128):
        if rows % size == 0:
            return size
    return rows


def near_block(rows):
    return 384 if rows % 384 == 0 else row_block(rows)


def complex_product(g_ref, rows, start, lower):
    real, imag = lower
    columns = pl.ds(start, real.shape[0])
    first = jnp.dot(
        g_ref[0, rows, columns], jnp.concatenate([real, imag], axis=1), preferred_element_type=F32
    )
    second = jnp.dot(
        g_ref[1, rows, columns], jnp.concatenate([-imag, real], axis=1), preferred_element_type=F32
    )
    return first + second


def near_kernel(g_hbm, own_ref, partner_ref, *rest):
    acc_refs, (far_ref, near_ref, near_sem, far_sem) = rest[:-4], rest[-4:]
    length, order = g_hbm.shape[1:]
    cols = order // length
    tile = near_block(length)
    tiles = length // tile
    m = pl.program_id(0)
    me = lax.axis_index("col")
    starts = [pl.multiple_of((me ^ mask) * length, length) for mask in range(cols)]

    def near_copy(step, mask):
        rows = pl.ds(step * tile, tile)
        return pltpu.make_async_copy(
            g_hbm.at[:, rows, pl.ds(starts[mask], length)],
            near_ref.at[:, rows, pl.ds(mask * length, length)],
            near_sem.at[step, mask],
        )

    def far_copy(mask):
        return pltpu.make_async_copy(
            g_hbm.at[:, :, pl.ds(starts[mask], length)],
            far_ref.at[:, :, pl.ds((mask - 2) * length, length)],
            far_sem.at[mask - 2],
        )

    @pl.when(m == 0)
    def _():
        near_copy(0, 0).start()
        near_copy(0, 1).start()

    near_copy(m, 0).wait()

    @pl.when(m == 0)
    def _():
        for step in range(1, tiles):
            near_copy(step, 0).start()
            near_copy(step, 1).start()

    @pl.when(m == min(1, tiles - 1))
    def _():
        for mask in range(2, cols):
            far_copy(mask).start()

    near_copy(m, 1).wait()
    rows = pl.ds(pl.multiple_of(m * tile, tile), tile)
    for q, acc_ref in enumerate(acc_refs):
        acc_ref[rows] = complex_product(
            near_ref, rows, 0, (own_ref[q, 0], own_ref[q, 1])
        ) + complex_product(near_ref, rows, length, (partner_ref[q, 0], partner_ref[q, 1]))

    @pl.when(m == tiles - 1)
    def _():
        for mask in range(2, cols):
            far_copy(mask).wait()


def near_product(matrix, own, partner):
    panels, _, rows, width = own.shape
    order = matrix.shape[2]
    tile = near_block(rows)
    results = pl.pallas_call(
        near_kernel,
        grid=(rows // tile,),
        in_specs=[pl.BlockSpec(memory_space=pl.ANY), VMEM, VMEM],
        out_specs=[VMEM] * (panels + 1),
        out_shape=[pltpu.VMEM((rows, 2 * width), F32)] * panels
        + [pltpu.VMEM((2, rows, order - 2 * rows), BF16)],
        scratch_shapes=[
            pltpu.VMEM((2, rows, 2 * rows), BF16),
            pltpu.SemaphoreType.DMA((rows // tile, 2)),
            pltpu.SemaphoreType.DMA((order // rows - 2,)),
        ],
        compiler_params=pltpu.CompilerParams(vmem_limit_bytes=NEAR_LIMIT),
        cost_estimate=pl.CostEstimate(
            flops=2 * 8 * rows * rows * panels * width, bytes_accessed=4 * rows * order, transcendentals=0
        ),
        name="near_product",
    )(matrix, own, partner)
    return list(results[:-1]), results[-1]


def far_terms(g_ref, rows, step, offset, left_ref, right_ref):
    length = g_ref.shape[1]
    total = None
    for mask, ref in ((2 * step, left_ref), (2 * step + 1, right_ref)):
        term = complex_product(g_ref, rows, (mask - 2) * length + offset, (ref[0], ref[1]))
        total = term if total is None else total + term
    return total


def far_kernel(step, offset, g_ref, left_ref, right_ref, acc_ref, out_ref):
    tile = row_block(out_ref.shape[0])
    rows = pl.ds(pl.multiple_of(pl.program_id(0) * tile, tile), tile)
    out_ref[rows] = acc_ref[rows] + far_terms(g_ref, rows, step, offset, left_ref, right_ref)


def far_product(g, left, right, acc, step, offset):
    _, depth, width = left.shape
    rows = g.shape[1]
    tile = row_block(rows)
    whole = pl.BlockSpec(left.shape, lambda m: (0, 0, 0), pipeline_mode=pl.Buffered(1))
    return pl.pallas_call(
        functools.partial(far_kernel, step, offset),
        grid=(rows // tile,),
        in_specs=[
            VMEM,
            whole,
            whole,
            VMEM,
        ],
        out_specs=VMEM,
        out_shape=pltpu.VMEM(acc.shape, F32),
        compiler_params=pltpu.CompilerParams(vmem_limit_bytes=LIMIT),
        cost_estimate=pl.CostEstimate(
            flops=2 * 8 * rows * depth * width, bytes_accessed=8 * rows * width, transcendentals=0
        ),
        name="far_product",
    )(g, left, right, acc)


def last_kernel(
    poles, step, offset, g_ref, left_ref, right_ref, acc_ref, own_ref, diag_ref, weight_ref, *rest
):
    out_refs, (y_ref, d_ref) = rest[:poles], rest[poles:]
    m = pl.program_id(0)
    tile, width = own_ref.shape[1:]
    count = tile // width
    blocks = y_ref.shape[0]
    rows = pl.ds(pl.multiple_of(m * tile, tile), tile)

    weight_real = weight_ref[0, 0]
    weight_imag = weight_ref[0, 1]
    total = acc_ref[rows] + far_terms(g_ref, rows, step, offset, left_ref, right_ref)
    real = -total[:, :width]
    imag = -total[:, width:]
    density = weight_real * imag + weight_imag * real
    other = weight_real * real - weight_imag * imag
    y_ref[pl.ds(m * count, count)] = density.reshape(count, poles, width // poles, width)

    def cross(lower, value):
        high = value.astype(BF16)
        low = (value - high.astype(F32)).astype(BF16)
        both = lax.dot_general(
            lower,
            jnp.concatenate([high, low], axis=1),
            (((0,), (0,)), ((), ())),
            preferred_element_type=F32,
        )
        return both[:, :width] + both[:, width:]

    part = (cross(own_ref[0], density) + cross(own_ref[1], other)).reshape(d_ref.shape)

    @pl.when(m == 0)
    def _():
        lead = (lax.axis_index("col") == 0).astype(F32)
        term = lead * (weight_real * diag_ref[1] + weight_imag * diag_ref[0])
        d_ref[...] = term.reshape(d_ref.shape) - part

    @pl.when(m > 0)
    def _():
        d_ref[...] -= part

    @pl.when(m == pl.num_programs(0) - 1)
    def _():
        for mask, out_ref in enumerate(out_refs):
            other_pole = lax.axis_index("pole") ^ mask
            kind = out_ref.dtype
            out_ref[:blocks] = y_ref[:, other_pole].astype(kind)
            diag = d_ref[other_pole]
            high = diag.astype(kind)
            out_ref[blocks] = high
            if kind != F32:
                out_ref[blocks + 1] = (diag - high.astype(F32)).astype(kind)


def last_product(g, left, right, acc, own, diag, weights, panel, step, offset, poles, kind):
    _, depth, width = left.shape
    rows = g.shape[1]
    tile = row_block(rows)
    blocks = rows // width
    whole = pl.BlockSpec(left.shape, lambda m: (0, 0, 0), pipeline_mode=pl.Buffered(1))
    shape = (blocks + (1 if kind == F32 else 2), width // poles, width)
    return pl.pallas_call(
        functools.partial(last_kernel, poles, step, offset),
        grid=(rows // tile,),
        in_specs=[
            VMEM,
            whole,
            whole,
            VMEM,
            pl.BlockSpec((None, 2, tile, width), lambda m: (panel, 0, m, 0)),
            pl.BlockSpec((None, 2, width, width), lambda m: (panel, 0, 0, 0)),
            SMEM,
        ],
        out_specs=[pl.BlockSpec(shape, lambda m: (0, 0, 0))] * poles,
        scratch_shapes=[
            pltpu.VMEM((blocks, poles, width // poles, width), F32),
            pltpu.VMEM((poles, width // poles, width), F32),
        ],
        out_shape=[jax.ShapeDtypeStruct(shape, kind)] * poles,
        compiler_params=pltpu.CompilerParams(vmem_limit_bytes=LIMIT),
        cost_estimate=pl.CostEstimate(
            flops=2 * 8 * rows * depth * width, bytes_accessed=8 * rows * width, transcendentals=0
        ),
        name="last_product",
    )(g, left, right, acc, own, diag, weights)


def table_kernel(per_device, panels, cols, order_ref, supports_ref, counts_ref, send_ref, plan_ref):
    most, tiles = supports_ref.shape
    total = cols * per_device
    me = lax.axis_index("col")
    supports = supports_ref[...]
    counts = counts_ref[...]
    ids = lax.broadcasted_iota(jnp.int32, (total, tiles), 0)
    named = [(supports[k : k + 1] == ids) & (counts > k) for k in range(most)]
    any_named = named[0]
    for hit in named[1:]:
        any_named = any_named | hit
    tile_hits = jnp.where(any_named, 1.0, 0.0).astype(BF16)
    share = tiles // cols
    group_tile = lax.broadcasted_iota(jnp.int32, (tiles, cols), 0)
    group_col = lax.broadcasted_iota(jnp.int32, (tiles, cols), 1)
    group = (group_tile >= group_col * share) & (group_tile < (group_col + 1) * share)
    needed = jnp.minimum(
        jnp.dot(tile_hits, jnp.where(group, 1.0, 0.0).astype(BF16), preferred_element_type=F32), 1.0
    )
    first = lax.broadcasted_iota(jnp.int32, (total, total), 0)
    second = lax.broadcasted_iota(jnp.int32, (total, total), 1)
    earlier = (second <= first) & (first // per_device == second // per_device)
    rank = jnp.dot(
        jnp.where(earlier, 1.0, 0.0).astype(BF16), needed.astype(BF16), preferred_element_type=F32
    )
    block = lax.broadcasted_iota(jnp.int32, (total, cols), 0)
    dest = lax.broadcasted_iota(jnp.int32, (total, cols), 1)
    owner = block // per_device
    local = block - owner * per_device
    row = local // panels
    spot = local - row * panels
    panel = jnp.zeros_like(spot)
    for j in range(panels):
        panel = jnp.where(spot == j, order_ref[j], panel)
    code = (panel * (per_device // panels) + row).astype(F32)
    mine = (needed > 0.5) & (owner == me)
    for c in range(CAP):
        value = jnp.sum(jnp.where(mine & (rank == c + 1.0), code, 0.0), axis=0, keepdims=True)
        send_ref[c : c + 1] = value.astype(jnp.int32)
    lane = lax.broadcasted_iota(jnp.int32, (1, cols), 1)
    order = jnp.zeros((1, cols), jnp.int32)
    for j in range(panels):
        order = jnp.where(lane == j, order_ref[j], order)
    send_ref[CAP : CAP + 1] = order
    mask = (owner ^ me).astype(F32)
    spots = jnp.where((needed > 0.5) & (dest == me), mask * CAP + jnp.minimum(rank, CAP) - 1.0, 0.0)
    spots = jnp.sum(spots, axis=1, keepdims=True)
    for k, hit in enumerate(named):
        slot = jnp.sum(jnp.where(hit, spots, 0.0), axis=0, keepdims=True)
        plan_ref[k : k + 1] = slot.astype(jnp.int32)
    plan_ref[most : 2 * most] = lax.rem(supports, panels)
    plan_ref[2 * most : 2 * most + 1] = counts


def tables(supports, counts, order, cols, per_device, panels):
    tiles, most = supports.shape
    return pl.pallas_call(
        functools.partial(table_kernel, per_device, panels, cols),
        in_specs=[SMEM, VMEM, VMEM],
        out_specs=[VMEM] * 2,
        out_shape=[
            jax.ShapeDtypeStruct((CAP + 1, cols), jnp.int32),
            jax.ShapeDtypeStruct((2 * most + 1, tiles), jnp.int32),
        ],
        compiler_params=pltpu.CompilerParams(vmem_limit_bytes=LIMIT),
        cost_estimate=pl.CostEstimate(flops=1 << 20, bytes_accessed=1 << 20, transcendentals=0),
        name="tables",
    )(order, supports.T, counts.reshape(1, tiles))


def total_of(parts, blocks):
    density = tree_sum([part[:blocks].astype(F32) for part in parts])
    diag = [part[blocks].astype(F32) for part in parts]
    if parts[0].dtype != F32:
        diag = [high + part[blocks + 1].astype(F32) for high, part in zip(diag, parts)]
    return density.astype(BF16), tree_sum(diag)


def settle_kernel(poles, blocks, *refs):
    density_ref, diag_ref = refs[-2:]
    for q in range(diag_ref.shape[0]):
        density, diag = total_of(refs[q * poles : (q + 1) * poles], blocks)
        density_ref[q * blocks : (q + 1) * blocks] = density
        diag_ref[q] = diag


def settle(groups, blocks):
    poles = len(groups[0])
    depth, width = groups[0][0].shape[1:]
    return pl.pallas_call(
        functools.partial(settle_kernel, poles, blocks),
        in_specs=[VMEM] * (poles * len(groups)),
        out_specs=[VMEM] * 2,
        out_shape=[
            jax.ShapeDtypeStruct((len(groups) * blocks, depth, width), BF16),
            jax.ShapeDtypeStruct((len(groups), depth, width), F32),
        ],
        compiler_params=pltpu.CompilerParams(vmem_limit_bytes=LIMIT),
        cost_estimate=pl.CostEstimate(flops=1 << 20, bytes_accessed=2 << 20, transcendentals=0),
        name="settle",
    )(*[part for group in groups for part in group])


def pick_kernel(poles, blocks, send_ref, early_ref, early_diag_ref, *rest):
    parts, out_refs, (all_ref, diag_ref) = rest[:poles], rest[poles:-2], rest[-2:]
    early = early_ref.shape[0]
    panels = diag_ref.shape[0]
    me = lax.axis_index("col")
    all_ref[:early] = early_ref[...]
    density, last_diag = total_of(parts, blocks)
    all_ref[early:] = density
    diag_ref[: panels - 1] = early_diag_ref[...]
    diag_ref[panels - 1] = last_diag
    for mask, out_ref in enumerate(out_refs):
        for c in range(CAP):
            out_ref[c] = all_ref[send_ref[c, me ^ mask]]
    for j in range(panels):
        diag = diag_ref[send_ref[CAP, j]]
        high = diag.astype(BF16)
        low = (diag - high.astype(F32)).astype(BF16)
        for out_ref in out_refs:
            out_ref[CAP + 2 * j] = high
            out_ref[CAP + 2 * j + 1] = low


def pick(send, early, early_diag, parts, blocks, cols):
    poles = len(parts)
    depth, width = early.shape[1:]
    panels = early_diag.shape[0] + 1
    shape = (CAP + 2 * panels, depth, width)
    return pl.pallas_call(
        functools.partial(pick_kernel, poles, blocks),
        in_specs=[SMEM] + [VMEM] * (2 + poles),
        out_specs=[VMEM] * cols,
        out_shape=[jax.ShapeDtypeStruct(shape, BF16)] * cols,
        scratch_shapes=[
            pltpu.VMEM((early.shape[0] + blocks, depth, width), BF16),
            pltpu.VMEM((panels, depth, width), F32),
        ],
        compiler_params=pltpu.CompilerParams(vmem_limit_bytes=LIMIT),
        name="pick",
    )(send, early, early_diag, *parts)


def join_kernel(*refs):
    parts, out_ref = refs[:-1], refs[-1]
    for mask, part in enumerate(parts):
        for c in range(CAP):
            out_ref[mask * CAP + c] = part[c]
    for q in range(out_ref.shape[0] - len(parts) * CAP):
        place = CAP + 2 * q
        total = tree_sum([part[place].astype(F32) + part[place + 1].astype(F32) for part in parts])
        out_ref[len(parts) * CAP + q] = total.astype(BF16)


def join(parts):
    depth, width = parts[0].shape[1:]
    extra = (parts[0].shape[0] - CAP) // 2
    return pl.pallas_call(
        join_kernel,
        in_specs=[VMEM] * len(parts),
        out_specs=VMEM,
        out_shape=jax.ShapeDtypeStruct((len(parts) * CAP + extra, depth, width), BF16),
        compiler_params=pltpu.CompilerParams(vmem_limit_bytes=LIMIT),
        name="join",
    )(*parts)


def tile_kernel(plan_ref, row_ref, orbital_ref, core_hbm, *rest):
    parts = rest[:-6]
    valence_ref, potential_ref, diag_ref, blocks_ref, core_ref, core_sem = rest[-6:]
    tiles, most = row_ref.shape[:2]
    slots, poles, depth, width = blocks_ref.shape
    panels = diag_ref.shape[0]
    first = lax.axis_index("col") * tiles
    core_copy = pltpu.make_async_copy(core_hbm, core_ref, core_sem)
    core_copy.start()

    for mask, part in enumerate(parts):
        owner = lax.axis_index("pole") ^ mask
        blocks_ref[:, owner] = part[:slots]
        for j in range(panels):
            diag_ref[j, owner] = part[slots + j].astype(F32)

    def one(t, _):
        valence = jnp.zeros((1, row_ref.shape[-1]), F32)
        for k in range(most):
            mixed = jnp.dot(
                blocks_ref[plan_ref[k, first + t]].reshape(poles * depth, width),
                orbital_ref[t, plan_ref[most + k, first + t]],
                preferred_element_type=F32,
            )
            term = jnp.sum(row_ref[t, k].astype(F32) * mixed, axis=0, keepdims=True)
            valence = valence + jnp.where(k < plan_ref[2 * most, first + t], term, 0.0)
        valence_ref[pl.ds(t, 1)] = valence
        return 0

    lax.fori_loop(0, tiles, one, 0, unroll=True)
    core_copy.wait()
    clamped = jnp.maximum(core_ref[...] + valence_ref[...], density_floor)
    potential_ref[...] = -exchange_coeff * clamped ** (1.0 / 3.0)


def tile_stage(plan, rows, orbitals, core, parts, cols):
    _, _, width, _ = rows.shape
    panels = orbitals.shape[1]
    slots = cols * CAP
    poles = len(parts)
    depth = width // poles
    valence, potential, diag = pl.pallas_call(
        tile_kernel,
        in_specs=[SMEM, VMEM, VMEM, pl.BlockSpec(memory_space=pl.ANY)] + [VMEM] * poles,
        out_specs=[VMEM] * 3,
        out_shape=[
            jax.ShapeDtypeStruct(core.shape, F32),
            jax.ShapeDtypeStruct(core.shape, F32),
            jax.ShapeDtypeStruct((panels, poles, depth, width), F32),
        ],
        scratch_shapes=[
            pltpu.VMEM((slots, poles, depth, width), BF16),
            pltpu.VMEM(core.shape, F32),
            pltpu.SemaphoreType.DMA(()),
        ],
        compiler_params=pltpu.CompilerParams(vmem_limit_bytes=LIMIT),
        name="tile_stage",
    )(plan, rows, orbitals, core, *parts)
    return valence, potential, diag.reshape(panels, width, width)


def body(
    inverse,
    panels,
    diag_inverse,
    pole_weights,
    supports,
    counts,
    panel_order,
    row_orbitals,
    panel_orbitals,
    core_density,
):
    cols = lax.axis_size("col")
    poles = lax.axis_size("pole")
    matrix = inverse[0]
    own = panels[0]
    diag = diag_inverse[0]
    panel_count, _, rows, width = own.shape
    blocks = rows // width
    per_device = blocks * panel_count
    steps = range(1, cols // 2)

    pieces = []
    for q in range(panel_count):
        parts = 2 if q == panel_count - 1 else 1
        pieces += [(q, part * (rows // parts), rows // parts) for part in range(parts)]

    partner = swap(own, "col", 1)
    remote = {}
    for piece, (q, offset, depth) in enumerate(pieces):
        for step in steps:
            remote[step, piece] = swap(own[q, :, offset : offset + depth], "col", 2 * step)
    forward = {}
    for (step, piece), value in remote.items():
        forward[step, piece] = swap(value, "col", 1)

    send, plan = tables(supports, counts, panel_order, cols, per_device, panel_count)
    acc, staged = near_product(matrix, own, partner)
    sums = []
    for piece, (q, offset, depth) in enumerate(pieces):
        for step in steps:
            left, right = remote[step, piece], forward[step, piece]
            if step < cols // 2 - 1 or offset + depth < rows:
                acc[q] = far_product(staged, left, right, acc[q], step, offset)
                continue
            kind = F32 if q == 0 else BF16
            parts = last_product(
                staged, left, right, acc[q], own, diag, pole_weights, q, step, offset, poles, kind
            )
            group = [parts[0]]
            for mask in range(1, poles):
                group.append(swap(parts[mask], "pole", mask))
            sums.append(group)

    early, early_diag = settle(sums[:-1], blocks)
    messages = pick(send, early, early_diag, sums[-1], blocks, cols)
    arrived = [messages[0]] + [swap(messages[mask], "col", mask) for mask in range(1, cols)]
    joined = join(arrived)
    gathered = [joined]
    for mask in range(1, poles):
        gathered.append(swap(joined, "pole", mask))
    return tile_stage(plan, row_orbitals, panel_orbitals, core_density, gathered, cols)


def solution(mesh):
    placed = (
        P(("job", "pole"), None, "col", None),
        P(("job", "pole"), None, None, "col", None),
        P(("job", "pole"), None, None, None, None),
        P(("job", "pole"), None),
        P(),
        P(),
        P(),
        P(("job", "col"), None, None, "pole"),
        P(("job", "col"), None, None, "pole"),
        P(("job", "col"), "pole"),
    )
    return jax.shard_map(
        body,
        mesh=mesh,
        in_specs=placed,
        out_specs=(P(("job", "col"), "pole"), P(("job", "col"), "pole"), P("job", None, None)),
        check_vma=False,
    )
```

time: 170 us -> 153 us (0.900)
  local copies, waits for them, and re-layouts: 15.6 us -> 1.7 us
  Pallas kernels: 55.7 us -> 44 us
  waiting for transfers between devices: 69.9 us -> 79.6 us
    unnamed x49 -> x18, local copies, waits for them, and re-layouts: 10.2 us -> 0.04 us
    ppermute x24, waiting for transfers between devices: 69.9 us -> 79.6 us  [swap(): return lax.ppermute(value, axis, [(i, i ^ mask) for i in range(size)])]
    pallas_call x3, Pallas kernels: 28.8 us -> 21.4 us  [the longest x1 18 us: near_product(): pl.pallas_call(near_kernel, grid=(rows // tile,), in_specs=[pl.BlockSpec(...]
    squeeze x3 -> x2, local copies, waits for them, and re-layouts: 5.23 us -> 1.67 us  [body(): own[q, :, offset:offset + depth]]
    pallas_call x3, Pallas kernels: 21.7 us -> 18.8 us  [last_product(): pl.pallas_call(functools.partial(last_kernel, poles, step, offset), grid=...]
  transfers between devices with their start and end apart: 24 -> 24, of which waited for: 8 -> 8; matrix products, arithmetic and copies ran while one was open for 3% -> 1% of each run, Pallas kernels for 31% -> 27%
where the time goes in v2:
time: 153 us; the launch traced here: 152 us
  waiting for transfers between devices  79.6 us (52%)
  Pallas kernels  44 us (29%)
  starting transfers between devices  26.2 us (17%)
  local copies, waits for them, and re-layouts  1.7 us (1%)
    ppermute x24, waiting for transfers between devices, swap(): return lax.ppermute(value, axis, [(i, i ^ mask) for i in range(size)])  79.6 us
    ppermute x24, starting transfers between devices, swap(): return lax.ppermute(value, axis, [(i, i ^ mask) for i in range(size)])  26.2 us
    pallas_call x3, Pallas kernels, last_product(): pl.pallas_call(functools.partial(last_kernel, poles, step, offset), grid=...  18.8 us
    pallas_call x1, Pallas kernels, near_product(): pl.pallas_call(near_kernel, grid=(rows // tile,), in_specs=[pl.BlockSpec(...  18 us
  transfers between devices with their start and end apart: 24, of which 8 were waited for; matrix products, arithmetic and copies ran while one was open for 1% of the time, Pallas kernels for 27%

profile of v2, /device:TPU:0, one launch (start us, length us, event | category | flops | bytes accessed | tf_op | source)
XLA Modules:
  0.0 152.4 jit_solution(11429195679070413999)
XLA Ops:
  1.2 1.6 %slice_bitcast_fusion = (bf16[2,1536,128]{2,1,0:T(8,128)(2,1)S(1)}, bf16[2,1536,128]{2,1,0:T(8,128)(2,1)S(1)}) fusion(bf16[1,3,2,1536,128]{4,3,2,1,0:T(8,128)(2,1)} %param.11), kind=kLoop, calls=%fused_computation | loop fusion | bytes 3145728 | tf_op jit(solution)/shard_map/squeeze | solution.py:526
  2.8 2.6 %collective-permute-start.6 = (bf16[2,1536,128]{2,1,0:T(8,128)(2,1)S(1)}, bf16[2,1536,128]{2,1,0:T(8,128)(2,1)S(1)}, u32[]{:S(2)}, u32[]{:S(2)}) collective-permute-start(bf16[2,1536,128]{2,1,0:T(8,128)(2,1)S(1)} %get-tuple-element.59), channel_id=1, source_target_pairs={{0,2},{1,3},{2,0},{3,1},{4,6},{5,7},{6,4},{7,5},{8,10},{9,11},{10,... | collective-permute-start | bytes 2359304 | tf_op jit(solution)/shard_map/ppermute | solution.py:26
  5.5 2.0 %collective-permute-start.13 = (bf16[2,768,128]{2,1,0:T(8,128)(2,1)S(1)}, bf16[2,768,128]{2,1,0:T(8,128)(2,1)S(1)}, u32[]{:S(2)}, u32[]{:S(2)}) collective-permute-start(bf16[2,768,128]{2,1,0:T(8,128)(2,1)S(1)} %get-tuple-element.57), channel_id=1, source_target_pairs={{0,2},{1,3},{2,0},{3,1},{4,6},{5,7},{6,4},{7,5},{8,10},{9,11},{10,... | collective-permute-start | bytes 1179656 | tf_op jit(solution)/shard_map/ppermute | solution.py:26
  7.6 41.4 %collective-permute-done.13.left_ref = bf16[2,768,128]{2,1,0:T(8,128)(2,1)S(1)} collective-permute-done((bf16[2,768,128]{2,1,0:T(8,128)(2,1)S(1)}, bf16[2,768,128]{2,1,0:T(8,128)(2,1)S(1)}, u32[]{:S(2)}, u32[]{:S(2)}) %collective-permute-start.13) | collective-permute-done | bytes 393248 | tf_op jit(solution)/shard_map/ppermute | solution.py:26
  49.1 8.1 %collective-permute-done.11.left_ref = bf16[2,768,128]{2,1,0:T(8,128)(2,1)S(1)} collective-permute-done((bf16[2,768,128]{2,1,0:T(8,128)(2,1)S(1)}, bf16[2,768,128]{2,1,0:T(8,128)(2,1)S(1)}, u32[]{:S(2)}, u32[]{:S(2)}) %collective-permute-start.11) | collective-permute-done | bytes 393248 | tf_op jit(solution)/shard_map/ppermute | solution.py:26
  57.7 18.0 %near_product.1 = (f32[1536,256]{1,0:T(8,128)S(1)}, f32[1536,256]{1,0:T(8,128)S(1)}, f32[1536,256]{1,0:T(8,128)S(1)}, bf16[2,1536,3072]{2,1,0:T(8,128)(2,1)S(1)}) custom-call(bf16[2,1536,6144]{2,1,0:T(8,128)(2,1)} %bitcast.25, bf16[3,2,1536,128]{3,2,1,0:T(8,128)(2,1)S(1)} %bitcast.16, bf16[3,2,1536,128]{3,2,1,0:T(8,128)(2,1)S(1)} %collective-permute-done.partner_ref), custom_call_target="tpu_custom_call" | custom-call | flops 14495514624 | bytes 37748736 | tf_op jit(solution)/shard_map/near_product/pallas_call | solution.py:118
  75.7 7.1 %last_product.4 = (bf16[14,32,128]{2,1,0:T(8,128)(2,1)S(1)}, bf16[14,32,128]{2,1,0:T(8,128)(2,1)S(1)}, bf16[14,32,128]{2,1,0:T(8,128)(2,1)S(1)}, bf16[14,32,128]{2,1,0:T(8,128)(2,1)S(1)}) custom-call(bf16[2,1536,3072]{2,1,0:T(8,128)(2,1)S(1)} %get-tuple-element.32.g_ref, bf16[2,1536,128]{2,1,0:T(8,128)(2,1)S(1)} %collective-permute-done.6.left_ref, ...), custom_call_target="tpu_custom_call" | custom-call | flops 4831838208 | bytes 1572864 | tf_op jit(solution)/shard_map/last_product/pallas_call | solution.py:240
  82.8 3.9 %collective-permute-start.10 = (bf16[14,32,128]{2,1,0:T(8,128)(2,1)S(1)}, bf16[14,32,128]{2,1,0:T(8,128)(2,1)S(1)}, u32[]{:S(2)}, u32[]{:S(2)}) collective-permute-start(bf16[14,32,128]{2,1,0:T(8,128)(2,1)S(1)} %get-tuple-element.42), channel_id=1, source_target_pairs={{0,12},{4,8},{8,4},{12,0},{1,13},{5,9},{9,5},{13,1},{2,14},{6,10},... | collective-permute-start | bytes 344072 | tf_op jit(solution)/shard_map/ppermute | solution.py:26
  87.4 7.0 %last_product.3 = (f32[13,32,128]{2,1,0:T(8,128)S(1)}, f32[13,32,128]{2,1,0:T(8,128)S(1)}, f32[13,32,128]{2,1,0:T(8,128)S(1)}, f32[13,32,128]{2,1,0:T(8,128)S(1)}) custom-call(bf16[2,1536,3072]{2,1,0:T(8,128)(2,1)S(1)} %get-tuple-element.32.g_ref, bf16[2,1536,128]{2,1,0:T(8,128)(2,1)S(1)} %collective-permute-done.1.left_ref, ...), custom_call_target="tpu_custom_call" | custom-call | flops 4831838208 | bytes 1572864 | tf_op jit(solution)/shard_map/last_product/pallas_call | solution.py:240
  94.5 1.5 collective-permute-start.3
  95.9 3.0 %far_product.1.acc_ref = f32[1536,256]{1,0:T(8,128)S(1)} custom-call(bf16[2,1536,3072]{2,1,0:T(8,128)(2,1)S(1)} %get-tuple-element.32.g_ref, bf16[2,768,128]{2,1,0:T(8,128)(2,1)S(1)} %collective-permute-done.13.left_ref, bf16[2,768,128]{2,1,0:T(8,128)(2,1)S(1)} %collective-permute-done.14.right_ref, f32[1536,256]{1,0:T(8,128)S(1)} %get-tuple-element.45.acc_ref), custom_call_target="tpu_custom_call" | custom-call | flops 2415919104 | bytes 1572864 | tf_op jit(solution)/shard_map/far_product/pallas_call | solution.py:159
  99.0 3.0 %collective-permute-start.4 = (f32[13,32,128]{2,1,0:T(8,128)S(1)}, f32[13,32,128]{2,1,0:T(8,128)S(1)}, u32[]{:S(2)}, u32[]{:S(2)}) collective-permute-start(f32[13,32,128]{2,1,0:T(8,128)S(1)} %get-tuple-element.36), channel_id=1, source_target_pairs={{0,8},{4,12},{8,0},{12,4},{1,9},{5,13},{9,1},{13,5},{2,10},{6,14},... | collective-permute-start | bytes 638984 | tf_op jit(solution)/shard_map/ppermute | solution.py:26
  102.1 4.6 %last_product.5 = (bf16[14,32,128]{2,1,0:T(8,128)(2,1)S(1)}, bf16[14,32,128]{2,1,0:T(8,128)(2,1)S(1)}, bf16[14,32,128]{2,1,0:T(8,128)(2,1)S(1)}, bf16[14,32,128]{2,1,0:T(8,128)(2,1)S(1)}) custom-call(bf16[2,1536,3072]{2,1,0:T(8,128)(2,1)S(1)} %get-tuple-element.32.g_ref, bf16[2,768,128]{2,1,0:T(8,128)(2,1)S(1)} %collective-permute-done.11.left_ref, ...), custom_call_target="tpu_custom_call" | custom-call | flops 2415919104 | bytes 1572864 | tf_op jit(solution)/shard_map/last_product/pallas_call | solution.py:240
  107.4 3.8 %collective-permute-start.16 = (bf16[14,32,128]{2,1,0:T(8,128)(2,1)S(1)}, bf16[14,32,128]{2,1,0:T(8,128)(2,1)S(1)}, u32[]{:S(2)}, u32[]{:S(2)}) collective-permute-start(bf16[14,32,128]{2,1,0:T(8,128)(2,1)S(1)} %get-tuple-element.48), channel_id=1, source_target_pairs={{0,8},{4,12},{8,0},{12,4},{1,9},{5,13},{9,1},{13,5},{2,10},{6,14},... | collective-permute-start | bytes 344072 | tf_op jit(solution)/shard_map/ppermute | solution.py:26
  112.4 9.1 %collective-permute-done.4.refs_2_ = f32[13,32,128]{2,1,0:T(8,128)S(1)} collective-permute-done((f32[13,32,128]{2,1,0:T(8,128)S(1)}, f32[13,32,128]{2,1,0:T(8,128)S(1)}, u32[]{:S(2)}, u32[]{:S(2)}) %collective-permute-start.4) | collective-permute-done | bytes 213024 | tf_op jit(solution)/shard_map/ppermute | solution.py:26
  121.6 6.9 %collective-permute-done.16.rest_2_ = bf16[14,32,128]{2,1,0:T(8,128)(2,1)S(1)} collective-permute-done((bf16[14,32,128]{2,1,0:T(8,128)(2,1)S(1)}, bf16[14,32,128]{2,1,0:T(8,128)(2,1)S(1)}, u32[]{:S(2)}, u32[]{:S(2)}) %collective-permute-start.16) | collective-permute-done | bytes 114720 | tf_op jit(solution)/shard_map/ppermute | solution.py:26
  129.3 1.6 %collective-permute-start.19 = (bf16[9,32,128]{2,1,0:T(8,128)(2,1)S(1)}, bf16[9,32,128]{2,1,0:T(8,128)(2,1)S(1)}, u32[]{:S(2)}, u32[]{:S(2)}) collective-permute-start(bf16[9,32,128]{2,1,0:T(8,128)(2,1)S(1)} %get-tuple-element.52), channel_id=1, source_target_pairs={{0,2},{1,3},{2,0},{3,1},{4,6},{5,7},{6,4},{7,5},{8,10},{9,11},{10,... | collective-permute-start | bytes 221192 | tf_op jit(solution)/shard_map/ppermute | solution.py:26
  131.1 2.9 %collective-permute-done.19.refs_2_ = bf16[9,32,128]{2,1,0:T(8,128)(2,1)S(1)} collective-permute-done((bf16[9,32,128]{2,1,0:T(8,128)(2,1)S(1)}, bf16[9,32,128]{2,1,0:T(8,128)(2,1)S(1)}, u32[]{:S(2)}, u32[]{:S(2)}) %collective-permute-start.19) | collective-permute-done | bytes 73760 | tf_op jit(solution)/shard_map/ppermute | solution.py:26
  134.1 1.2 collective-permute-done.20.refs_3_
  135.4 2.4 %collective-permute-start.21 = (bf16[15,32,128]{2,1,0:T(8,128)(2,1)S(1)}, bf16[15,32,128]{2,1,0:T(8,128)(2,1)S(1)}, u32[]{:S(2)}, u32[]{:S(2)}) collective-permute-start(bf16[15,32,128]{2,1,0:T(8,128)(2,1)S(1)} %join.1.rest_0_), channel_id=1, source_target_pairs={{0,4},{4,0},{8,12},{12,8},{1,5},{5,1},{9,13},{13,9},{2,6},{6,2},{1... | collective-permute-start | bytes 368648 | tf_op jit(solution)/shard_map/ppermute | solution.py:26
  138.9 1.3 collective-permute-start.23
  140.2 2.8 %collective-permute-done.21.rest_1_ = bf16[15,32,128]{2,1,0:T(8,128)(2,1)S(1)} collective-permute-done((bf16[15,32,128]{2,1,0:T(8,128)(2,1)S(1)}, bf16[15,32,128]{2,1,0:T(8,128)(2,1)S(1)}, u32[]{:S(2)}, u32[]{:S(2)}) %collective-permute-start.21) | collective-permute-done | bytes 122912 | tf_op jit(solution)/shard_map/ppermute | solution.py:26
  142.9 7.2 %collective-permute-done.22.rest_2_ = bf16[15,32,128]{2,1,0:T(8,128)(2,1)S(1)} collective-permute-done((bf16[15,32,128]{2,1,0:T(8,128)(2,1)S(1)}, bf16[15,32,128]{2,1,0:T(8,128)(2,1)S(1)}, u32[]{:S(2)}, u32[]{:S(2)}) %collective-permute-start.22) | collective-permute-done | bytes 122912 | tf_op jit(solution)/shard_map/ppermute | solution.py:26
  150.1 2.2 %tile_stage.1 = (f32[8,128]{1,0:T(8,128)}, f32[8,128]{1,0:T(8,128)}, f32[3,4,32,128]{3,2,1,0:T(8,128)}) custom-call(s32[17,32]{1,0:T(8,128)S(1)} %get-tuple-element.30.plan_ref, bf16[8,8,128,128]{3,2,1,0:T(8,128)(2,1)S(1)} %copy-done.2, bf16[8,3,128,128]{3,2,1,0:T(8,128)(2,1)S(1)} %copy-done.3, f32[8,128]{1,0:T(8,128)S(1)} %copy-done.5, ...), custom_call_target="tpu_custom_call" | custom-call | tf_op jit(solution)/shard_map/tile_stage/pallas_call | solution.py:475
  (54 shorter events, 6.4 us)
Async XLA Ops:
  0.6 57.1 %collective-permute-start = (bf16[3,2,1536,128]{3,2,1,0:T(8,128)(2,1)}, bf16[3,2,1536,128]{3,2,1,0:T(8,128)(2,1)S(1)}, u32[]{:S(2)}, u32[]{:S(2)}) collective-permute-start(bf16[3,2,1536,128]{3,2,1,0:T(8,128)(2,1)} %bitcast.14), channel_id=1, source_target_pairs={{0,1},{1,0},{2,3},{3,2},{4,5},{5,4},{6,7},{7,6},{8,9},{9,8},{10,11... | collective-permute-start | bytes 7077896 | tf_op jit(solution)/shard_map/ppermute | solution.py:26
  2.8 54.3 %collective-permute-start.6 = (bf16[2,1536,128]{2,1,0:T(8,128)(2,1)S(1)}, bf16[2,1536,128]{2,1,0:T(8,128)(2,1)S(1)}, u32[]{:S(2)}, u32[]{:S(2)}) collective-permute-start(bf16[2,1536,128]{2,1,0:T(8,128)(2,1)S(1)} %get-tuple-element.59), channel_id=1, source_target_pairs={{0,2},{1,3},{2,0},{3,1},{4,6},{5,7},{6,4},{7,5},{8,10},{9,11},{10,... | collective-permute-start | bytes 2359304 | tf_op jit(solution)/shard_map/ppermute | solution.py:26
  5.4 52.3 %collective-permute-start.1 = (bf16[2,1536,128]{2,1,0:T(8,128)(2,1)S(1)}, bf16[2,1536,128]{2,1,0:T(8,128)(2,1)S(1)}, u32[]{:S(2)}, u32[]{:S(2)}) collective-permute-start(bf16[2,1536,128]{2,1,0:T(8,128)(2,1)S(1)} %get-tuple-element.60), channel_id=1, source_target_pairs={{0,2},{1,3},{2,0},{3,1},{4,6},{5,7},{6,4},{7,5},{8,10},{9,11},{10,... | collective-permute-start | bytes 2359304 | tf_op jit(solution)/shard_map/ppermute | solution.py:26
  5.5 43.5 %collective-permute-start.13 = (bf16[2,768,128]{2,1,0:T(8,128)(2,1)S(1)}, bf16[2,768,128]{2,1,0:T(8,128)(2,1)S(1)}, u32[]{:S(2)}, u32[]{:S(2)}) collective-permute-start(bf16[2,768,128]{2,1,0:T(8,128)(2,1)S(1)} %get-tuple-element.57), channel_id=1, source_target_pairs={{0,2},{1,3},{2,0},{3,1},{4,6},{5,7},{6,4},{7,5},{8,10},{9,11},{10,... | collective-permute-start | bytes 1179656 | tf_op jit(solution)/shard_map/ppermute | solution.py:26
  7.5 49.6 %collective-permute-start.11 = (bf16[2,768,128]{2,1,0:T(8,128)(2,1)S(1)}, bf16[2,768,128]{2,1,0:T(8,128)(2,1)S(1)}, u32[]{:S(2)}, u32[]{:S(2)}) collective-permute-start(bf16[2,768,128]{2,1,0:T(8,128)(2,1)S(1)} %get-tuple-element.58), channel_id=1, source_target_pairs={{0,2},{1,3},{2,0},{3,1},{4,6},{5,7},{6,4},{7,5},{8,10},{9,11},{10,... | collective-permute-start | bytes 1179656 | tf_op jit(solution)/shard_map/ppermute | solution.py:26
  49.0 45.4 %collective-permute-start.14 = (bf16[2,768,128]{2,1,0:T(8,128)(2,1)S(1)}, bf16[2,768,128]{2,1,0:T(8,128)(2,1)S(1)}, u32[]{:S(2)}, u32[]{:S(2)}) collective-permute-start(bf16[2,768,128]{2,1,0:T(8,128)(2,1)S(1)} %collective-permute-done.13.left_ref), channel_id=1, source_target_pairs={{0,1},{1,0},{2,3},{3,2},{4,5},{5,4},{6,7},{7,6},{8,9},{9,8},{10,11... | collective-permute-start | bytes 1179656 | tf_op jit(solution)/shard_map/ppermute | solution.py:26
  57.1 41.8 %collective-permute-start.12 = (bf16[2,768,128]{2,1,0:T(8,128)(2,1)S(1)}, bf16[2,768,128]{2,1,0:T(8,128)(2,1)S(1)}, u32[]{:S(2)}, u32[]{:S(2)}) collective-permute-start(bf16[2,768,128]{2,1,0:T(8,128)(2,1)S(1)} %collective-permute-done.11.left_ref), channel_id=1, source_target_pairs={{0,1},{1,0},{2,3},{3,2},{4,5},{5,4},{6,7},{7,6},{8,9},{9,8},{10,11... | collective-permute-start | bytes 1179656 | tf_op jit(solution)/shard_map/ppermute | solution.py:26
  57.1 18.6 %collective-permute-start.7 = (bf16[2,1536,128]{2,1,0:T(8,128)(2,1)S(1)}, bf16[2,1536,128]{2,1,0:T(8,128)(2,1)S(1)}, u32[]{:S(2)}, u32[]{:S(2)}) collective-permute-start(bf16[2,1536,128]{2,1,0:T(8,128)(2,1)S(1)} %collective-permute-done.6.left_ref), channel_id=1, source_target_pairs={{0,1},{1,0},{2,3},{3,2},{4,5},{5,4},{6,7},{7,6},{8,9},{9,8},{10,11... | collective-permute-start | bytes 2359304 | tf_op jit(solution)/shard_map/ppermute | solution.py:26
  57.7 29.1 %collective-permute-start.2 = (bf16[2,1536,128]{2,1,0:T(8,128)(2,1)S(1)}, bf16[2,1536,128]{2,1,0:T(8,128)(2,1)S(1)}, u32[]{:S(2)}, u32[]{:S(2)}) collective-permute-start(bf16[2,1536,128]{2,1,0:T(8,128)(2,1)S(1)} %collective-permute-done.1.left_ref), channel_id=1, source_target_pairs={{0,1},{1,0},{2,3},{3,2},{4,5},{5,4},{6,7},{7,6},{8,9},{9,8},{10,11... | collective-permute-start | bytes 2359304 | tf_op jit(solution)/shard_map/ppermute | solution.py:26
  82.8 19.1 %collective-permute-start.10 = (bf16[14,32,128]{2,1,0:T(8,128)(2,1)S(1)}, bf16[14,32,128]{2,1,0:T(8,128)(2,1)S(1)}, u32[]{:S(2)}, u32[]{:S(2)}) collective-permute-start(bf16[14,32,128]{2,1,0:T(8,128)(2,1)S(1)} %get-tuple-element.42), channel_id=1, source_target_pairs={{0,12},{4,8},{8,4},{12,0},{1,13},{5,9},{9,5},{13,1},{2,14},{6,10},... | collective-permute-start | bytes 344072 | tf_op jit(solution)/shard_map/ppermute | solution.py:26
  86.8 20.0 %collective-permute-start.8 = (bf16[14,32,128]{2,1,0:T(8,128)(2,1)S(1)}, bf16[14,32,128]{2,1,0:T(8,128)(2,1)S(1)}, u32[]{:S(2)}, u32[]{:S(2)}) collective-permute-start(bf16[14,32,128]{2,1,0:T(8,128)(2,1)S(1)} %get-tuple-element.40), channel_id=1, source_target_pairs={{0,4},{4,0},{8,12},{12,8},{1,5},{5,1},{9,13},{13,9},{2,6},{6,2},{1... | collective-permute-start | bytes 344072 | tf_op jit(solution)/shard_map/ppermute | solution.py:26
  86.8 20.6 %collective-permute-start.9 = (bf16[14,32,128]{2,1,0:T(8,128)(2,1)S(1)}, bf16[14,32,128]{2,1,0:T(8,128)(2,1)S(1)}, u32[]{:S(2)}, u32[]{:S(2)}) collective-permute-start(bf16[14,32,128]{2,1,0:T(8,128)(2,1)S(1)} %get-tuple-element.41), channel_id=1, source_target_pairs={{0,8},{4,12},{8,0},{12,4},{1,9},{5,13},{9,1},{13,5},{2,10},{6,14},... | collective-permute-start | bytes 344072 | tf_op jit(solution)/shard_map/ppermute | solution.py:26
  94.5 16.7 %collective-permute-start.3 = (f32[13,32,128]{2,1,0:T(8,128)S(1)}, f32[13,32,128]{2,1,0:T(8,128)S(1)}, u32[]{:S(2)}, u32[]{:S(2)}) collective-permute-start(f32[13,32,128]{2,1,0:T(8,128)S(1)} %get-tuple-element.35), channel_id=1, source_target_pairs={{0,4},{4,0},{8,12},{12,8},{1,5},{5,1},{9,13},{13,9},{2,6},{6,2},{1... | collective-permute-start | bytes 638984 | tf_op jit(solution)/shard_map/ppermute | solution.py:26
  99.0 22.5 %collective-permute-start.4 = (f32[13,32,128]{2,1,0:T(8,128)S(1)}, f32[13,32,128]{2,1,0:T(8,128)S(1)}, u32[]{:S(2)}, u32[]{:S(2)}) collective-permute-start(f32[13,32,128]{2,1,0:T(8,128)S(1)} %get-tuple-element.36), channel_id=1, source_target_pairs={{0,8},{4,12},{8,0},{12,4},{1,9},{5,13},{9,1},{13,5},{2,10},{6,14},... | collective-permute-start | bytes 638984 | tf_op jit(solution)/shard_map/ppermute | solution.py:26
  102.0 19.5 %collective-permute-start.5 = (f32[13,32,128]{2,1,0:T(8,128)S(1)}, f32[13,32,128]{2,1,0:T(8,128)S(1)}, u32[]{:S(2)}, u32[]{:S(2)}) collective-permute-start(f32[13,32,128]{2,1,0:T(8,128)S(1)} %get-tuple-element.37), channel_id=1, source_target_pairs={{0,12},{4,8},{8,4},{12,0},{1,13},{5,9},{9,5},{13,1},{2,14},{6,10},... | collective-permute-start | bytes 638984 | tf_op jit(solution)/shard_map/ppermute | solution.py:26
  106.8 14.8 %collective-permute-start.15 = (bf16[14,32,128]{2,1,0:T(8,128)(2,1)S(1)}, bf16[14,32,128]{2,1,0:T(8,128)(2,1)S(1)}, u32[]{:S(2)}, u32[]{:S(2)}) collective-permute-start(bf16[14,32,128]{2,1,0:T(8,128)(2,1)S(1)} %get-tuple-element.47), channel_id=1, source_target_pairs={{0,4},{4,0},{8,12},{12,8},{1,5},{5,1},{9,13},{13,9},{2,6},{6,2},{1... | collective-permute-start | bytes 344072 | tf_op jit(solution)/shard_map/ppermute | solution.py:26
  107.4 21.1 %collective-permute-start.16 = (bf16[14,32,128]{2,1,0:T(8,128)(2,1)S(1)}, bf16[14,32,128]{2,1,0:T(8,128)(2,1)S(1)}, u32[]{:S(2)}, u32[]{:S(2)}) collective-permute-start(bf16[14,32,128]{2,1,0:T(8,128)(2,1)S(1)} %get-tuple-element.48), channel_id=1, source_target_pairs={{0,8},{4,12},{8,0},{12,4},{1,9},{5,13},{9,1},{13,5},{2,10},{6,14},... | collective-permute-start | bytes 344072 | tf_op jit(solution)/shard_map/ppermute | solution.py:26
  111.2 17.3 %collective-permute-start.17 = (bf16[14,32,128]{2,1,0:T(8,128)(2,1)S(1)}, bf16[14,32,128]{2,1,0:T(8,128)(2,1)S(1)}, u32[]{:S(2)}, u32[]{:S(2)}) collective-permute-start(bf16[14,32,128]{2,1,0:T(8,128)(2,1)S(1)} %get-tuple-element.49), channel_id=1, source_target_pairs={{0,12},{4,8},{8,4},{12,0},{1,13},{5,9},{9,5},{13,1},{2,14},{6,10},... | collective-permute-start | bytes 344072 | tf_op jit(solution)/shard_map/ppermute | solution.py:26
  129.2 1.9 %collective-permute-start.18 = (bf16[9,32,128]{2,1,0:T(8,128)(2,1)S(1)}, bf16[9,32,128]{2,1,0:T(8,128)(2,1)S(1)}, u32[]{:S(2)}, u32[]{:S(2)}) collective-permute-start(bf16[9,32,128]{2,1,0:T(8,128)(2,1)S(1)} %get-tuple-element.51), channel_id=1, source_target_pairs={{0,1},{1,0},{2,3},{3,2},{4,5},{5,4},{6,7},{7,6},{8,9},{9,8},{10,11... | collective-permute-start | bytes 221192 | tf_op jit(solution)/shard_map/ppermute | solution.py:26
  129.3 4.8 %collective-permute-start.19 = (bf16[9,32,128]{2,1,0:T(8,128)(2,1)S(1)}, bf16[9,32,128]{2,1,0:T(8,128)(2,1)S(1)}, u32[]{:S(2)}, u32[]{:S(2)}) collective-permute-start(bf16[9,32,128]{2,1,0:T(8,128)(2,1)S(1)} %get-tuple-element.52), channel_id=1, source_target_pairs={{0,2},{1,3},{2,0},{3,1},{4,6},{5,7},{6,4},{7,5},{8,10},{9,11},{10,... | collective-permute-start | bytes 221192 | tf_op jit(solution)/shard_map/ppermute | solution.py:26
  130.9 4.5 %collective-permute-start.20 = (bf16[9,32,128]{2,1,0:T(8,128)(2,1)S(1)}, bf16[9,32,128]{2,1,0:T(8,128)(2,1)S(1)}, u32[]{:S(2)}, u32[]{:S(2)}) collective-permute-start(bf16[9,32,128]{2,1,0:T(8,128)(2,1)S(1)} %get-tuple-element.53), channel_id=1, source_target_pairs={{0,3},{1,2},{2,1},{3,0},{4,7},{5,6},{6,5},{7,4},{8,11},{9,10},{10,... | collective-permute-start | bytes 221192 | tf_op jit(solution)/shard_map/ppermute | solution.py:26
  135.4 7.6 %collective-permute-start.21 = (bf16[15,32,128]{2,1,0:T(8,128)(2,1)S(1)}, bf16[15,32,128]{2,1,0:T(8,128)(2,1)S(1)}, u32[]{:S(2)}, u32[]{:S(2)}) collective-permute-start(bf16[15,32,128]{2,1,0:T(8,128)(2,1)S(1)} %join.1.rest_0_), channel_id=1, source_target_pairs={{0,4},{4,0},{8,12},{12,8},{1,5},{5,1},{9,13},{13,9},{2,6},{6,2},{1... | collective-permute-start | bytes 368648 | tf_op jit(solution)/shard_map/ppermute | solution.py:26
  137.7 12.4 %collective-permute-start.22 = (bf16[15,32,128]{2,1,0:T(8,128)(2,1)S(1)}, bf16[15,32,128]{2,1,0:T(8,128)(2,1)S(1)}, u32[]{:S(2)}, u32[]{:S(2)}) collective-permute-start(bf16[15,32,128]{2,1,0:T(8,128)(2,1)S(1)} %join.1.rest_0_), channel_id=1, source_target_pairs={{0,8},{4,12},{8,0},{12,4},{1,9},{5,13},{9,1},{13,5},{2,10},{6,14},... | collective-permute-start | bytes 368648 | tf_op jit(solution)/shard_map/ppermute | solution.py:26
  138.9 11.2 %collective-permute-start.23 = (bf16[15,32,128]{2,1,0:T(8,128)(2,1)S(1)}, bf16[15,32,128]{2,1,0:T(8,128)(2,1)S(1)}, u32[]{:S(2)}, u32[]{:S(2)}) collective-permute-start(bf16[15,32,128]{2,1,0:T(8,128)(2,1)S(1)} %join.1.rest_0_), channel_id=1, source_target_pairs={{0,12},{4,8},{8,4},{12,0},{1,13},{5,9},{9,5},{13,1},{2,14},{6,10},... | collective-permute-start | bytes 368648 | tf_op jit(solution)/shard_map/ppermute | solution.py:26
  (9 other events, 203.4 us)

commit v3 on v2

--- a/solution.py
+++ b/solution.py
@@ -223,11 +223,7 @@
             other_pole = lax.axis_index("pole") ^ mask
             kind = out_ref.dtype
             out_ref[:blocks] = y_ref[:, other_pole].astype(kind)
-            diag = d_ref[other_pole]
-            high = diag.astype(kind)
-            out_ref[blocks] = high
-            if kind != F32:
-                out_ref[blocks + 1] = (diag - high.astype(F32)).astype(kind)
+            out_ref[blocks] = d_ref[other_pole].astype(kind)
 
 
 def last_product(g, left, right, acc, own, diag, weights, panel, step, offset, poles, kind):
@@ -236,7 +232,7 @@
     tile = row_block(rows)
     blocks = rows // width
     whole = pl.BlockSpec(left.shape, lambda m: (0, 0, 0), pipeline_mode=pl.Buffered(1))
-    shape = (blocks + (1 if kind == F32 else 2), width // poles, width)
+    shape = (blocks + 1, width // poles, width)
     return pl.pallas_call(
         functools.partial(last_kernel, poles, step, offset),
         grid=(rows // tile,),
@@ -302,11 +298,11 @@
     for c in range(CAP):
         value = jnp.sum(jnp.where(mine & (rank == c + 1.0), code, 0.0), axis=0, keepdims=True)
         send_ref[c : c + 1] = value.astype(jnp.int32)
-    lane = lax.broadcasted_iota(jnp.int32, (1, cols), 1)
-    order = jnp.zeros((1, cols), jnp.int32)
+    lane = lax.broadcasted_iota(jnp.int32, (1, tiles), 1)
+    order = jnp.zeros((1, tiles), jnp.int32)
     for j in range(panels):
         order = jnp.where(lane == j, order_ref[j], order)
-    send_ref[CAP : CAP + 1] = order
+    plan_ref[2 * most + 1 : 2 * most + 2] = order
     mask = (owner ^ me).astype(F32)
     spots = jnp.where((needed > 0.5) & (dest == me), mask * CAP + jnp.minimum(rank, CAP) - 1.0, 0.0)
     spots = jnp.sum(spots, axis=1, keepdims=True)
@@ -324,8 +320,8 @@
         in_specs=[SMEM, VMEM, VMEM],
         out_specs=[VMEM] * 2,
         out_shape=[
-            jax.ShapeDtypeStruct((CAP + 1, cols), jnp.int32),
-            jax.ShapeDtypeStruct((2 * most + 1, tiles), jnp.int32),
+            jax.ShapeDtypeStruct((CAP, cols), jnp.int32),
+            jax.ShapeDtypeStruct((2 * most + 2, tiles), jnp.int32),
         ],
         compiler_params=pltpu.CompilerParams(vmem_limit_bytes=LIMIT),
         cost_estimate=pl.CostEstimate(flops=1 << 20, bytes_accessed=1 << 20, transcendentals=0),
@@ -335,10 +331,7 @@
 
 def total_of(parts, blocks):
     density = tree_sum([part[:blocks].astype(F32) for part in parts])
-    diag = [part[blocks].astype(F32) for part in parts]
-    if parts[0].dtype != F32:
-        diag = [high + part[blocks + 1].astype(F32) for high, part in zip(diag, parts)]
-    return density.astype(BF16), tree_sum(diag)
+    return density.astype(BF16), tree_sum([part[blocks].astype(F32) for part in parts])
 
 
 def settle_kernel(poles, blocks, *refs):
@@ -366,74 +359,78 @@
     )(*[part for group in groups for part in group])
 
 
-def pick_kernel(poles, blocks, send_ref, early_ref, early_diag_ref, *rest):
-    parts, out_refs, (all_ref, diag_ref) = rest[:poles], rest[poles:-2], rest[-2:]
+def pick_kernel(poles, blocks, send_ref, early_ref, *rest):
+    parts, out_refs, all_ref = rest[:poles], rest[poles:-1], rest[-1]
     early = early_ref.shape[0]
-    panels = diag_ref.shape[0]
     me = lax.axis_index("col")
     all_ref[:early] = early_ref[...]
-    density, last_diag = total_of(parts, blocks)
+    density, diag = total_of(parts, blocks)
     all_ref[early:] = density
-    diag_ref[: panels - 1] = early_diag_ref[...]
-    diag_ref[panels - 1] = last_diag
     for mask, out_ref in enumerate(out_refs):
         for c in range(CAP):
             out_ref[c] = all_ref[send_ref[c, me ^ mask]]
-    for j in range(panels):
-        diag = diag_ref[send_ref[CAP, j]]
-        high = diag.astype(BF16)
-        low = (diag - high.astype(F32)).astype(BF16)
-        for out_ref in out_refs:
-            out_ref[CAP + 2 * j] = high
-            out_ref[CAP + 2 * j + 1] = low
-
-
-def pick(send, early, early_diag, parts, blocks, cols):
+        out_ref[CAP] = diag.astype(BF16)
+
+
+def pick(send, early, parts, blocks, cols):
     poles = len(parts)
     depth, width = early.shape[1:]
-    panels = early_diag.shape[0] + 1
-    shape = (CAP + 2 * panels, depth, width)
     return pl.pallas_call(
         functools.partial(pick_kernel, poles, blocks),
-        in_specs=[SMEM] + [VMEM] * (2 + poles),
+        in_specs=[SMEM] + [VMEM] * (1 + poles),
         out_specs=[VMEM] * cols,
-        out_shape=[jax.ShapeDtypeStruct(shape, BF16)] * cols,
-        scratch_shapes=[
-            pltpu.VMEM((early.shape[0] + blocks, depth, width), BF16),
-            pltpu.VMEM((panels, depth, width), F32),
-        ],
+        out_shape=[jax.ShapeDtypeStruct((CAP + 1, depth, width), BF16)] * cols,
+        scratch_shapes=[pltpu.VMEM((early.shape[0] + blocks, depth, width), BF16)],
         compiler_params=pltpu.CompilerParams(vmem_limit_bytes=LIMIT),
         name="pick",
-    )(send, early, early_diag, *parts)
-
-
-def join_kernel(*refs):
+    )(send, early, *parts)
+
+
+def near_join_kernel(diag_ref, *refs):
     parts, out_ref = refs[:-1], refs[-1]
-    for mask, part in enumerate(parts):
-        for c in range(CAP):
-            out_ref[mask * CAP + c] = part[c]
-    for q in range(out_ref.shape[0] - len(parts) * CAP):
-        place = CAP + 2 * q
-        total = tree_sum([part[place].astype(F32) + part[place + 1].astype(F32) for part in parts])
-        out_ref[len(parts) * CAP + q] = total.astype(BF16)
-
-
-def join(parts):
-    depth, width = parts[0].shape[1:]
-    extra = (parts[0].shape[0] - CAP) // 2
-    return pl.pallas_call(
-        join_kernel,
+    end = len(parts) * CAP
+    for place, part in enumerate(parts):
+        out_ref[place * CAP : (place + 1) * CAP] = part[:CAP]
+    out_ref[end:] = diag_ref[...].astype(BF16)
+
+
+def far_join_kernel(skip, *refs):
+    parts, out_ref = refs[:-1], refs[-1]
+    for place, part in enumerate(parts[skip:]):
+        out_ref[place * CAP : (place + 1) * CAP] = part[:CAP]
+    out_ref[out_ref.shape[0] - 1] = tree_sum([part[CAP].astype(F32) for part in parts]).astype(BF16)
+
+
+def join(kernel, operands, slots):
+    depth, width = operands[0].shape[1:]
+    return pl.pallas_call(
+        kernel,
+        in_specs=[VMEM] * len(operands),
+        out_specs=VMEM,
+        out_shape=jax.ShapeDtypeStruct((slots, depth, width), BF16),
+        compiler_params=pltpu.CompilerParams(vmem_limit_bytes=LIMIT),
+    )(*operands)
+
+
+def add_kernel(*refs):
+    refs[-1][...] = tree_sum([ref[...] for ref in refs[:-1]])
+
+
+def add(parts):
+    return pl.pallas_call(
+        add_kernel,
         in_specs=[VMEM] * len(parts),
         out_specs=VMEM,
-        out_shape=jax.ShapeDtypeStruct((len(parts) * CAP + extra, depth, width), BF16),
-        compiler_params=pltpu.CompilerParams(vmem_limit_bytes=LIMIT),
-        name="join",
+        out_shape=jax.ShapeDtypeStruct(parts[0].shape, F32),
+        compiler_params=pltpu.CompilerParams(vmem_limit_bytes=LIMIT),
+        name="add",
     )(*parts)
 
 
 def tile_kernel(plan_ref, row_ref, orbital_ref, core_hbm, *rest):
-    parts = rest[:-6]
-    valence_ref, potential_ref, diag_ref, blocks_ref, core_ref, core_sem = rest[-6:]
+    poles = (len(rest) - 7) // 2
+    near_parts, far_parts = rest[:poles], rest[poles : 2 * poles]
+    valence_ref, potential_ref, diag_ref, blocks_ref, raw_ref, core_ref, core_sem = rest[-7:]
     tiles, most = row_ref.shape[:2]
     slots, poles, depth, width = blocks_ref.shape
     panels = diag_ref.shape[0]
@@ -441,11 +438,15 @@
     core_copy = pltpu.make_async_copy(core_hbm, core_ref, core_sem)
     core_copy.start()
 
-    for mask, part in enumerate(parts):
+    first_slots = 2 * CAP
+    for mask, (near, far) in enumerate(zip(near_parts, far_parts)):
         owner = lax.axis_index("pole") ^ mask
-        blocks_ref[:, owner] = part[:slots]
-        for j in range(panels):
-            diag_ref[j, owner] = part[slots + j].astype(F32)
+        blocks_ref[:first_slots, owner] = near[:first_slots]
+        blocks_ref[first_slots:, owner] = far[: slots - first_slots]
+        raw_ref[: panels - 1, owner] = near[first_slots:]
+        raw_ref[panels - 1, owner] = far[slots - first_slots]
+    for j in range(panels):
+        diag_ref[j] = raw_ref[plan_ref[2 * most + 1, j]].astype(F32)
 
     def one(t, _):
         valence = jnp.zeros((1, row_ref.shape[-1]), F32)
@@ -466,15 +467,15 @@
     potential_ref[...] = -exchange_coeff * clamped ** (1.0 / 3.0)
 
 
-def tile_stage(plan, rows, orbitals, core, parts, cols):
+def tile_stage(plan, rows, orbitals, core, near_parts, far_parts, cols):
     _, _, width, _ = rows.shape
     panels = orbitals.shape[1]
     slots = cols * CAP
-    poles = len(parts)
+    poles = len(near_parts)
     depth = width // poles
     valence, potential, diag = pl.pallas_call(
         tile_kernel,
-        in_specs=[SMEM, VMEM, VMEM, pl.BlockSpec(memory_space=pl.ANY)] + [VMEM] * poles,
+        in_specs=[SMEM, VMEM, VMEM, pl.BlockSpec(memory_space=pl.ANY)] + [VMEM] * (2 * poles),
         out_specs=[VMEM] * 3,
         out_shape=[
             jax.ShapeDtypeStruct(core.shape, F32),
@@ -483,12 +484,13 @@
         ],
         scratch_shapes=[
             pltpu.VMEM((slots, poles, depth, width), BF16),
+            pltpu.VMEM((panels, poles, depth, width), BF16),
             pltpu.VMEM(core.shape, F32),
             pltpu.SemaphoreType.DMA(()),
         ],
         compiler_params=pltpu.CompilerParams(vmem_limit_bytes=LIMIT),
         name="tile_stage",
-    )(plan, rows, orbitals, core, *parts)
+    )(plan, rows, orbitals, core, *near_parts, *far_parts)
     return valence, potential, diag.reshape(panels, width, width)
 
 
@@ -547,13 +549,24 @@
             sums.append(group)
 
     early, early_diag = settle(sums[:-1], blocks)
-    messages = pick(send, early, early_diag, sums[-1], blocks, cols)
-    arrived = [messages[0]] + [swap(messages[mask], "col", mask) for mask in range(1, cols)]
-    joined = join(arrived)
-    gathered = [joined]
+    spread = [early_diag]
+    for mask in range(1, cols):
+        spread.append(swap(early_diag, "col", mask))
+    diag_rows = add(spread)
+    messages = pick(send, early, sums[-1], blocks, cols)
+    arrived = [messages[0]]
+    for mask in range(1, cols):
+        arrived.append(swap(messages[mask], "col", mask))
+    panels_early = diag_rows.shape[0]
+    near = join(near_join_kernel, [diag_rows] + arrived[:2], 2 * CAP + panels_early)
+    gathered_near = [near]
     for mask in range(1, poles):
-        gathered.append(swap(joined, "pole", mask))
-    return tile_stage(plan, row_orbitals, panel_orbitals, core_density, gathered, cols)
+        gathered_near.append(swap(near, "pole", mask))
+    far = join(functools.partial(far_join_kernel, 2), arrived, (cols - 2) * CAP + 1)
+    gathered_far = [far]
+    for mask in range(1, poles):
+        gathered_far.append(swap(far, "pole", mask))
+    return tile_stage(plan, row_orbitals, panel_orbitals, core_density, gathered_near, gathered_far, cols)
 
 
 def solution(mesh):

time: 153 us -> 157 us (1.026)
  starting transfers between devices: 26.2 us -> 32.3 us
  waiting for transfers between devices: 79.6 us -> 77.7 us
    ppermute x24 -> x30, starting transfers between devices: 26.2 us -> 32.3 us  [swap(): return lax.ppermute(value, axis, [(i, i ^ mask) for i in range(size)])]
    ppermute x24 -> x30, waiting for transfers between devices: 79.6 us -> 77.7 us  [swap(): return lax.ppermute(value, axis, [(i, i ^ mask) for i in range(size)])]
  transfers between devices with their start and end apart: 24 -> 30, of which waited for: 8 -> 9; matrix products, arithmetic and copies ran while one was open for 1% -> 1% of each run, Pallas kernels for 27% -> 26%
where the time goes in v3:
time: 157 us
  waiting for transfers between devices  77.7 us (49%)
  Pallas kernels  44 us (28%)
  starting transfers between devices  32.3 us (21%)
  local copies, waits for them, and re-layouts  1.7 us (1%)
    ppermute x30, waiting for transfers between devices, swap(): return lax.ppermute(value, axis, [(i, i ^ mask) for i in range(size)])  77.7 us
    ppermute x30, starting transfers between devices, swap(): return lax.ppermute(value, axis, [(i, i ^ mask) for i in range(size)])  32.3 us
    pallas_call x3, Pallas kernels, last_product(): pl.pallas_call(functools.partial(last_kernel, poles, step, offset), grid=...  18.8 us
    pallas_call x1, Pallas kernels, near_product(): pl.pallas_call(near_kernel, grid=(rows // tile,), in_specs=[pl.BlockSpec(...  18 us
  transfers between devices with their start and end apart: 30, of which 9 were waited for; matrix products, arithmetic and copies ran while one was open for 1% of the time, Pallas kernels for 26%

profile of v3, /device:TPU:0, one launch (start us, length us, event | category | flops | bytes accessed | tf_op | source)
XLA Modules:
  0.0 156.6 jit_solution(12444275483516989837)
XLA Ops:
  1.2 1.6 %slice_bitcast_fusion = (bf16[2,1536,128]{2,1,0:T(8,128)(2,1)S(1)}, bf16[2,1536,128]{2,1,0:T(8,128)(2,1)S(1)}) fusion(bf16[1,3,2,1536,128]{4,3,2,1,0:T(8,128)(2,1)} %param.11), kind=kLoop, calls=%fused_computation | loop fusion | bytes 3145728 | tf_op jit(solution)/shard_map/squeeze | solution.py:528
  2.8 2.6 %collective-permute-start.6 = (bf16[2,1536,128]{2,1,0:T(8,128)(2,1)S(1)}, bf16[2,1536,128]{2,1,0:T(8,128)(2,1)S(1)}, u32[]{:S(2)}, u32[]{:S(2)}) collective-permute-start(bf16[2,1536,128]{2,1,0:T(8,128)(2,1)S(1)} %get-tuple-element.59), channel_id=1, source_target_pairs={{0,2},{1,3},{2,0},{3,1},{4,6},{5,7},{6,4},{7,5},{8,10},{9,11},{10,... | collective-permute-start | bytes 2359304 | tf_op jit(solution)/shard_map/ppermute | solution.py:26
  5.5 2.0 %collective-permute-start.16 = (bf16[2,768,128]{2,1,0:T(8,128)(2,1)S(1)}, bf16[2,768,128]{2,1,0:T(8,128)(2,1)S(1)}, u32[]{:S(2)}, u32[]{:S(2)}) collective-permute-start(bf16[2,768,128]{2,1,0:T(8,128)(2,1)S(1)} %get-tuple-element.57), channel_id=1, source_target_pairs={{0,2},{1,3},{2,0},{3,1},{4,6},{5,7},{6,4},{7,5},{8,10},{9,11},{10,... | collective-permute-start | bytes 1179656 | tf_op jit(solution)/shard_map/ppermute | solution.py:26
  7.6 41.4 %collective-permute-done.16.left_ref = bf16[2,768,128]{2,1,0:T(8,128)(2,1)S(1)} collective-permute-done((bf16[2,768,128]{2,1,0:T(8,128)(2,1)S(1)}, bf16[2,768,128]{2,1,0:T(8,128)(2,1)S(1)}, u32[]{:S(2)}, u32[]{:S(2)}) %collective-permute-start.16) | collective-permute-done | bytes 393248 | tf_op jit(solution)/shard_map/ppermute | solution.py:26
  49.1 8.1 %collective-permute-done.14.left_ref = bf16[2,768,128]{2,1,0:T(8,128)(2,1)S(1)} collective-permute-done((bf16[2,768,128]{2,1,0:T(8,128)(2,1)S(1)}, bf16[2,768,128]{2,1,0:T(8,128)(2,1)S(1)}, u32[]{:S(2)}, u32[]{:S(2)}) %collective-permute-start.14) | collective-permute-done | bytes 393248 | tf_op jit(solution)/shard_map/ppermute | solution.py:26
  57.7 18.0 %near_product.1 = (f32[1536,256]{1,0:T(8,128)S(1)}, f32[1536,256]{1,0:T(8,128)S(1)}, f32[1536,256]{1,0:T(8,128)S(1)}, bf16[2,1536,3072]{2,1,0:T(8,128)(2,1)S(1)}) custom-call(bf16[2,1536,6144]{2,1,0:T(8,128)(2,1)} %bitcast.25, bf16[3,2,1536,128]{3,2,1,0:T(8,128)(2,1)S(1)} %bitcast.16, bf16[3,2,1536,128]{3,2,1,0:T(8,128)(2,1)S(1)} %collective-permute-done.partner_ref), custom_call_target="tpu_custom_call" | custom-call | flops 14495514624 | bytes 37748736 | tf_op jit(solution)/shard_map/near_product/pallas_call | solution.py:118
  75.7 7.1 %last_product.4 = (bf16[13,32,128]{2,1,0:T(8,128)(2,1)S(1)}, bf16[13,32,128]{2,1,0:T(8,128)(2,1)S(1)}, bf16[13,32,128]{2,1,0:T(8,128)(2,1)S(1)}, bf16[13,32,128]{2,1,0:T(8,128)(2,1)S(1)}) custom-call(bf16[2,1536,3072]{2,1,0:T(8,128)(2,1)S(1)} %get-tuple-element.31.g_ref, bf16[2,1536,128]{2,1,0:T(8,128)(2,1)S(1)} %collective-permute-done.6.left_ref, ...), custom_call_target="tpu_custom_call" | custom-call | flops 4831838208 | bytes 1572864 | tf_op jit(solution)/shard_map/last_product/pallas_call | solution.py:236
  82.8 3.9 %collective-permute-start.10 = (bf16[13,32,128]{2,1,0:T(8,128)(2,1)S(1)}, bf16[13,32,128]{2,1,0:T(8,128)(2,1)S(1)}, u32[]{:S(2)}, u32[]{:S(2)}) collective-permute-start(bf16[13,32,128]{2,1,0:T(8,128)(2,1)S(1)} %get-tuple-element.41), channel_id=1, source_target_pairs={{0,12},{4,8},{8,4},{12,0},{1,13},{5,9},{9,5},{13,1},{2,14},{6,10},... | collective-permute-start | bytes 319496 | tf_op jit(solution)/shard_map/ppermute | solution.py:26
  87.4 7.1 %last_product.3 = (f32[13,32,128]{2,1,0:T(8,128)S(1)}, f32[13,32,128]{2,1,0:T(8,128)S(1)}, f32[13,32,128]{2,1,0:T(8,128)S(1)}, f32[13,32,128]{2,1,0:T(8,128)S(1)}) custom-call(bf16[2,1536,3072]{2,1,0:T(8,128)(2,1)S(1)} %get-tuple-element.31.g_ref, bf16[2,1536,128]{2,1,0:T(8,128)(2,1)S(1)} %collective-permute-done.1.left_ref, ...), custom_call_target="tpu_custom_call" | custom-call | flops 4831838208 | bytes 1572864 | tf_op jit(solution)/shard_map/last_product/pallas_call | solution.py:236
  94.5 1.5 collective-permute-start.3
  95.9 3.0 %far_product.1.acc_ref = f32[1536,256]{1,0:T(8,128)S(1)} custom-call(bf16[2,1536,3072]{2,1,0:T(8,128)(2,1)S(1)} %get-tuple-element.31.g_ref, bf16[2,768,128]{2,1,0:T(8,128)(2,1)S(1)} %collective-permute-done.16.left_ref, bf16[2,768,128]{2,1,0:T(8,128)(2,1)S(1)} %collective-permute-done.17.right_ref, f32[1536,256]{1,0:T(8,128)S(1)} %get-tuple-element.45.acc_ref), custom_call_target="tpu_custom_call" | custom-call | flops 2415919104 | bytes 1572864 | tf_op jit(solution)/shard_map/far_product/pallas_call | solution.py:159
  99.0 3.0 %collective-permute-start.4 = (f32[13,32,128]{2,1,0:T(8,128)S(1)}, f32[13,32,128]{2,1,0:T(8,128)S(1)}, u32[]{:S(2)}, u32[]{:S(2)}) collective-permute-start(f32[13,32,128]{2,1,0:T(8,128)S(1)} %get-tuple-element.35), channel_id=1, source_target_pairs={{0,8},{4,12},{8,0},{12,4},{1,9},{5,13},{9,1},{13,5},{2,10},{6,14},... | collective-permute-start | bytes 638984 | tf_op jit(solution)/shard_map/ppermute | solution.py:26
  102.1 4.6 %last_product.5 = (bf16[13,32,128]{2,1,0:T(8,128)(2,1)S(1)}, bf16[13,32,128]{2,1,0:T(8,128)(2,1)S(1)}, bf16[13,32,128]{2,1,0:T(8,128)(2,1)S(1)}, bf16[13,32,128]{2,1,0:T(8,128)(2,1)S(1)}) custom-call(bf16[2,1536,3072]{2,1,0:T(8,128)(2,1)S(1)} %get-tuple-element.31.g_ref, bf16[2,768,128]{2,1,0:T(8,128)(2,1)S(1)} %collective-permute-done.14.left_ref, ...), custom_call_target="tpu_custom_call" | custom-call | flops 2415919104 | bytes 1572864 | tf_op jit(solution)/shard_map/last_product/pallas_call | solution.py:236
  107.4 3.8 %collective-permute-start.19 = (bf16[13,32,128]{2,1,0:T(8,128)(2,1)S(1)}, bf16[13,32,128]{2,1,0:T(8,128)(2,1)S(1)}, u32[]{:S(2)}, u32[]{:S(2)}) collective-permute-start(bf16[13,32,128]{2,1,0:T(8,128)(2,1)S(1)} %get-tuple-element.48), channel_id=1, source_target_pairs={{0,8},{4,12},{8,0},{12,4},{1,9},{5,13},{9,1},{13,5},{2,10},{6,14},... | collective-permute-start | bytes 319496 | tf_op jit(solution)/shard_map/ppermute | solution.py:26
  112.4 8.7 %collective-permute-done.4.refs_2_ = f32[13,32,128]{2,1,0:T(8,128)S(1)} collective-permute-done((f32[13,32,128]{2,1,0:T(8,128)S(1)}, f32[13,32,128]{2,1,0:T(8,128)S(1)}, u32[]{:S(2)}, u32[]{:S(2)}) %collective-permute-start.4) | collective-permute-done | bytes 213024 | tf_op jit(solution)/shard_map/ppermute | solution.py:26
  121.3 6.7 %collective-permute-done.19.rest_2_ = bf16[13,32,128]{2,1,0:T(8,128)(2,1)S(1)} collective-permute-done((bf16[13,32,128]{2,1,0:T(8,128)(2,1)S(1)}, bf16[13,32,128]{2,1,0:T(8,128)(2,1)S(1)}, u32[]{:S(2)}, u32[]{:S(2)}) %collective-permute-start.19) | collective-permute-done | bytes 106528 | tf_op jit(solution)/shard_map/ppermute | solution.py:26
  128.7 1.6 collective-permute-start.25
  130.6 2.1 %collective-permute-done.25.refs_2_ = bf16[4,32,128]{2,1,0:T(8,128)(2,1)S(1)} collective-permute-done((bf16[4,32,128]{2,1,0:T(8,128)(2,1)S(1)}, bf16[4,32,128]{2,1,0:T(8,128)(2,1)S(1)}, u32[]{:S(2)}, u32[]{:S(2)}) %collective-permute-start.25) | collective-permute-done | bytes 32800 | tf_op jit(solution)/shard_map/ppermute | solution.py:26
  133.7 2.2 %collective-permute-start.27 = (bf16[7,32,128]{2,1,0:T(8,128)(2,1)S(1)}, bf16[7,32,128]{2,1,0:T(8,128)(2,1)S(1)}, u32[]{:S(2)}, u32[]{:S(2)}) collective-permute-start(bf16[7,32,128]{2,1,0:T(8,128)(2,1)S(1)} %shard_map.122.rest_4_), channel_id=1, source_target_pairs={{0,4},{4,0},{8,12},{12,8},{1,5},{5,1},{9,13},{13,9},{2,6},{6,2},{1... | collective-permute-start | bytes 172040 | tf_op jit(solution)/shard_map/ppermute | solution.py:26
  137.7 2.1 %collective-permute-done.12.refs_2_ = f32[2,32,128]{2,1,0:T(8,128)S(1)} collective-permute-done((f32[2,32,128]{2,1,0:T(8,128)S(1)}, f32[2,32,128]{2,1,0:T(8,128)S(1)}, u32[]{:S(2)}, u32[]{:S(2)}) %collective-permute-start.12) | collective-permute-done | bytes 32800 | tf_op jit(solution)/shard_map/ppermute | solution.py:26
  140.6 2.6 %collective-permute-start.23 = (bf16[8,32,128]{2,1,0:T(8,128)(2,1)S(1)}, bf16[8,32,128]{2,1,0:T(8,128)(2,1)S(1)}, u32[]{:S(2)}, u32[]{:S(2)}) collective-permute-start(bf16[8,32,128]{2,1,0:T(8,128)(2,1)S(1)} %shard_map.121.rest_0_), channel_id=1, source_target_pairs={{0,8},{4,12},{8,0},{12,4},{1,9},{5,13},{9,1},{13,5},{2,10},{6,14},... | collective-permute-start | bytes 196616 | tf_op jit(solution)/shard_map/ppermute | solution.py:26
  145.0 2.0 %collective-permute-start.29 = (bf16[7,32,128]{2,1,0:T(8,128)(2,1)S(1)}, bf16[7,32,128]{2,1,0:T(8,128)(2,1)S(1)}, u32[]{:S(2)}, u32[]{:S(2)}) collective-permute-start(bf16[7,32,128]{2,1,0:T(8,128)(2,1)S(1)} %shard_map.122.rest_4_), channel_id=1, source_target_pairs={{0,12},{4,8},{8,4},{12,0},{1,13},{5,9},{9,5},{13,1},{2,14},{6,10},... | collective-permute-start | bytes 172040 | tf_op jit(solution)/shard_map/ppermute | solution.py:26
  147.0 7.2 %collective-permute-done.28.rest_6_ = bf16[7,32,128]{2,1,0:T(8,128)(2,1)S(1)} collective-permute-done((bf16[7,32,128]{2,1,0:T(8,128)(2,1)S(1)}, bf16[7,32,128]{2,1,0:T(8,128)(2,1)S(1)}, u32[]{:S(2)}, u32[]{:S(2)}) %collective-permute-start.28) | collective-permute-done | bytes 57376 | tf_op jit(solution)/shard_map/ppermute | solution.py:26
  154.3 2.2 %tile_stage.1 = (f32[8,128]{1,0:T(8,128)}, f32[8,128]{1,0:T(8,128)}, f32[3,4,32,128]{3,2,1,0:T(8,128)}) custom-call(s32[18,32]{1,0:T(8,128)S(1)} %get-tuple-element.30.plan_ref, bf16[8,8,128,128]{3,2,1,0:T(8,128)(2,1)S(1)} %copy-done.2, bf16[8,3,128,128]{3,2,1,0:T(8,128)(2,1)S(1)} %copy-done.3, f32[8,128]{1,0:T(8,128)S(1)} %copy-done.5, ...), custom_call_target="tpu_custom_call" | custom-call | tf_op jit(solution)/shard_map/tile_stage/pallas_call | solution.py:476
  (68 shorter events, 10.6 us)
Async XLA Ops:
  0.6 57.1 %collective-permute-start = (bf16[3,2,1536,128]{3,2,1,0:T(8,128)(2,1)}, bf16[3,2,1536,128]{3,2,1,0:T(8,128)(2,1)S(1)}, u32[]{:S(2)}, u32[]{:S(2)}) collective-permute-start(bf16[3,2,1536,128]{3,2,1,0:T(8,128)(2,1)} %bitcast.14), channel_id=1, source_target_pairs={{0,1},{1,0},{2,3},{3,2},{4,5},{5,4},{6,7},{7,6},{8,9},{9,8},{10,11... | collective-permute-start | bytes 7077896 | tf_op jit(solution)/shard_map/ppermute | solution.py:26
  2.8 54.3 %collective-permute-start.6 = (bf16[2,1536,128]{2,1,0:T(8,128)(2,1)S(1)}, bf16[2,1536,128]{2,1,0:T(8,128)(2,1)S(1)}, u32[]{:S(2)}, u32[]{:S(2)}) collective-permute-start(bf16[2,1536,128]{2,1,0:T(8,128)(2,1)S(1)} %get-tuple-element.59), channel_id=1, source_target_pairs={{0,2},{1,3},{2,0},{3,1},{4,6},{5,7},{6,4},{7,5},{8,10},{9,11},{10,... | collective-permute-start | bytes 2359304 | tf_op jit(solution)/shard_map/ppermute | solution.py:26
  5.4 52.3 %collective-permute-start.1 = (bf16[2,1536,128]{2,1,0:T(8,128)(2,1)S(1)}, bf16[2,1536,128]{2,1,0:T(8,128)(2,1)S(1)}, u32[]{:S(2)}, u32[]{:S(2)}) collective-permute-start(bf16[2,1536,128]{2,1,0:T(8,128)(2,1)S(1)} %get-tuple-element.60), channel_id=1, source_target_pairs={{0,2},{1,3},{2,0},{3,1},{4,6},{5,7},{6,4},{7,5},{8,10},{9,11},{10,... | collective-permute-start | bytes 2359304 | tf_op jit(solution)/shard_map/ppermute | solution.py:26
  5.5 43.5 %collective-permute-start.16 = (bf16[2,768,128]{2,1,0:T(8,128)(2,1)S(1)}, bf16[2,768,128]{2,1,0:T(8,128)(2,1)S(1)}, u32[]{:S(2)}, u32[]{:S(2)}) collective-permute-start(bf16[2,768,128]{2,1,0:T(8,128)(2,1)S(1)} %get-tuple-element.57), channel_id=1, source_target_pairs={{0,2},{1,3},{2,0},{3,1},{4,6},{5,7},{6,4},{7,5},{8,10},{9,11},{10,... | collective-permute-start | bytes 1179656 | tf_op jit(solution)/shard_map/ppermute | solution.py:26
  7.5 49.6 %collective-permute-start.14 = (bf16[2,768,128]{2,1,0:T(8,128)(2,1)S(1)}, bf16[2,768,128]{2,1,0:T(8,128)(2,1)S(1)}, u32[]{:S(2)}, u32[]{:S(2)}) collective-permute-start(bf16[2,768,128]{2,1,0:T(8,128)(2,1)S(1)} %get-tuple-element.58), channel_id=1, source_target_pairs={{0,2},{1,3},{2,0},{3,1},{4,6},{5,7},{6,4},{7,5},{8,10},{9,11},{10,... | collective-permute-start | bytes 1179656 | tf_op jit(solution)/shard_map/ppermute | solution.py:26
  49.0 45.4 %collective-permute-start.17 = (bf16[2,768,128]{2,1,0:T(8,128)(2,1)S(1)}, bf16[2,768,128]{2,1,0:T(8,128)(2,1)S(1)}, u32[]{:S(2)}, u32[]{:S(2)}) collective-permute-start(bf16[2,768,128]{2,1,0:T(8,128)(2,1)S(1)} %collective-permute-done.16.left_ref), channel_id=1, source_target_pairs={{0,1},{1,0},{2,3},{3,2},{4,5},{5,4},{6,7},{7,6},{8,9},{9,8},{10,11... | collective-permute-start | bytes 1179656 | tf_op jit(solution)/shard_map/ppermute | solution.py:26
  57.1 41.8 %collective-permute-start.15 = (bf16[2,768,128]{2,1,0:T(8,128)(2,1)S(1)}, bf16[2,768,128]{2,1,0:T(8,128)(2,1)S(1)}, u32[]{:S(2)}, u32[]{:S(2)}) collective-permute-start(bf16[2,768,128]{2,1,0:T(8,128)(2,1)S(1)} %collective-permute-done.14.left_ref), channel_id=1, source_target_pairs={{0,1},{1,0},{2,3},{3,2},{4,5},{5,4},{6,7},{7,6},{8,9},{9,8},{10,11... | collective-permute-start | bytes 1179656 | tf_op jit(solution)/shard_map/ppermute | solution.py:26
  57.1 18.6 %collective-permute-start.7 = (bf16[2,1536,128]{2,1,0:T(8,128)(2,1)S(1)}, bf16[2,1536,128]{2,1,0:T(8,128)(2,1)S(1)}, u32[]{:S(2)}, u32[]{:S(2)}) collective-permute-start(bf16[2,1536,128]{2,1,0:T(8,128)(2,1)S(1)} %collective-permute-done.6.left_ref), channel_id=1, source_target_pairs={{0,1},{1,0},{2,3},{3,2},{4,5},{5,4},{6,7},{7,6},{8,9},{9,8},{10,11... | collective-permute-start | bytes 2359304 | tf_op jit(solution)/shard_map/ppermute | solution.py:26
  57.7 29.1 %collective-permute-start.2 = (bf16[2,1536,128]{2,1,0:T(8,128)(2,1)S(1)}, bf16[2,1536,128]{2,1,0:T(8,128)(2,1)S(1)}, u32[]{:S(2)}, u32[]{:S(2)}) collective-permute-start(bf16[2,1536,128]{2,1,0:T(8,128)(2,1)S(1)} %collective-permute-done.1.left_ref), channel_id=1, source_target_pairs={{0,1},{1,0},{2,3},{3,2},{4,5},{5,4},{6,7},{7,6},{8,9},{9,8},{10,11... | collective-permute-start | bytes 2359304 | tf_op jit(solution)/shard_map/ppermute | solution.py:26
  82.8 19.1 %collective-permute-start.10 = (bf16[13,32,128]{2,1,0:T(8,128)(2,1)S(1)}, bf16[13,32,128]{2,1,0:T(8,128)(2,1)S(1)}, u32[]{:S(2)}, u32[]{:S(2)}) collective-permute-start(bf16[13,32,128]{2,1,0:T(8,128)(2,1)S(1)} %get-tuple-element.41), channel_id=1, source_target_pairs={{0,12},{4,8},{8,4},{12,0},{1,13},{5,9},{9,5},{13,1},{2,14},{6,10},... | collective-permute-start | bytes 319496 | tf_op jit(solution)/shard_map/ppermute | solution.py:26
  86.8 20.0 %collective-permute-start.8 = (bf16[13,32,128]{2,1,0:T(8,128)(2,1)S(1)}, bf16[13,32,128]{2,1,0:T(8,128)(2,1)S(1)}, u32[]{:S(2)}, u32[]{:S(2)}) collective-permute-start(bf16[13,32,128]{2,1,0:T(8,128)(2,1)S(1)} %get-tuple-element.39), channel_id=1, source_target_pairs={{0,4},{4,0},{8,12},{12,8},{1,5},{5,1},{9,13},{13,9},{2,6},{6,2},{1... | collective-permute-start | bytes 319496 | tf_op jit(solution)/shard_map/ppermute | solution.py:26
  86.8 20.6 %collective-permute-start.9 = (bf16[13,32,128]{2,1,0:T(8,128)(2,1)S(1)}, bf16[13,32,128]{2,1,0:T(8,128)(2,1)S(1)}, u32[]{:S(2)}, u32[]{:S(2)}) collective-permute-start(bf16[13,32,128]{2,1,0:T(8,128)(2,1)S(1)} %get-tuple-element.40), channel_id=1, source_target_pairs={{0,8},{4,12},{8,0},{12,4},{1,9},{5,13},{9,1},{13,5},{2,10},{6,14},... | collective-permute-start | bytes 319496 | tf_op jit(solution)/shard_map/ppermute | solution.py:26
  94.5 16.7 %collective-permute-start.3 = (f32[13,32,128]{2,1,0:T(8,128)S(1)}, f32[13,32,128]{2,1,0:T(8,128)S(1)}, u32[]{:S(2)}, u32[]{:S(2)}) collective-permute-start(f32[13,32,128]{2,1,0:T(8,128)S(1)} %get-tuple-element.34), channel_id=1, source_target_pairs={{0,4},{4,0},{8,12},{12,8},{1,5},{5,1},{9,13},{13,9},{2,6},{6,2},{1... | collective-permute-start | bytes 638984 | tf_op jit(solution)/shard_map/ppermute | solution.py:26
  99.0 22.2 %collective-permute-start.4 = (f32[13,32,128]{2,1,0:T(8,128)S(1)}, f32[13,32,128]{2,1,0:T(8,128)S(1)}, u32[]{:S(2)}, u32[]{:S(2)}) collective-permute-start(f32[13,32,128]{2,1,0:T(8,128)S(1)} %get-tuple-element.35), channel_id=1, source_target_pairs={{0,8},{4,12},{8,0},{12,4},{1,9},{5,13},{9,1},{13,5},{2,10},{6,14},... | collective-permute-start | bytes 638984 | tf_op jit(solution)/shard_map/ppermute | solution.py:26
  102.0 19.2 %collective-permute-start.5 = (f32[13,32,128]{2,1,0:T(8,128)S(1)}, f32[13,32,128]{2,1,0:T(8,128)S(1)}, u32[]{:S(2)}, u32[]{:S(2)}) collective-permute-start(f32[13,32,128]{2,1,0:T(8,128)S(1)} %get-tuple-element.36), channel_id=1, source_target_pairs={{0,12},{4,8},{8,4},{12,0},{1,13},{5,9},{9,5},{13,1},{2,14},{6,10},... | collective-permute-start | bytes 638984 | tf_op jit(solution)/shard_map/ppermute | solution.py:26
  106.8 14.5 %collective-permute-start.18 = (bf16[13,32,128]{2,1,0:T(8,128)(2,1)S(1)}, bf16[13,32,128]{2,1,0:T(8,128)(2,1)S(1)}, u32[]{:S(2)}, u32[]{:S(2)}) collective-permute-start(bf16[13,32,128]{2,1,0:T(8,128)(2,1)S(1)} %get-tuple-element.47), channel_id=1, source_target_pairs={{0,4},{4,0},{8,12},{12,8},{1,5},{5,1},{9,13},{13,9},{2,6},{6,2},{1... | collective-permute-start | bytes 319496 | tf_op jit(solution)/shard_map/ppermute | solution.py:26
  107.4 20.6 %collective-permute-start.19 = (bf16[13,32,128]{2,1,0:T(8,128)(2,1)S(1)}, bf16[13,32,128]{2,1,0:T(8,128)(2,1)S(1)}, u32[]{:S(2)}, u32[]{:S(2)}) collective-permute-start(bf16[13,32,128]{2,1,0:T(8,128)(2,1)S(1)} %get-tuple-element.48), channel_id=1, source_target_pairs={{0,8},{4,12},{8,0},{12,4},{1,9},{5,13},{9,1},{13,5},{2,10},{6,14},... | collective-permute-start | bytes 319496 | tf_op jit(solution)/shard_map/ppermute | solution.py:26
  111.2 16.8 %collective-permute-start.20 = (bf16[13,32,128]{2,1,0:T(8,128)(2,1)S(1)}, bf16[13,32,128]{2,1,0:T(8,128)(2,1)S(1)}, u32[]{:S(2)}, u32[]{:S(2)}) collective-permute-start(bf16[13,32,128]{2,1,0:T(8,128)(2,1)S(1)} %get-tuple-element.49), channel_id=1, source_target_pairs={{0,12},{4,8},{8,4},{12,0},{1,13},{5,9},{9,5},{13,1},{2,14},{6,10},... | collective-permute-start | bytes 319496 | tf_op jit(solution)/shard_map/ppermute | solution.py:26
  133.7 11.3 %collective-permute-start.27 = (bf16[7,32,128]{2,1,0:T(8,128)(2,1)S(1)}, bf16[7,32,128]{2,1,0:T(8,128)(2,1)S(1)}, u32[]{:S(2)}, u32[]{:S(2)}) collective-permute-start(bf16[7,32,128]{2,1,0:T(8,128)(2,1)S(1)} %shard_map.122.rest_4_), channel_id=1, source_target_pairs={{0,4},{4,0},{8,12},{12,8},{1,5},{5,1},{9,13},{13,9},{2,6},{6,2},{1... | collective-permute-start | bytes 172040 | tf_op jit(solution)/shard_map/ppermute | solution.py:26
  140.2 14.1 %collective-permute-start.22 = (bf16[8,32,128]{2,1,0:T(8,128)(2,1)S(1)}, bf16[8,32,128]{2,1,0:T(8,128)(2,1)S(1)}, u32[]{:S(2)}, u32[]{:S(2)}) collective-permute-start(bf16[8,32,128]{2,1,0:T(8,128)(2,1)S(1)} %shard_map.121.rest_0_), channel_id=1, source_target_pairs={{0,4},{4,0},{8,12},{12,8},{1,5},{5,1},{9,13},{13,9},{2,6},{6,2},{1... | collective-permute-start | bytes 196616 | tf_op jit(solution)/shard_map/ppermute | solution.py:26
  140.6 13.7 %collective-permute-start.23 = (bf16[8,32,128]{2,1,0:T(8,128)(2,1)S(1)}, bf16[8,32,128]{2,1,0:T(8,128)(2,1)S(1)}, u32[]{:S(2)}, u32[]{:S(2)}) collective-permute-start(bf16[8,32,128]{2,1,0:T(8,128)(2,1)S(1)} %shard_map.121.rest_0_), channel_id=1, source_target_pairs={{0,8},{4,12},{8,0},{12,4},{1,9},{5,13},{9,1},{13,5},{2,10},{6,14},... | collective-permute-start | bytes 196616 | tf_op jit(solution)/shard_map/ppermute | solution.py:26
  143.2 11.1 %collective-permute-start.24 = (bf16[8,32,128]{2,1,0:T(8,128)(2,1)S(1)}, bf16[8,32,128]{2,1,0:T(8,128)(2,1)S(1)}, u32[]{:S(2)}, u32[]{:S(2)}) collective-permute-start(bf16[8,32,128]{2,1,0:T(8,128)(2,1)S(1)} %shard_map.121.rest_0_), channel_id=1, source_target_pairs={{0,12},{4,8},{8,4},{12,0},{1,13},{5,9},{9,5},{13,1},{2,14},{6,10},... | collective-permute-start | bytes 196616 | tf_op jit(solution)/shard_map/ppermute | solution.py:26
  144.6 9.7 %collective-permute-start.28 = (bf16[7,32,128]{2,1,0:T(8,128)(2,1)S(1)}, bf16[7,32,128]{2,1,0:T(8,128)(2,1)S(1)}, u32[]{:S(2)}, u32[]{:S(2)}) collective-permute-start(bf16[7,32,128]{2,1,0:T(8,128)(2,1)S(1)} %shard_map.122.rest_4_), channel_id=1, source_target_pairs={{0,8},{4,12},{8,0},{12,4},{1,9},{5,13},{9,1},{13,5},{2,10},{6,14},... | collective-permute-start | bytes 172040 | tf_op jit(solution)/shard_map/ppermute | solution.py:26
  145.0 9.3 %collective-permute-start.29 = (bf16[7,32,128]{2,1,0:T(8,128)(2,1)S(1)}, bf16[7,32,128]{2,1,0:T(8,128)(2,1)S(1)}, u32[]{:S(2)}, u32[]{:S(2)}) collective-permute-start(bf16[7,32,128]{2,1,0:T(8,128)(2,1)S(1)} %shard_map.122.rest_4_), channel_id=1, source_target_pairs={{0,12},{4,8},{8,4},{12,0},{1,13},{5,9},{9,5},{13,1},{2,14},{6,10},... | collective-permute-start | bytes 172040 | tf_op jit(solution)/shard_map/ppermute | solution.py:26
  (15 other events, 234.4 us)

commit v4 on v3

--- a/solution.py
+++ b/solution.py
@@ -155,14 +155,13 @@
     _, depth, width = left.shape
     rows = g.shape[1]
     tile = row_block(rows)
-    whole = pl.BlockSpec(left.shape, lambda m: (0, 0, 0), pipeline_mode=pl.Buffered(1))
     return pl.pallas_call(
         functools.partial(far_kernel, step, offset),
         grid=(rows // tile,),
         in_specs=[
             VMEM,
-            whole,
-            whole,
+            VMEM,
+            VMEM,
             VMEM,
         ],
         out_specs=VMEM,
@@ -231,26 +230,25 @@
     rows = g.shape[1]
     tile = row_block(rows)
     blocks = rows // width
-    whole = pl.BlockSpec(left.shape, lambda m: (0, 0, 0), pipeline_mode=pl.Buffered(1))
     shape = (blocks + 1, width // poles, width)
     return pl.pallas_call(
         functools.partial(last_kernel, poles, step, offset),
         grid=(rows // tile,),
         in_specs=[
             VMEM,
-            whole,
-            whole,
+            VMEM,
+            VMEM,
             VMEM,
             pl.BlockSpec((None, 2, tile, width), lambda m: (panel, 0, m, 0)),
             pl.BlockSpec((None, 2, width, width), lambda m: (panel, 0, 0, 0)),
             SMEM,
         ],
-        out_specs=[pl.BlockSpec(shape, lambda m: (0, 0, 0))] * poles,
+        out_specs=[VMEM] * poles,
         scratch_shapes=[
             pltpu.VMEM((blocks, poles, width // poles, width), F32),
             pltpu.VMEM((poles, width // poles, width), F32),
         ],
-        out_shape=[jax.ShapeDtypeStruct(shape, kind)] * poles,
+        out_shape=[pltpu.VMEM(shape, kind)] * poles,
         compiler_params=pltpu.CompilerParams(vmem_limit_bytes=LIMIT),
         cost_estimate=pl.CostEstimate(
             flops=2 * 8 * rows * depth * width, bytes_accessed=8 * rows * width, transcendentals=0
@@ -518,8 +516,8 @@
 
     pieces = []
     for q in range(panel_count):
-        parts = 2 if q == panel_count - 1 else 1
-        pieces += [(q, part * (rows // parts), rows // parts) for part in range(parts)]
+        cut = rows if q == 0 else rows // 2
+        pieces += [(q, 0, cut)] + ([(q, cut, rows - cut)] if cut < rows else [])
 
     partner = swap(own, "col", 1)
     remote = {}

time: 157 us -> 153 us (0.975)
  waiting for transfers between devices: 77.7 us -> 70 us
  starting transfers between devices: 32.3 us -> 36.2 us
    ppermute x30 -> x32, waiting for transfers between devices: 77.7 us -> 70 us  [swap(): return lax.ppermute(value, axis, [(i, i ^ mask) for i in range(size)])]
    ppermute x30 -> x32, starting transfers between devices: 32.3 us -> 36.2 us  [swap(): return lax.ppermute(value, axis, [(i, i ^ mask) for i in range(size)])]
    pallas_call x1 -> x2, Pallas kernels: 3.03 us -> 6.02 us  [far_product(): pl.pallas_call(functools.partial(far_kernel, step, offset), grid=(rows //...]
    pallas_call x3, Pallas kernels: 18.8 us -> 16.3 us  [last_product(): pl.pallas_call(functools.partial(last_kernel, poles, step, offset), grid=...]
  transfers between devices with their start and end apart: 30 -> 32, of which waited for: 9 -> 13; matrix products, arithmetic and copies ran while one was open for 1% -> 1% of each run, Pallas kernels for 26% -> 27%
where the time goes in v4:
time: 153 us
  waiting for transfers between devices  70 us (46%)
  Pallas kernels  44.5 us (29%)
  starting transfers between devices  36.2 us (24%)
  local copies, waits for them, and re-layouts  1.69 us (1%)
    ppermute x32, waiting for transfers between devices, swap(): return lax.ppermute(value, axis, [(i, i ^ mask) for i in range(size)])  70 us
    ppermute x32, starting transfers between devices, swap(): return lax.ppermute(value, axis, [(i, i ^ mask) for i in range(size)])  36.2 us
    pallas_call x1, Pallas kernels, near_product(): pl.pallas_call(near_kernel, grid=(rows // tile,), in_specs=[pl.BlockSpec(...  17.9 us
    pallas_call x3, Pallas kernels, last_product(): pl.pallas_call(functools.partial(last_kernel, poles, step, offset), grid=...  16.3 us
    pallas_call x2, Pallas kernels, far_product(): pl.pallas_call(functools.partial(far_kernel, step, offset), grid=(rows //...  6.02 us
  transfers between devices with their start and end apart: 32, of which 13 were waited for; matrix products, arithmetic and copies ran while one was open for 1% of the time, Pallas kernels for 27%

profile of v4, /device:TPU:0, one launch (start us, length us, event | category | flops | bytes accessed | tf_op | source)
XLA Modules:
  0.0 153.3 jit_solution(4509659741667492451)
XLA Ops:
  2.8 2.6 %collective-permute-start.6 = (bf16[2,768,128]{2,1,0:T(8,128)(2,1)S(1)}, bf16[2,768,128]{2,1,0:T(8,128)(2,1)S(1)}, u32[]{:S(2)}, u32[]{:S(2)}) collective-permute-start(bf16[2,768,128]{2,1,0:T(8,128)(2,1)S(1)} %get-tuple-element.60), channel_id=1, source_target_pairs={{0,2},{1,3},{2,0},{3,1},{4,6},{5,7},{6,4},{7,5},{8,10},{9,11},{10,... | collective-permute-start | bytes 1179656 | tf_op jit(solution)/shard_map/ppermute | solution.py:26
  7.9 7.5 %collective-permute-done.6.left_ref = bf16[2,768,128]{2,1,0:T(8,128)(2,1)S(1)} collective-permute-done((bf16[2,768,128]{2,1,0:T(8,128)(2,1)S(1)}, bf16[2,768,128]{2,1,0:T(8,128)(2,1)S(1)}, u32[]{:S(2)}, u32[]{:S(2)}) %collective-permute-start.6) | collective-permute-done | bytes 393248 | tf_op jit(solution)/shard_map/ppermute | solution.py:26
  15.3 2.0 %collective-permute-start.18 = (bf16[2,768,128]{2,1,0:T(8,128)(2,1)S(1)}, bf16[2,768,128]{2,1,0:T(8,128)(2,1)S(1)}, u32[]{:S(2)}, u32[]{:S(2)}) collective-permute-start(bf16[2,768,128]{2,1,0:T(8,128)(2,1)S(1)} %get-tuple-element.57), channel_id=1, source_target_pairs={{0,2},{1,3},{2,0},{3,1},{4,6},{5,7},{6,4},{7,5},{8,10},{9,11},{10,... | collective-permute-start | bytes 1179656 | tf_op jit(solution)/shard_map/ppermute | solution.py:26
  17.4 23.3 %collective-permute-done.8.left_ref = bf16[2,768,128]{2,1,0:T(8,128)(2,1)S(1)} collective-permute-done((bf16[2,768,128]{2,1,0:T(8,128)(2,1)S(1)}, bf16[2,768,128]{2,1,0:T(8,128)(2,1)S(1)}, u32[]{:S(2)}, u32[]{:S(2)}) %collective-permute-start.8) | collective-permute-done | bytes 393248 | tf_op jit(solution)/shard_map/ppermute | solution.py:26
  40.6 8.4 %collective-permute-done.16.left_ref = bf16[2,768,128]{2,1,0:T(8,128)(2,1)S(1)} collective-permute-done((bf16[2,768,128]{2,1,0:T(8,128)(2,1)S(1)}, bf16[2,768,128]{2,1,0:T(8,128)(2,1)S(1)}, u32[]{:S(2)}, u32[]{:S(2)}) %collective-permute-start.16) | collective-permute-done | bytes 393248 | tf_op jit(solution)/shard_map/ppermute | solution.py:26
  49.1 8.1 %collective-permute-done.18.left_ref = bf16[2,768,128]{2,1,0:T(8,128)(2,1)S(1)} collective-permute-done((bf16[2,768,128]{2,1,0:T(8,128)(2,1)S(1)}, bf16[2,768,128]{2,1,0:T(8,128)(2,1)S(1)}, u32[]{:S(2)}, u32[]{:S(2)}) %collective-permute-start.18) | collective-permute-done | bytes 393248 | tf_op jit(solution)/shard_map/ppermute | solution.py:26
  57.7 17.9 %near_product.1 = (f32[1536,256]{1,0:T(8,128)S(1)}, f32[1536,256]{1,0:T(8,128)S(1)}, f32[1536,256]{1,0:T(8,128)S(1)}, bf16[2,1536,3072]{2,1,0:T(8,128)(2,1)S(1)}) custom-call(bf16[2,1536,6144]{2,1,0:T(8,128)(2,1)} %bitcast.27, bf16[3,2,1536,128]{3,2,1,0:T(8,128)(2,1)S(1)} %bitcast.18, bf16[3,2,1536,128]{3,2,1,0:T(8,128)(2,1)S(1)} %collective-permute-done.partner_ref), custom_call_target="tpu_custom_call" | custom-call | flops 14495514624 | bytes 37748736 | tf_op jit(solution)/shard_map/near_product/pallas_call | solution.py:118
  75.7 7.1 %last_product.3 = (f32[13,32,128]{2,1,0:T(8,128)S(1)}, f32[13,32,128]{2,1,0:T(8,128)S(1)}, f32[13,32,128]{2,1,0:T(8,128)S(1)}, f32[13,32,128]{2,1,0:T(8,128)S(1)}) custom-call(bf16[2,1536,3072]{2,1,0:T(8,128)(2,1)S(1)} %get-tuple-element.31.g_ref, bf16[2,1536,128]{2,1,0:T(8,128)(2,1)S(1)} %collective-permute-done.1.left_ref, ...), custom_call_target="tpu_custom_call" | custom-call | flops 4831838208 | bytes 1572864 | tf_op jit(solution)/shard_map/last_product/pallas_call | solution.py:234
  84.7 2.6 %collective-permute-start.4 = (f32[13,32,128]{2,1,0:T(8,128)S(1)}, f32[13,32,128]{2,1,0:T(8,128)S(1)}, u32[]{:S(2)}, u32[]{:S(2)}) collective-permute-start(f32[13,32,128]{2,1,0:T(8,128)S(1)} %get-tuple-element.35), channel_id=1, source_target_pairs={{0,8},{4,12},{8,0},{12,4},{1,9},{5,13},{9,1},{13,5},{2,10},{6,14},... | collective-permute-start | bytes 638984 | tf_op jit(solution)/shard_map/ppermute | solution.py:26
  87.3 3.1 %far_product.2.acc_ref = f32[1536,256]{1,0:T(8,128)S(1)} custom-call(bf16[2,1536,3072]{2,1,0:T(8,128)(2,1)S(1)} %get-tuple-element.31.g_ref, bf16[2,768,128]{2,1,0:T(8,128)(2,1)S(1)} %collective-permute-done.8.left_ref, bf16[2,768,128]{2,1,0:T(8,128)(2,1)S(1)} %collective-permute-done.9.right_ref, f32[1536,256]{1,0:T(8,128)S(1)} %get-tuple-element.37.acc_ref), custom_call_target="tpu_custom_call" | custom-call | flops 2415919104 | bytes 1572864 | tf_op jit(solution)/shard_map/far_product/pallas_call | solution.py:158
  90.4 4.6 %last_product.4 = (bf16[13,32,128]{2,1,0:T(8,128)(2,1)S(1)}, bf16[13,32,128]{2,1,0:T(8,128)(2,1)S(1)}, bf16[13,32,128]{2,1,0:T(8,128)(2,1)S(1)}, bf16[13,32,128]{2,1,0:T(8,128)(2,1)S(1)}) custom-call(bf16[2,1536,3072]{2,1,0:T(8,128)(2,1)S(1)} %get-tuple-element.31.g_ref, bf16[2,768,128]{2,1,0:T(8,128)(2,1)S(1)} %collective-permute-done.6.left_ref, ...), custom_call_target="tpu_custom_call" | custom-call | flops 2415919104 | bytes 1572864 | tf_op jit(solution)/shard_map/last_product/pallas_call | solution.py:234
  96.0 3.0 %far_product.3.acc_ref = f32[1536,256]{1,0:T(8,128)S(1)} custom-call(bf16[2,1536,3072]{2,1,0:T(8,128)(2,1)S(1)} %get-tuple-element.31.g_ref, bf16[2,768,128]{2,1,0:T(8,128)(2,1)S(1)} %collective-permute-done.18.left_ref, bf16[2,768,128]{2,1,0:T(8,128)(2,1)S(1)} %collective-permute-done.19.right_ref, f32[1536,256]{1,0:T(8,128)S(1)} %get-tuple-element.45.acc_ref), custom_call_target="tpu_custom_call" | custom-call | flops 2415919104 | bytes 1572864 | tf_op jit(solution)/shard_map/far_product/pallas_call | solution.py:158
  99.0 3.5 %collective-permute-start.11 = (bf16[13,32,128]{2,1,0:T(8,128)(2,1)S(1)}, bf16[13,32,128]{2,1,0:T(8,128)(2,1)S(1)}, u32[]{:S(2)}, u32[]{:S(2)}) collective-permute-start(bf16[13,32,128]{2,1,0:T(8,128)(2,1)S(1)} %get-tuple-element.40), channel_id=1, source_target_pairs={{0,8},{4,12},{8,0},{12,4},{1,9},{5,13},{9,1},{13,5},{2,10},{6,14},... | collective-permute-start | bytes 319496 | tf_op jit(solution)/shard_map/ppermute | solution.py:26
  104.4 2.4 %collective-permute-start.12 = (bf16[13,32,128]{2,1,0:T(8,128)(2,1)S(1)}, bf16[13,32,128]{2,1,0:T(8,128)(2,1)S(1)}, u32[]{:S(2)}, u32[]{:S(2)}) collective-permute-start(bf16[13,32,128]{2,1,0:T(8,128)(2,1)S(1)} %get-tuple-element.41), channel_id=1, source_target_pairs={{0,12},{4,8},{8,4},{12,0},{1,13},{5,9},{9,5},{13,1},{2,14},{6,10},... | collective-permute-start | bytes 319496 | tf_op jit(solution)/shard_map/ppermute | solution.py:26
  106.8 4.6 %last_product.5 = (bf16[13,32,128]{2,1,0:T(8,128)(2,1)S(1)}, bf16[13,32,128]{2,1,0:T(8,128)(2,1)S(1)}, bf16[13,32,128]{2,1,0:T(8,128)(2,1)S(1)}, bf16[13,32,128]{2,1,0:T(8,128)(2,1)S(1)}) custom-call(bf16[2,1536,3072]{2,1,0:T(8,128)(2,1)S(1)} %get-tuple-element.31.g_ref, bf16[2,768,128]{2,1,0:T(8,128)(2,1)S(1)} %collective-permute-done.16.left_ref, ...), custom_call_target="tpu_custom_call" | custom-call | flops 2415919104 | bytes 1572864 | tf_op jit(solution)/shard_map/last_product/pallas_call | solution.py:234
  111.5 2.5 %collective-permute-done.11.refs_6_ = bf16[13,32,128]{2,1,0:T(8,128)(2,1)S(1)} collective-permute-done((bf16[13,32,128]{2,1,0:T(8,128)(2,1)S(1)}, bf16[13,32,128]{2,1,0:T(8,128)(2,1)S(1)}, u32[]{:S(2)}, u32[]{:S(2)}) %collective-permute-start.11) | collective-permute-done | bytes 106528 | tf_op jit(solution)/shard_map/ppermute | solution.py:26
  114.0 3.4 %collective-permute-start.21 = (bf16[13,32,128]{2,1,0:T(8,128)(2,1)S(1)}, bf16[13,32,128]{2,1,0:T(8,128)(2,1)S(1)}, u32[]{:S(2)}, u32[]{:S(2)}) collective-permute-start(bf16[13,32,128]{2,1,0:T(8,128)(2,1)S(1)} %get-tuple-element.48), channel_id=1, source_target_pairs={{0,8},{4,12},{8,0},{12,4},{1,9},{5,13},{9,1},{13,5},{2,10},{6,14},... | collective-permute-start | bytes 319496 | tf_op jit(solution)/shard_map/ppermute | solution.py:26
  120.2 5.4 %collective-permute-done.21.rest_2_ = bf16[13,32,128]{2,1,0:T(8,128)(2,1)S(1)} collective-permute-done((bf16[13,32,128]{2,1,0:T(8,128)(2,1)S(1)}, bf16[13,32,128]{2,1,0:T(8,128)(2,1)S(1)}, u32[]{:S(2)}, u32[]{:S(2)}) %collective-permute-start.21) | collective-permute-done | bytes 106528 | tf_op jit(solution)/shard_map/ppermute | solution.py:26
  128.1 2.1 %collective-permute-done.27.refs_2_ = bf16[4,32,128]{2,1,0:T(8,128)(2,1)S(1)} collective-permute-done((bf16[4,32,128]{2,1,0:T(8,128)(2,1)S(1)}, bf16[4,32,128]{2,1,0:T(8,128)(2,1)S(1)}, u32[]{:S(2)}, u32[]{:S(2)}) %collective-permute-start.27) | collective-permute-done | bytes 32800 | tf_op jit(solution)/shard_map/ppermute | solution.py:26
  134.8 2.1 %collective-permute-done.14.refs_2_ = f32[2,32,128]{2,1,0:T(8,128)S(1)} collective-permute-done((f32[2,32,128]{2,1,0:T(8,128)S(1)}, f32[2,32,128]{2,1,0:T(8,128)S(1)}, u32[]{:S(2)}, u32[]{:S(2)}) %collective-permute-start.14) | collective-permute-done | bytes 32800 | tf_op jit(solution)/shard_map/ppermute | solution.py:26
  137.7 1.9 %collective-permute-start.25 = (bf16[8,32,128]{2,1,0:T(8,128)(2,1)S(1)}, bf16[8,32,128]{2,1,0:T(8,128)(2,1)S(1)}, u32[]{:S(2)}, u32[]{:S(2)}) collective-permute-start(bf16[8,32,128]{2,1,0:T(8,128)(2,1)S(1)} %shard_map.121.rest_0_), channel_id=1, source_target_pairs={{0,8},{4,12},{8,0},{12,4},{1,9},{5,13},{9,1},{13,5},{2,10},{6,14},... | collective-permute-start | bytes 196616 | tf_op jit(solution)/shard_map/ppermute | solution.py:26
  139.6 2.1 %collective-permute-start.26 = (bf16[8,32,128]{2,1,0:T(8,128)(2,1)S(1)}, bf16[8,32,128]{2,1,0:T(8,128)(2,1)S(1)}, u32[]{:S(2)}, u32[]{:S(2)}) collective-permute-start(bf16[8,32,128]{2,1,0:T(8,128)(2,1)S(1)} %shard_map.121.rest_0_), channel_id=1, source_target_pairs={{0,12},{4,8},{8,4},{12,0},{1,13},{5,9},{9,5},{13,1},{2,14},{6,10},... | collective-permute-start | bytes 196616 | tf_op jit(solution)/shard_map/ppermute | solution.py:26
  143.5 7.5 %collective-permute-done.30.rest_6_ = bf16[7,32,128]{2,1,0:T(8,128)(2,1)S(1)} collective-permute-done((bf16[7,32,128]{2,1,0:T(8,128)(2,1)S(1)}, bf16[7,32,128]{2,1,0:T(8,128)(2,1)S(1)}, u32[]{:S(2)}, u32[]{:S(2)}) %collective-permute-start.30) | collective-permute-done | bytes 57376 | tf_op jit(solution)/shard_map/ppermute | solution.py:26
  151.1 2.2 %tile_stage.1 = (f32[8,128]{1,0:T(8,128)}, f32[8,128]{1,0:T(8,128)}, f32[3,4,32,128]{3,2,1,0:T(8,128)}) custom-call(s32[18,32]{1,0:T(8,128)S(1)} %get-tuple-element.30.plan_ref, bf16[8,8,128,128]{3,2,1,0:T(8,128)(2,1)S(1)} %copy-done.2, bf16[8,3,128,128]{3,2,1,0:T(8,128)(2,1)S(1)} %copy-done.3, f32[8,128]{1,0:T(8,128)S(1)} %copy-done.5, ...), custom_call_target="tpu_custom_call" | custom-call | tf_op jit(solution)/shard_map/tile_stage/pallas_call | solution.py:474
  (73 shorter events, 22.4 us)
Async XLA Ops:
  0.6 57.0 %collective-permute-start = (bf16[3,2,1536,128]{3,2,1,0:T(8,128)(2,1)}, bf16[3,2,1536,128]{3,2,1,0:T(8,128)(2,1)S(1)}, u32[]{:S(2)}, u32[]{:S(2)}) collective-permute-start(bf16[3,2,1536,128]{3,2,1,0:T(8,128)(2,1)} %bitcast.16), channel_id=1, source_target_pairs={{0,1},{1,0},{2,3},{3,2},{4,5},{5,4},{6,7},{7,6},{8,9},{9,8},{10,11... | collective-permute-start | bytes 7077896 | tf_op jit(solution)/shard_map/ppermute | solution.py:26
  2.8 12.5 %collective-permute-start.6 = (bf16[2,768,128]{2,1,0:T(8,128)(2,1)S(1)}, bf16[2,768,128]{2,1,0:T(8,128)(2,1)S(1)}, u32[]{:S(2)}, u32[]{:S(2)}) collective-permute-start(bf16[2,768,128]{2,1,0:T(8,128)(2,1)S(1)} %get-tuple-element.60), channel_id=1, source_target_pairs={{0,2},{1,3},{2,0},{3,1},{4,6},{5,7},{6,4},{7,5},{8,10},{9,11},{10,... | collective-permute-start | bytes 1179656 | tf_op jit(solution)/shard_map/ppermute | solution.py:26
  5.4 51.7 %collective-permute-start.1 = (bf16[2,1536,128]{2,1,0:T(8,128)(2,1)S(1)}, bf16[2,1536,128]{2,1,0:T(8,128)(2,1)S(1)}, u32[]{:S(2)}, u32[]{:S(2)}) collective-permute-start(bf16[2,1536,128]{2,1,0:T(8,128)(2,1)S(1)} %slice_bitcast_fusion), channel_id=1, source_target_pairs={{0,2},{1,3},{2,0},{3,1},{4,6},{5,7},{6,4},{7,5},{8,10},{9,11},{10,... | collective-permute-start | bytes 2359304 | tf_op jit(solution)/shard_map/ppermute | solution.py:26
  5.9 34.8 %collective-permute-start.8 = (bf16[2,768,128]{2,1,0:T(8,128)(2,1)S(1)}, bf16[2,768,128]{2,1,0:T(8,128)(2,1)S(1)}, u32[]{:S(2)}, u32[]{:S(2)}) collective-permute-start(bf16[2,768,128]{2,1,0:T(8,128)(2,1)S(1)} %get-tuple-element.59), channel_id=1, source_target_pairs={{0,2},{1,3},{2,0},{3,1},{4,6},{5,7},{6,4},{7,5},{8,10},{9,11},{10,... | collective-permute-start | bytes 1179656 | tf_op jit(solution)/shard_map/ppermute | solution.py:26
  7.5 41.5 %collective-permute-start.16 = (bf16[2,768,128]{2,1,0:T(8,128)(2,1)S(1)}, bf16[2,768,128]{2,1,0:T(8,128)(2,1)S(1)}, u32[]{:S(2)}, u32[]{:S(2)}) collective-permute-start(bf16[2,768,128]{2,1,0:T(8,128)(2,1)S(1)} %get-tuple-element.58), channel_id=1, source_target_pairs={{0,2},{1,3},{2,0},{3,1},{4,6},{5,7},{6,4},{7,5},{8,10},{9,11},{10,... | collective-permute-start | bytes 1179656 | tf_op jit(solution)/shard_map/ppermute | solution.py:26
  15.3 41.8 %collective-permute-start.18 = (bf16[2,768,128]{2,1,0:T(8,128)(2,1)S(1)}, bf16[2,768,128]{2,1,0:T(8,128)(2,1)S(1)}, u32[]{:S(2)}, u32[]{:S(2)}) collective-permute-start(bf16[2,768,128]{2,1,0:T(8,128)(2,1)S(1)} %get-tuple-element.57), channel_id=1, source_target_pairs={{0,2},{1,3},{2,0},{3,1},{4,6},{5,7},{6,4},{7,5},{8,10},{9,11},{10,... | collective-permute-start | bytes 1179656 | tf_op jit(solution)/shard_map/ppermute | solution.py:26
  40.6 49.7 %collective-permute-start.7 = (bf16[2,768,128]{2,1,0:T(8,128)(2,1)S(1)}, bf16[2,768,128]{2,1,0:T(8,128)(2,1)S(1)}, u32[]{:S(2)}, u32[]{:S(2)}) collective-permute-start(bf16[2,768,128]{2,1,0:T(8,128)(2,1)S(1)} %collective-permute-done.6.left_ref), channel_id=1, source_target_pairs={{0,1},{1,0},{2,3},{3,2},{4,5},{5,4},{6,7},{7,6},{8,9},{9,8},{10,11... | collective-permute-start | bytes 1179656 | tf_op jit(solution)/shard_map/ppermute | solution.py:26
  49.0 35.6 %collective-permute-start.9 = (bf16[2,768,128]{2,1,0:T(8,128)(2,1)S(1)}, bf16[2,768,128]{2,1,0:T(8,128)(2,1)S(1)}, u32[]{:S(2)}, u32[]{:S(2)}) collective-permute-start(bf16[2,768,128]{2,1,0:T(8,128)(2,1)S(1)} %collective-permute-done.8.left_ref), channel_id=1, source_target_pairs={{0,1},{1,0},{2,3},{3,2},{4,5},{5,4},{6,7},{7,6},{8,9},{9,8},{10,11... | collective-permute-start | bytes 1179656 | tf_op jit(solution)/shard_map/ppermute | solution.py:26
  57.1 41.9 %collective-permute-start.17 = (bf16[2,768,128]{2,1,0:T(8,128)(2,1)S(1)}, bf16[2,768,128]{2,1,0:T(8,128)(2,1)S(1)}, u32[]{:S(2)}, u32[]{:S(2)}) collective-permute-start(bf16[2,768,128]{2,1,0:T(8,128)(2,1)S(1)} %collective-permute-done.16.left_ref), channel_id=1, source_target_pairs={{0,1},{1,0},{2,3},{3,2},{4,5},{5,4},{6,7},{7,6},{8,9},{9,8},{10,11... | collective-permute-start | bytes 1179656 | tf_op jit(solution)/shard_map/ppermute | solution.py:26
  57.1 37.9 %collective-permute-start.19 = (bf16[2,768,128]{2,1,0:T(8,128)(2,1)S(1)}, bf16[2,768,128]{2,1,0:T(8,128)(2,1)S(1)}, u32[]{:S(2)}, u32[]{:S(2)}) collective-permute-start(bf16[2,768,128]{2,1,0:T(8,128)(2,1)S(1)} %collective-permute-done.18.left_ref), channel_id=1, source_target_pairs={{0,1},{1,0},{2,3},{3,2},{4,5},{5,4},{6,7},{7,6},{8,9},{9,8},{10,11... | collective-permute-start | bytes 1179656 | tf_op jit(solution)/shard_map/ppermute | solution.py:26
  57.6 18.0 %collective-permute-start.2 = (bf16[2,1536,128]{2,1,0:T(8,128)(2,1)S(1)}, bf16[2,1536,128]{2,1,0:T(8,128)(2,1)S(1)}, u32[]{:S(2)}, u32[]{:S(2)}) collective-permute-start(bf16[2,1536,128]{2,1,0:T(8,128)(2,1)S(1)} %collective-permute-done.1.left_ref), channel_id=1, source_target_pairs={{0,1},{1,0},{2,3},{3,2},{4,5},{5,4},{6,7},{7,6},{8,9},{9,8},{10,11... | collective-permute-start | bytes 2359304 | tf_op jit(solution)/shard_map/ppermute | solution.py:26
  82.8 34.6 %collective-permute-start.3 = (f32[13,32,128]{2,1,0:T(8,128)S(1)}, f32[13,32,128]{2,1,0:T(8,128)S(1)}, u32[]{:S(2)}, u32[]{:S(2)}) collective-permute-start(f32[13,32,128]{2,1,0:T(8,128)S(1)} %get-tuple-element.34), channel_id=1, source_target_pairs={{0,4},{4,0},{8,12},{12,8},{1,5},{5,1},{9,13},{13,9},{2,6},{6,2},{1... | collective-permute-start | bytes 638984 | tf_op jit(solution)/shard_map/ppermute | solution.py:26
  84.7 35.2 %collective-permute-start.4 = (f32[13,32,128]{2,1,0:T(8,128)S(1)}, f32[13,32,128]{2,1,0:T(8,128)S(1)}, u32[]{:S(2)}, u32[]{:S(2)}) collective-permute-start(f32[13,32,128]{2,1,0:T(8,128)S(1)} %get-tuple-element.35), channel_id=1, source_target_pairs={{0,8},{4,12},{8,0},{12,4},{1,9},{5,13},{9,1},{13,5},{2,10},{6,14},... | collective-permute-start | bytes 638984 | tf_op jit(solution)/shard_map/ppermute | solution.py:26
  90.3 29.6 %collective-permute-start.5 = (f32[13,32,128]{2,1,0:T(8,128)S(1)}, f32[13,32,128]{2,1,0:T(8,128)S(1)}, u32[]{:S(2)}, u32[]{:S(2)}) collective-permute-start(f32[13,32,128]{2,1,0:T(8,128)S(1)} %get-tuple-element.36), channel_id=1, source_target_pairs={{0,12},{4,8},{8,4},{12,0},{1,13},{5,9},{9,5},{13,1},{2,14},{6,10},... | collective-permute-start | bytes 638984 | tf_op jit(solution)/shard_map/ppermute | solution.py:26
  95.1 9.3 %collective-permute-start.10 = (bf16[13,32,128]{2,1,0:T(8,128)(2,1)S(1)}, bf16[13,32,128]{2,1,0:T(8,128)(2,1)S(1)}, u32[]{:S(2)}, u32[]{:S(2)}) collective-permute-start(bf16[13,32,128]{2,1,0:T(8,128)(2,1)S(1)} %get-tuple-element.39), channel_id=1, source_target_pairs={{0,4},{4,0},{8,12},{12,8},{1,5},{5,1},{9,13},{13,9},{2,6},{6,2},{1... | collective-permute-start | bytes 319496 | tf_op jit(solution)/shard_map/ppermute | solution.py:26
  99.0 15.0 %collective-permute-start.11 = (bf16[13,32,128]{2,1,0:T(8,128)(2,1)S(1)}, bf16[13,32,128]{2,1,0:T(8,128)(2,1)S(1)}, u32[]{:S(2)}, u32[]{:S(2)}) collective-permute-start(bf16[13,32,128]{2,1,0:T(8,128)(2,1)S(1)} %get-tuple-element.40), channel_id=1, source_target_pairs={{0,8},{4,12},{8,0},{12,4},{1,9},{5,13},{9,1},{13,5},{2,10},{6,14},... | collective-permute-start | bytes 319496 | tf_op jit(solution)/shard_map/ppermute | solution.py:26
  104.4 9.6 %collective-permute-start.12 = (bf16[13,32,128]{2,1,0:T(8,128)(2,1)S(1)}, bf16[13,32,128]{2,1,0:T(8,128)(2,1)S(1)}, u32[]{:S(2)}, u32[]{:S(2)}) collective-permute-start(bf16[13,32,128]{2,1,0:T(8,128)(2,1)S(1)} %get-tuple-element.41), channel_id=1, source_target_pairs={{0,12},{4,8},{8,4},{12,0},{1,13},{5,9},{9,5},{13,1},{2,14},{6,10},... | collective-permute-start | bytes 319496 | tf_op jit(solution)/shard_map/ppermute | solution.py:26
  114.0 11.5 %collective-permute-start.21 = (bf16[13,32,128]{2,1,0:T(8,128)(2,1)S(1)}, bf16[13,32,128]{2,1,0:T(8,128)(2,1)S(1)}, u32[]{:S(2)}, u32[]{:S(2)}) collective-permute-start(bf16[13,32,128]{2,1,0:T(8,128)(2,1)S(1)} %get-tuple-element.48), channel_id=1, source_target_pairs={{0,8},{4,12},{8,0},{12,4},{1,9},{5,13},{9,1},{13,5},{2,10},{6,14},... | collective-permute-start | bytes 319496 | tf_op jit(solution)/shard_map/ppermute | solution.py:26
  131.2 10.5 %collective-permute-start.29 = (bf16[7,32,128]{2,1,0:T(8,128)(2,1)S(1)}, bf16[7,32,128]{2,1,0:T(8,128)(2,1)S(1)}, u32[]{:S(2)}, u32[]{:S(2)}) collective-permute-start(bf16[7,32,128]{2,1,0:T(8,128)(2,1)S(1)} %shard_map.122.rest_4_), channel_id=1, source_target_pairs={{0,4},{4,0},{8,12},{12,8},{1,5},{5,1},{9,13},{13,9},{2,6},{6,2},{1... | collective-permute-start | bytes 172040 | tf_op jit(solution)/shard_map/ppermute | solution.py:26
  137.3 13.7 %collective-permute-start.24 = (bf16[8,32,128]{2,1,0:T(8,128)(2,1)S(1)}, bf16[8,32,128]{2,1,0:T(8,128)(2,1)S(1)}, u32[]{:S(2)}, u32[]{:S(2)}) collective-permute-start(bf16[8,32,128]{2,1,0:T(8,128)(2,1)S(1)} %shard_map.121.rest_0_), channel_id=1, source_target_pairs={{0,4},{4,0},{8,12},{12,8},{1,5},{5,1},{9,13},{13,9},{2,6},{6,2},{1... | collective-permute-start | bytes 196616 | tf_op jit(solution)/shard_map/ppermute | solution.py:26
  137.7 13.3 %collective-permute-start.25 = (bf16[8,32,128]{2,1,0:T(8,128)(2,1)S(1)}, bf16[8,32,128]{2,1,0:T(8,128)(2,1)S(1)}, u32[]{:S(2)}, u32[]{:S(2)}) collective-permute-start(bf16[8,32,128]{2,1,0:T(8,128)(2,1)S(1)} %shard_map.121.rest_0_), channel_id=1, source_target_pairs={{0,8},{4,12},{8,0},{12,4},{1,9},{5,13},{9,1},{13,5},{2,10},{6,14},... | collective-permute-start | bytes 196616 | tf_op jit(solution)/shard_map/ppermute | solution.py:26
  139.6 11.4 %collective-permute-start.26 = (bf16[8,32,128]{2,1,0:T(8,128)(2,1)S(1)}, bf16[8,32,128]{2,1,0:T(8,128)(2,1)S(1)}, u32[]{:S(2)}, u32[]{:S(2)}) collective-permute-start(bf16[8,32,128]{2,1,0:T(8,128)(2,1)S(1)} %shard_map.121.rest_0_), channel_id=1, source_target_pairs={{0,12},{4,8},{8,4},{12,0},{1,13},{5,9},{9,5},{13,1},{2,14},{6,10},... | collective-permute-start | bytes 196616 | tf_op jit(solution)/shard_map/ppermute | solution.py:26
  141.7 9.3 %collective-permute-start.30 = (bf16[7,32,128]{2,1,0:T(8,128)(2,1)S(1)}, bf16[7,32,128]{2,1,0:T(8,128)(2,1)S(1)}, u32[]{:S(2)}, u32[]{:S(2)}) collective-permute-start(bf16[7,32,128]{2,1,0:T(8,128)(2,1)S(1)} %shard_map.122.rest_4_), channel_id=1, source_target_pairs={{0,8},{4,12},{8,0},{12,4},{1,9},{5,13},{9,1},{13,5},{2,10},{6,14},... | collective-permute-start | bytes 172040 | tf_op jit(solution)/shard_map/ppermute | solution.py:26
  141.7 9.3 %collective-permute-start.31 = (bf16[7,32,128]{2,1,0:T(8,128)(2,1)S(1)}, bf16[7,32,128]{2,1,0:T(8,128)(2,1)S(1)}, u32[]{:S(2)}, u32[]{:S(2)}) collective-permute-start(bf16[7,32,128]{2,1,0:T(8,128)(2,1)S(1)} %shard_map.122.rest_4_), channel_id=1, source_target_pairs={{0,12},{4,8},{8,4},{12,0},{1,13},{5,9},{9,5},{13,1},{2,14},{6,10},... | collective-permute-start | bytes 172040 | tf_op jit(solution)/shard_map/ppermute | solution.py:26
  (17 other events, 239.9 us)

commit v5 on v4

--- a/solution.py
+++ b/solution.py
@@ -33,7 +33,7 @@
 
 
 def row_block(rows):
-    for size in (512, 384, 256, 128):
+    for size in (768, 512, 384, 256, 128):
         if rows % size == 0:
             return size
     return rows
@@ -131,7 +131,6 @@
         cost_estimate=pl.CostEstimate(
             flops=2 * 8 * rows * rows * panels * width, bytes_accessed=4 * rows * order, transcendentals=0
         ),
-        name="near_product",
     )(matrix, own, partner)
     return list(results[:-1]), results[-1]
 
@@ -170,7 +169,6 @@
         cost_estimate=pl.CostEstimate(
             flops=2 * 8 * rows * depth * width, bytes_accessed=8 * rows * width, transcendentals=0
         ),
-        name="far_product",
     )(g, left, right, acc)
 
 
@@ -204,7 +202,8 @@
         )
         return both[:, :width] + both[:, width:]
 
-    part = (cross(own_ref[0], density) + cross(own_ref[1], other)).reshape(d_ref.shape)
+    lower = jnp.concatenate([own_ref[0], own_ref[1]], axis=0)
+    part = cross(lower, jnp.concatenate([density, other], axis=0)).reshape(d_ref.shape)
 
     @pl.when(m == 0)
     def _():
@@ -253,7 +252,6 @@
         cost_estimate=pl.CostEstimate(
             flops=2 * 8 * rows * depth * width, bytes_accessed=8 * rows * width, transcendentals=0
         ),
-        name="last_product",
     )(g, left, right, acc, own, diag, weights)
 
 
@@ -323,7 +321,6 @@
         ],
         compiler_params=pltpu.CompilerParams(vmem_limit_bytes=LIMIT),
         cost_estimate=pl.CostEstimate(flops=1 << 20, bytes_accessed=1 << 20, transcendentals=0),
-        name="tables",
     )(order, supports.T, counts.reshape(1, tiles))
 
 
@@ -353,7 +350,6 @@
         ],
         compiler_params=pltpu.CompilerParams(vmem_limit_bytes=LIMIT),
         cost_estimate=pl.CostEstimate(flops=1 << 20, bytes_accessed=2 << 20, transcendentals=0),
-        name="settle",
     )(*[part for group in groups for part in group])
 
 
@@ -380,7 +376,6 @@
         out_shape=[jax.ShapeDtypeStruct((CAP + 1, depth, width), BF16)] * cols,
         scratch_shapes=[pltpu.VMEM((early.shape[0] + blocks, depth, width), BF16)],
         compiler_params=pltpu.CompilerParams(vmem_limit_bytes=LIMIT),
-        name="pick",
     )(send, early, *parts)
 
 
@@ -421,7 +416,6 @@
         out_specs=VMEM,
         out_shape=jax.ShapeDtypeStruct(parts[0].shape, F32),
         compiler_params=pltpu.CompilerParams(vmem_limit_bytes=LIMIT),
-        name="add",
     )(*parts)
 
 
@@ -487,7 +481,6 @@
             pltpu.SemaphoreType.DMA(()),
         ],
         compiler_params=pltpu.CompilerParams(vmem_limit_bytes=LIMIT),
-        name="tile_stage",
     )(plan, rows, orbitals, core, *near_parts, *far_parts)
     return valence, potential, diag.reshape(panels, width, width)
 

time: 153 us -> 153 us (level)
  transfers between devices with their start and end apart: 32 -> 32, of which waited for: 13 -> 13; matrix products, arithmetic and copies ran while one was open for 1% -> 1% of each run, Pallas kernels for 27% -> 26%
where the time goes in v5:
time: 153 us
  waiting for transfers between devices  70.8 us (46%)
  Pallas kernels  43.1 us (28%)
  starting transfers between devices  36.3 us (24%)
  local copies, waits for them, and re-layouts  1.69 us (1%)
    ppermute x32, waiting for transfers between devices, swap(): return lax.ppermute(value, axis, [(i, i ^ mask) for i in range(size)])  70.8 us
    ppermute x32, starting transfers between devices, swap(): return lax.ppermute(value, axis, [(i, i ^ mask) for i in range(size)])  36.3 us
    pallas_call x1, Pallas kernels, near_product(): pl.pallas_call(near_kernel, grid=(rows // tile,), in_specs=[pl.BlockSpec(...  17.9 us
    pallas_call x3, Pallas kernels, last_product(): pl.pallas_call(functools.partial(last_kernel, poles, step, offset), grid=...  15.4 us
    pallas_call x2, Pallas kernels, far_product(): pl.pallas_call(functools.partial(far_kernel, step, offset), grid=(rows //...  5.61 us
  transfers between devices with their start and end apart: 32, of which 13 were waited for; matrix products, arithmetic and copies ran while one was open for 1% of the time, Pallas kernels for 26%

profile of v5, /device:TPU:0, one launch (start us, length us, event | category | flops | bytes accessed | tf_op | source)
XLA Modules:
  0.0 153.1 jit_solution(13838906898001050582)
XLA Ops:
  2.8 2.6 %collective-permute-start.6 = (bf16[2,768,128]{2,1,0:T(8,128)(2,1)S(1)}, bf16[2,768,128]{2,1,0:T(8,128)(2,1)S(1)}, u32[]{:S(2)}, u32[]{:S(2)}) collective-permute-start(bf16[2,768,128]{2,1,0:T(8,128)(2,1)S(1)} %get-tuple-element.60), channel_id=1, source_target_pairs={{0,2},{1,3},{2,0},{3,1},{4,6},{5,7},{6,4},{7,5},{8,10},{9,11},{10,... | collective-permute-start | bytes 1179656 | tf_op jit(solution)/shard_map/ppermute | solution.py:26
  7.9 7.5 %collective-permute-done.6.left_ref = bf16[2,768,128]{2,1,0:T(8,128)(2,1)S(1)} collective-permute-done((bf16[2,768,128]{2,1,0:T(8,128)(2,1)S(1)}, bf16[2,768,128]{2,1,0:T(8,128)(2,1)S(1)}, u32[]{:S(2)}, u32[]{:S(2)}) %collective-permute-start.6) | collective-permute-done | bytes 393248 | tf_op jit(solution)/shard_map/ppermute | solution.py:26
  15.3 2.0 %collective-permute-start.18 = (bf16[2,768,128]{2,1,0:T(8,128)(2,1)S(1)}, bf16[2,768,128]{2,1,0:T(8,128)(2,1)S(1)}, u32[]{:S(2)}, u32[]{:S(2)}) collective-permute-start(bf16[2,768,128]{2,1,0:T(8,128)(2,1)S(1)} %get-tuple-element.57), channel_id=1, source_target_pairs={{0,2},{1,3},{2,0},{3,1},{4,6},{5,7},{6,4},{7,5},{8,10},{9,11},{10,... | collective-permute-start | bytes 1179656 | tf_op jit(solution)/shard_map/ppermute | solution.py:26
  17.4 23.3 %collective-permute-done.8.left_ref = bf16[2,768,128]{2,1,0:T(8,128)(2,1)S(1)} collective-permute-done((bf16[2,768,128]{2,1,0:T(8,128)(2,1)S(1)}, bf16[2,768,128]{2,1,0:T(8,128)(2,1)S(1)}, u32[]{:S(2)}, u32[]{:S(2)}) %collective-permute-start.8) | collective-permute-done | bytes 393248 | tf_op jit(solution)/shard_map/ppermute | solution.py:26
  40.6 8.4 %collective-permute-done.16.left_ref = bf16[2,768,128]{2,1,0:T(8,128)(2,1)S(1)} collective-permute-done((bf16[2,768,128]{2,1,0:T(8,128)(2,1)S(1)}, bf16[2,768,128]{2,1,0:T(8,128)(2,1)S(1)}, u32[]{:S(2)}, u32[]{:S(2)}) %collective-permute-start.16) | collective-permute-done | bytes 393248 | tf_op jit(solution)/shard_map/ppermute | solution.py:26
  49.1 8.1 %collective-permute-done.18.left_ref = bf16[2,768,128]{2,1,0:T(8,128)(2,1)S(1)} collective-permute-done((bf16[2,768,128]{2,1,0:T(8,128)(2,1)S(1)}, bf16[2,768,128]{2,1,0:T(8,128)(2,1)S(1)}, u32[]{:S(2)}, u32[]{:S(2)}) %collective-permute-start.18) | collective-permute-done | bytes 393248 | tf_op jit(solution)/shard_map/ppermute | solution.py:26
  57.7 17.9 %shard_map.122 = (f32[1536,256]{1,0:T(8,128)S(1)}, f32[1536,256]{1,0:T(8,128)S(1)}, f32[1536,256]{1,0:T(8,128)S(1)}, bf16[2,1536,3072]{2,1,0:T(8,128)(2,1)S(1)}) custom-call(bf16[2,1536,6144]{2,1,0:T(8,128)(2,1)} %bitcast.27, bf16[3,2,1536,128]{3,2,1,0:T(8,128)(2,1)S(1)} %bitcast.18, bf16[3,2,1536,128]{3,2,1,0:T(8,128)(2,1)S(1)} %collective-permute-done.partner_ref), custom_call_target="tpu_custom_call" | custom-call | flops 14495514624 | bytes 37748736 | tf_op jit(solution)/shard_map/pallas_call | solution.py:118
  75.7 6.7 %shard_map.123 = (f32[13,32,128]{2,1,0:T(8,128)S(1)}, f32[13,32,128]{2,1,0:T(8,128)S(1)}, f32[13,32,128]{2,1,0:T(8,128)S(1)}, f32[13,32,128]{2,1,0:T(8,128)S(1)}) custom-call(bf16[2,1536,3072]{2,1,0:T(8,128)(2,1)S(1)} %get-tuple-element.31.g_ref, bf16[2,1536,128]{2,1,0:T(8,128)(2,1)S(1)} %collective-permute-done.1.left_ref, ...), custom_call_target="tpu_custom_call" | custom-call | flops 4831838208 | bytes 1572864 | tf_op jit(solution)/shard_map/pallas_call | solution.py:233
  84.3 2.6 %collective-permute-start.4 = (f32[13,32,128]{2,1,0:T(8,128)S(1)}, f32[13,32,128]{2,1,0:T(8,128)S(1)}, u32[]{:S(2)}, u32[]{:S(2)}) collective-permute-start(f32[13,32,128]{2,1,0:T(8,128)S(1)} %get-tuple-element.35), channel_id=1, source_target_pairs={{0,8},{4,12},{8,0},{12,4},{1,9},{5,13},{9,1},{13,5},{2,10},{6,14},... | collective-permute-start | bytes 638984 | tf_op jit(solution)/shard_map/ppermute | solution.py:26
  86.9 2.8 %shard_map.124.acc_ref = f32[1536,256]{1,0:T(8,128)S(1)} custom-call(bf16[2,1536,3072]{2,1,0:T(8,128)(2,1)S(1)} %get-tuple-element.31.g_ref, bf16[2,768,128]{2,1,0:T(8,128)(2,1)S(1)} %collective-permute-done.8.left_ref, bf16[2,768,128]{2,1,0:T(8,128)(2,1)S(1)} %collective-permute-done.9.right_ref, f32[1536,256]{1,0:T(8,128)S(1)} %get-tuple-element.37.acc_ref), custom_call_target="tpu_custom_call" | custom-call | flops 2415919104 | bytes 1572864 | tf_op jit(solution)/shard_map/pallas_call | solution.py:157
  89.8 4.3 %shard_map.125 = (bf16[13,32,128]{2,1,0:T(8,128)(2,1)S(1)}, bf16[13,32,128]{2,1,0:T(8,128)(2,1)S(1)}, bf16[13,32,128]{2,1,0:T(8,128)(2,1)S(1)}, bf16[13,32,128]{2,1,0:T(8,128)(2,1)S(1)}) custom-call(bf16[2,1536,3072]{2,1,0:T(8,128)(2,1)S(1)} %get-tuple-element.31.g_ref, bf16[2,768,128]{2,1,0:T(8,128)(2,1)S(1)} %collective-permute-done.6.left_ref, ...), custom_call_target="tpu_custom_call" | custom-call | flops 2415919104 | bytes 1572864 | tf_op jit(solution)/shard_map/pallas_call | solution.py:233
  95.0 2.8 %shard_map.128.acc_ref = f32[1536,256]{1,0:T(8,128)S(1)} custom-call(bf16[2,1536,3072]{2,1,0:T(8,128)(2,1)S(1)} %get-tuple-element.31.g_ref, bf16[2,768,128]{2,1,0:T(8,128)(2,1)S(1)} %collective-permute-done.18.left_ref, bf16[2,768,128]{2,1,0:T(8,128)(2,1)S(1)} %collective-permute-done.19.right_ref, f32[1536,256]{1,0:T(8,128)S(1)} %get-tuple-element.45.acc_ref), custom_call_target="tpu_custom_call" | custom-call | flops 2415919104 | bytes 1572864 | tf_op jit(solution)/shard_map/pallas_call | solution.py:157
  97.8 3.5 %collective-permute-start.11 = (bf16[13,32,128]{2,1,0:T(8,128)(2,1)S(1)}, bf16[13,32,128]{2,1,0:T(8,128)(2,1)S(1)}, u32[]{:S(2)}, u32[]{:S(2)}) collective-permute-start(bf16[13,32,128]{2,1,0:T(8,128)(2,1)S(1)} %get-tuple-element.40), channel_id=1, source_target_pairs={{0,8},{4,12},{8,0},{12,4},{1,9},{5,13},{9,1},{13,5},{2,10},{6,14},... | collective-permute-start | bytes 319496 | tf_op jit(solution)/shard_map/ppermute | solution.py:26
  101.4 2.4 %collective-permute-done.10.refs_5_ = bf16[13,32,128]{2,1,0:T(8,128)(2,1)S(1)} collective-permute-done((bf16[13,32,128]{2,1,0:T(8,128)(2,1)S(1)}, bf16[13,32,128]{2,1,0:T(8,128)(2,1)S(1)}, u32[]{:S(2)}, u32[]{:S(2)}) %collective-permute-start.10) | collective-permute-done | bytes 106528 | tf_op jit(solution)/shard_map/ppermute | solution.py:26
  103.7 2.7 %collective-permute-start.12 = (bf16[13,32,128]{2,1,0:T(8,128)(2,1)S(1)}, bf16[13,32,128]{2,1,0:T(8,128)(2,1)S(1)}, u32[]{:S(2)}, u32[]{:S(2)}) collective-permute-start(bf16[13,32,128]{2,1,0:T(8,128)(2,1)S(1)} %get-tuple-element.41), channel_id=1, source_target_pairs={{0,12},{4,8},{8,4},{12,0},{1,13},{5,9},{9,5},{13,1},{2,14},{6,10},... | collective-permute-start | bytes 319496 | tf_op jit(solution)/shard_map/ppermute | solution.py:26
  106.4 4.4 %shard_map.129 = (bf16[13,32,128]{2,1,0:T(8,128)(2,1)S(1)}, bf16[13,32,128]{2,1,0:T(8,128)(2,1)S(1)}, bf16[13,32,128]{2,1,0:T(8,128)(2,1)S(1)}, bf16[13,32,128]{2,1,0:T(8,128)(2,1)S(1)}) custom-call(bf16[2,1536,3072]{2,1,0:T(8,128)(2,1)S(1)} %get-tuple-element.31.g_ref, bf16[2,768,128]{2,1,0:T(8,128)(2,1)S(1)} %collective-permute-done.16.left_ref, ...), custom_call_target="tpu_custom_call" | custom-call | flops 2415919104 | bytes 1572864 | tf_op jit(solution)/shard_map/pallas_call | solution.py:233
  110.9 2.8 %collective-permute-done.11.refs_6_ = bf16[13,32,128]{2,1,0:T(8,128)(2,1)S(1)} collective-permute-done((bf16[13,32,128]{2,1,0:T(8,128)(2,1)S(1)}, bf16[13,32,128]{2,1,0:T(8,128)(2,1)S(1)}, u32[]{:S(2)}, u32[]{:S(2)}) %collective-permute-start.11) | collective-permute-done | bytes 106528 | tf_op jit(solution)/shard_map/ppermute | solution.py:26
  113.7 3.3 %collective-permute-start.21 = (bf16[13,32,128]{2,1,0:T(8,128)(2,1)S(1)}, bf16[13,32,128]{2,1,0:T(8,128)(2,1)S(1)}, u32[]{:S(2)}, u32[]{:S(2)}) collective-permute-start(bf16[13,32,128]{2,1,0:T(8,128)(2,1)S(1)} %get-tuple-element.48), channel_id=1, source_target_pairs={{0,8},{4,12},{8,0},{12,4},{1,9},{5,13},{9,1},{13,5},{2,10},{6,14},... | collective-permute-start | bytes 319496 | tf_op jit(solution)/shard_map/ppermute | solution.py:26
  119.7 5.4 %collective-permute-done.21.rest_2_ = bf16[13,32,128]{2,1,0:T(8,128)(2,1)S(1)} collective-permute-done((bf16[13,32,128]{2,1,0:T(8,128)(2,1)S(1)}, bf16[13,32,128]{2,1,0:T(8,128)(2,1)S(1)}, u32[]{:S(2)}, u32[]{:S(2)}) %collective-permute-start.21) | collective-permute-done | bytes 106528 | tf_op jit(solution)/shard_map/ppermute | solution.py:26
  127.7 2.1 %collective-permute-done.27.refs_2_ = bf16[4,32,128]{2,1,0:T(8,128)(2,1)S(1)} collective-permute-done((bf16[4,32,128]{2,1,0:T(8,128)(2,1)S(1)}, bf16[4,32,128]{2,1,0:T(8,128)(2,1)S(1)}, u32[]{:S(2)}, u32[]{:S(2)}) %collective-permute-start.27) | collective-permute-done | bytes 32800 | tf_op jit(solution)/shard_map/ppermute | solution.py:26
  134.4 2.1 %collective-permute-done.14.refs_2_ = f32[2,32,128]{2,1,0:T(8,128)S(1)} collective-permute-done((f32[2,32,128]{2,1,0:T(8,128)S(1)}, f32[2,32,128]{2,1,0:T(8,128)S(1)}, u32[]{:S(2)}, u32[]{:S(2)}) %collective-permute-start.14) | collective-permute-done | bytes 32800 | tf_op jit(solution)/shard_map/ppermute | solution.py:26
  139.1 2.2 %collective-permute-start.26 = (bf16[8,32,128]{2,1,0:T(8,128)(2,1)S(1)}, bf16[8,32,128]{2,1,0:T(8,128)(2,1)S(1)}, u32[]{:S(2)}, u32[]{:S(2)}) collective-permute-start(bf16[8,32,128]{2,1,0:T(8,128)(2,1)S(1)} %shard_map.131.rest_0_), channel_id=1, source_target_pairs={{0,12},{4,8},{8,4},{12,0},{1,13},{5,9},{9,5},{13,1},{2,14},{6,10},... | collective-permute-start | bytes 196616 | tf_op jit(solution)/shard_map/ppermute | solution.py:26
  143.1 7.5 %collective-permute-done.30.rest_6_ = bf16[7,32,128]{2,1,0:T(8,128)(2,1)S(1)} collective-permute-done((bf16[7,32,128]{2,1,0:T(8,128)(2,1)S(1)}, bf16[7,32,128]{2,1,0:T(8,128)(2,1)S(1)}, u32[]{:S(2)}, u32[]{:S(2)}) %collective-permute-start.30) | collective-permute-done | bytes 57376 | tf_op jit(solution)/shard_map/ppermute | solution.py:26
  150.7 2.2 %shard_map.133 = (f32[8,128]{1,0:T(8,128)}, f32[8,128]{1,0:T(8,128)}, f32[3,4,32,128]{3,2,1,0:T(8,128)}) custom-call(s32[18,32]{1,0:T(8,128)S(1)} %get-tuple-element.30.plan_ref, bf16[8,8,128,128]{3,2,1,0:T(8,128)(2,1)S(1)} %copy-done.2, bf16[8,3,128,128]{3,2,1,0:T(8,128)(2,1)S(1)} %copy-done.3, f32[8,128]{1,0:T(8,128)S(1)} %copy-done.5, ...), custom_call_target="tpu_custom_call" | custom-call | tf_op jit(solution)/shard_map/pallas_call | solution.py:468
  (73 shorter events, 22.4 us)
Async XLA Ops:
  0.6 57.0 %collective-permute-start = (bf16[3,2,1536,128]{3,2,1,0:T(8,128)(2,1)}, bf16[3,2,1536,128]{3,2,1,0:T(8,128)(2,1)S(1)}, u32[]{:S(2)}, u32[]{:S(2)}) collective-permute-start(bf16[3,2,1536,128]{3,2,1,0:T(8,128)(2,1)} %bitcast.16), channel_id=1, source_target_pairs={{0,1},{1,0},{2,3},{3,2},{4,5},{5,4},{6,7},{7,6},{8,9},{9,8},{10,11... | collective-permute-start | bytes 7077896 | tf_op jit(solution)/shard_map/ppermute | solution.py:26
  2.8 12.5 %collective-permute-start.6 = (bf16[2,768,128]{2,1,0:T(8,128)(2,1)S(1)}, bf16[2,768,128]{2,1,0:T(8,128)(2,1)S(1)}, u32[]{:S(2)}, u32[]{:S(2)}) collective-permute-start(bf16[2,768,128]{2,1,0:T(8,128)(2,1)S(1)} %get-tuple-element.60), channel_id=1, source_target_pairs={{0,2},{1,3},{2,0},{3,1},{4,6},{5,7},{6,4},{7,5},{8,10},{9,11},{10,... | collective-permute-start | bytes 1179656 | tf_op jit(solution)/shard_map/ppermute | solution.py:26
  5.4 51.7 %collective-permute-start.1 = (bf16[2,1536,128]{2,1,0:T(8,128)(2,1)S(1)}, bf16[2,1536,128]{2,1,0:T(8,128)(2,1)S(1)}, u32[]{:S(2)}, u32[]{:S(2)}) collective-permute-start(bf16[2,1536,128]{2,1,0:T(8,128)(2,1)S(1)} %slice_bitcast_fusion), channel_id=1, source_target_pairs={{0,2},{1,3},{2,0},{3,1},{4,6},{5,7},{6,4},{7,5},{8,10},{9,11},{10,... | collective-permute-start | bytes 2359304 | tf_op jit(solution)/shard_map/ppermute | solution.py:26
  5.9 34.8 %collective-permute-start.8 = (bf16[2,768,128]{2,1,0:T(8,128)(2,1)S(1)}, bf16[2,768,128]{2,1,0:T(8,128)(2,1)S(1)}, u32[]{:S(2)}, u32[]{:S(2)}) collective-permute-start(bf16[2,768,128]{2,1,0:T(8,128)(2,1)S(1)} %get-tuple-element.59), channel_id=1, source_target_pairs={{0,2},{1,3},{2,0},{3,1},{4,6},{5,7},{6,4},{7,5},{8,10},{9,11},{10,... | collective-permute-start | bytes 1179656 | tf_op jit(solution)/shard_map/ppermute | solution.py:26
  7.5 41.5 %collective-permute-start.16 = (bf16[2,768,128]{2,1,0:T(8,128)(2,1)S(1)}, bf16[2,768,128]{2,1,0:T(8,128)(2,1)S(1)}, u32[]{:S(2)}, u32[]{:S(2)}) collective-permute-start(bf16[2,768,128]{2,1,0:T(8,128)(2,1)S(1)} %get-tuple-element.58), channel_id=1, source_target_pairs={{0,2},{1,3},{2,0},{3,1},{4,6},{5,7},{6,4},{7,5},{8,10},{9,11},{10,... | collective-permute-start | bytes 1179656 | tf_op jit(solution)/shard_map/ppermute | solution.py:26
  15.3 41.8 %collective-permute-start.18 = (bf16[2,768,128]{2,1,0:T(8,128)(2,1)S(1)}, bf16[2,768,128]{2,1,0:T(8,128)(2,1)S(1)}, u32[]{:S(2)}, u32[]{:S(2)}) collective-permute-start(bf16[2,768,128]{2,1,0:T(8,128)(2,1)S(1)} %get-tuple-element.57), channel_id=1, source_target_pairs={{0,2},{1,3},{2,0},{3,1},{4,6},{5,7},{6,4},{7,5},{8,10},{9,11},{10,... | collective-permute-start | bytes 1179656 | tf_op jit(solution)/shard_map/ppermute | solution.py:26
  40.6 49.1 %collective-permute-start.7 = (bf16[2,768,128]{2,1,0:T(8,128)(2,1)S(1)}, bf16[2,768,128]{2,1,0:T(8,128)(2,1)S(1)}, u32[]{:S(2)}, u32[]{:S(2)}) collective-permute-start(bf16[2,768,128]{2,1,0:T(8,128)(2,1)S(1)} %collective-permute-done.6.left_ref), channel_id=1, source_target_pairs={{0,1},{1,0},{2,3},{3,2},{4,5},{5,4},{6,7},{7,6},{8,9},{9,8},{10,11... | collective-permute-start | bytes 1179656 | tf_op jit(solution)/shard_map/ppermute | solution.py:26
  49.0 35.2 %collective-permute-start.9 = (bf16[2,768,128]{2,1,0:T(8,128)(2,1)S(1)}, bf16[2,768,128]{2,1,0:T(8,128)(2,1)S(1)}, u32[]{:S(2)}, u32[]{:S(2)}) collective-permute-start(bf16[2,768,128]{2,1,0:T(8,128)(2,1)S(1)} %collective-permute-done.8.left_ref), channel_id=1, source_target_pairs={{0,1},{1,0},{2,3},{3,2},{4,5},{5,4},{6,7},{7,6},{8,9},{9,8},{10,11... | collective-permute-start | bytes 1179656 | tf_op jit(solution)/shard_map/ppermute | solution.py:26
  57.1 40.7 %collective-permute-start.17 = (bf16[2,768,128]{2,1,0:T(8,128)(2,1)S(1)}, bf16[2,768,128]{2,1,0:T(8,128)(2,1)S(1)}, u32[]{:S(2)}, u32[]{:S(2)}) collective-permute-start(bf16[2,768,128]{2,1,0:T(8,128)(2,1)S(1)} %collective-permute-done.16.left_ref), channel_id=1, source_target_pairs={{0,1},{1,0},{2,3},{3,2},{4,5},{5,4},{6,7},{7,6},{8,9},{9,8},{10,11... | collective-permute-start | bytes 1179656 | tf_op jit(solution)/shard_map/ppermute | solution.py:26
  57.1 36.9 %collective-permute-start.19 = (bf16[2,768,128]{2,1,0:T(8,128)(2,1)S(1)}, bf16[2,768,128]{2,1,0:T(8,128)(2,1)S(1)}, u32[]{:S(2)}, u32[]{:S(2)}) collective-permute-start(bf16[2,768,128]{2,1,0:T(8,128)(2,1)S(1)} %collective-permute-done.18.left_ref), channel_id=1, source_target_pairs={{0,1},{1,0},{2,3},{3,2},{4,5},{5,4},{6,7},{7,6},{8,9},{9,8},{10,11... | collective-permute-start | bytes 1179656 | tf_op jit(solution)/shard_map/ppermute | solution.py:26
  57.6 18.0 %collective-permute-start.2 = (bf16[2,1536,128]{2,1,0:T(8,128)(2,1)S(1)}, bf16[2,1536,128]{2,1,0:T(8,128)(2,1)S(1)}, u32[]{:S(2)}, u32[]{:S(2)}) collective-permute-start(bf16[2,1536,128]{2,1,0:T(8,128)(2,1)S(1)} %collective-permute-done.1.left_ref), channel_id=1, source_target_pairs={{0,1},{1,0},{2,3},{3,2},{4,5},{5,4},{6,7},{7,6},{8,9},{9,8},{10,11... | collective-permute-start | bytes 2359304 | tf_op jit(solution)/shard_map/ppermute | solution.py:26
  82.4 34.6 %collective-permute-start.3 = (f32[13,32,128]{2,1,0:T(8,128)S(1)}, f32[13,32,128]{2,1,0:T(8,128)S(1)}, u32[]{:S(2)}, u32[]{:S(2)}) collective-permute-start(f32[13,32,128]{2,1,0:T(8,128)S(1)} %get-tuple-element.34), channel_id=1, source_target_pairs={{0,4},{4,0},{8,12},{12,8},{1,5},{5,1},{9,13},{13,9},{2,6},{6,2},{1... | collective-permute-start | bytes 638984 | tf_op jit(solution)/shard_map/ppermute | solution.py:26
  84.3 35.2 %collective-permute-start.4 = (f32[13,32,128]{2,1,0:T(8,128)S(1)}, f32[13,32,128]{2,1,0:T(8,128)S(1)}, u32[]{:S(2)}, u32[]{:S(2)}) collective-permute-start(f32[13,32,128]{2,1,0:T(8,128)S(1)} %get-tuple-element.35), channel_id=1, source_target_pairs={{0,8},{4,12},{8,0},{12,4},{1,9},{5,13},{9,1},{13,5},{2,10},{6,14},... | collective-permute-start | bytes 638984 | tf_op jit(solution)/shard_map/ppermute | solution.py:26
  89.7 29.8 %collective-permute-start.5 = (f32[13,32,128]{2,1,0:T(8,128)S(1)}, f32[13,32,128]{2,1,0:T(8,128)S(1)}, u32[]{:S(2)}, u32[]{:S(2)}) collective-permute-start(f32[13,32,128]{2,1,0:T(8,128)S(1)} %get-tuple-element.36), channel_id=1, source_target_pairs={{0,12},{4,8},{8,4},{12,0},{1,13},{5,9},{9,5},{13,1},{2,14},{6,10},... | collective-permute-start | bytes 638984 | tf_op jit(solution)/shard_map/ppermute | solution.py:26
  94.1 9.7 %collective-permute-start.10 = (bf16[13,32,128]{2,1,0:T(8,128)(2,1)S(1)}, bf16[13,32,128]{2,1,0:T(8,128)(2,1)S(1)}, u32[]{:S(2)}, u32[]{:S(2)}) collective-permute-start(bf16[13,32,128]{2,1,0:T(8,128)(2,1)S(1)} %get-tuple-element.39), channel_id=1, source_target_pairs={{0,4},{4,0},{8,12},{12,8},{1,5},{5,1},{9,13},{13,9},{2,6},{6,2},{1... | collective-permute-start | bytes 319496 | tf_op jit(solution)/shard_map/ppermute | solution.py:26
  97.8 15.9 %collective-permute-start.11 = (bf16[13,32,128]{2,1,0:T(8,128)(2,1)S(1)}, bf16[13,32,128]{2,1,0:T(8,128)(2,1)S(1)}, u32[]{:S(2)}, u32[]{:S(2)}) collective-permute-start(bf16[13,32,128]{2,1,0:T(8,128)(2,1)S(1)} %get-tuple-element.40), channel_id=1, source_target_pairs={{0,8},{4,12},{8,0},{12,4},{1,9},{5,13},{9,1},{13,5},{2,10},{6,14},... | collective-permute-start | bytes 319496 | tf_op jit(solution)/shard_map/ppermute | solution.py:26
  103.7 10.0 %collective-permute-start.12 = (bf16[13,32,128]{2,1,0:T(8,128)(2,1)S(1)}, bf16[13,32,128]{2,1,0:T(8,128)(2,1)S(1)}, u32[]{:S(2)}, u32[]{:S(2)}) collective-permute-start(bf16[13,32,128]{2,1,0:T(8,128)(2,1)S(1)} %get-tuple-element.41), channel_id=1, source_target_pairs={{0,12},{4,8},{8,4},{12,0},{1,13},{5,9},{9,5},{13,1},{2,14},{6,10},... | collective-permute-start | bytes 319496 | tf_op jit(solution)/shard_map/ppermute | solution.py:26
  113.7 11.4 %collective-permute-start.21 = (bf16[13,32,128]{2,1,0:T(8,128)(2,1)S(1)}, bf16[13,32,128]{2,1,0:T(8,128)(2,1)S(1)}, u32[]{:S(2)}, u32[]{:S(2)}) collective-permute-start(bf16[13,32,128]{2,1,0:T(8,128)(2,1)S(1)} %get-tuple-element.48), channel_id=1, source_target_pairs={{0,8},{4,12},{8,0},{12,4},{1,9},{5,13},{9,1},{13,5},{2,10},{6,14},... | collective-permute-start | bytes 319496 | tf_op jit(solution)/shard_map/ppermute | solution.py:26
  130.8 10.5 %collective-permute-start.29 = (bf16[7,32,128]{2,1,0:T(8,128)(2,1)S(1)}, bf16[7,32,128]{2,1,0:T(8,128)(2,1)S(1)}, u32[]{:S(2)}, u32[]{:S(2)}) collective-permute-start(bf16[7,32,128]{2,1,0:T(8,128)(2,1)S(1)} %shard_map.132.rest_4_), channel_id=1, source_target_pairs={{0,4},{4,0},{8,12},{12,8},{1,5},{5,1},{9,13},{13,9},{2,6},{6,2},{1... | collective-permute-start | bytes 172040 | tf_op jit(solution)/shard_map/ppermute | solution.py:26
  136.9 13.7 %collective-permute-start.24 = (bf16[8,32,128]{2,1,0:T(8,128)(2,1)S(1)}, bf16[8,32,128]{2,1,0:T(8,128)(2,1)S(1)}, u32[]{:S(2)}, u32[]{:S(2)}) collective-permute-start(bf16[8,32,128]{2,1,0:T(8,128)(2,1)S(1)} %shard_map.131.rest_0_), channel_id=1, source_target_pairs={{0,4},{4,0},{8,12},{12,8},{1,5},{5,1},{9,13},{13,9},{2,6},{6,2},{1... | collective-permute-start | bytes 196616 | tf_op jit(solution)/shard_map/ppermute | solution.py:26
  137.3 13.4 %collective-permute-start.25 = (bf16[8,32,128]{2,1,0:T(8,128)(2,1)S(1)}, bf16[8,32,128]{2,1,0:T(8,128)(2,1)S(1)}, u32[]{:S(2)}, u32[]{:S(2)}) collective-permute-start(bf16[8,32,128]{2,1,0:T(8,128)(2,1)S(1)} %shard_map.131.rest_0_), channel_id=1, source_target_pairs={{0,8},{4,12},{8,0},{12,4},{1,9},{5,13},{9,1},{13,5},{2,10},{6,14},... | collective-permute-start | bytes 196616 | tf_op jit(solution)/shard_map/ppermute | solution.py:26
  139.1 11.5 %collective-permute-start.26 = (bf16[8,32,128]{2,1,0:T(8,128)(2,1)S(1)}, bf16[8,32,128]{2,1,0:T(8,128)(2,1)S(1)}, u32[]{:S(2)}, u32[]{:S(2)}) collective-permute-start(bf16[8,32,128]{2,1,0:T(8,128)(2,1)S(1)} %shard_map.131.rest_0_), channel_id=1, source_target_pairs={{0,12},{4,8},{8,4},{12,0},{1,13},{5,9},{9,5},{13,1},{2,14},{6,10},... | collective-permute-start | bytes 196616 | tf_op jit(solution)/shard_map/ppermute | solution.py:26
  141.3 9.3 %collective-permute-start.30 = (bf16[7,32,128]{2,1,0:T(8,128)(2,1)S(1)}, bf16[7,32,128]{2,1,0:T(8,128)(2,1)S(1)}, u32[]{:S(2)}, u32[]{:S(2)}) collective-permute-start(bf16[7,32,128]{2,1,0:T(8,128)(2,1)S(1)} %shard_map.132.rest_4_), channel_id=1, source_target_pairs={{0,8},{4,12},{8,0},{12,4},{1,9},{5,13},{9,1},{13,5},{2,10},{6,14},... | collective-permute-start | bytes 172040 | tf_op jit(solution)/shard_map/ppermute | solution.py:26
  141.3 9.3 %collective-permute-start.31 = (bf16[7,32,128]{2,1,0:T(8,128)(2,1)S(1)}, bf16[7,32,128]{2,1,0:T(8,128)(2,1)S(1)}, u32[]{:S(2)}, u32[]{:S(2)}) collective-permute-start(bf16[7,32,128]{2,1,0:T(8,128)(2,1)S(1)} %shard_map.132.rest_4_), channel_id=1, source_target_pairs={{0,12},{4,8},{8,4},{12,0},{1,13},{5,9},{9,5},{13,1},{2,14},{6,10},... | collective-permute-start | bytes 172040 | tf_op jit(solution)/shard_map/ppermute | solution.py:26
  (17 other events, 240.9 us)
